TPU v7x, 32 devices: a whole 2x2x4 slice. The times are simulated.
32 devices in a mesh: dp: 8 (over y, x, core), mp: 4 (over z).
Axes of the slice: x: 2, y: 2, z: 4, core: 2. Of those that a mesh axis runs over, the one named last changes fastest.
Arguments:
- tokens: bfloat16 [16, 512, 1024], P('dp', 'mp'), may hold values from -6 to 6
- memory: bfloat16 [16, 512, 1024], P('dp', 'mp'), may hold values from -6 to 6
- compressed: bfloat16 [16, 512, 1024], P('dp', 'mp'), may hold values from -6 to 6
- valid_counts: int32 [16], P('dp'), may hold values from 64 to 512, as said below
- attention_norm_gain: float32 [1024], replicated, may hold values from 0.5 to 1.5
- attention_norm_bias: float32 [1024], replicated, may hold values from -1.75 to 1.75
- query_projection: bfloat16 [1024, 1024], P(None, 'mp'), may hold values from -0.1875 to 0.1875
- key_projection: bfloat16 [1024, 1024], P(None, 'mp'), may hold values from -0.1875 to 0.1875
- value_projection: bfloat16 [1024, 1024], P(None, 'mp'), may hold values from -0.1875 to 0.1875
- out_weight: bfloat16 [1024, 1024], P('mp'), may hold values from -2 to 2
- feedforward_norm_gain: float32 [1024], replicated, may hold values from 0.5 to 1.5
- feedforward_norm_bias: float32 [1024], replicated, may hold values from -1.75 to 1.75
- up_weight: bfloat16 [1024, 4096], P(None, 'mp'), may hold values from -0.1875 to 0.1875
- up_bias: float32 [4096], P('mp'), may hold values from -3 to 3
- down_weight: bfloat16 [4096, 1024], P('mp'), may hold values from -0.09375 to 0.09375
- down_bias: float32 [1024], replicated, may hold values from -3 to 3
- squeeze_weight: bfloat16 [3072, 1024], replicated, may hold values from -0.109375 to 0.109375
- cotangent: bfloat16 [16, 512, 1024], P('dp', 'mp'), may hold values from -6 to 6
Outputs:
- output: bfloat16 [16, 512, 1024], P('dp', 'mp')
- tokens_grad: float32 [16, 512, 1024], P('dp', 'mp')
- attention_gain_gradient: float32 [1024], replicated
- first_bias_grad: float32 [1024], replicated
- query_weight_grad: float32 [1024, 1024], P(None, 'mp')
- key_weight_grad: float32 [1024, 1024], P(None, 'mp')
- value_weight_grad: float32 [1024, 1024], P(None, 'mp')
- out_weight_grad: float32 [1024, 1024], P('mp')
- feedforward_gain_gradient: float32 [1024], replicated
- second_bias_grad: float32 [1024], replicated
- up_weight_grad: float32 [1024, 4096], P(None, 'mp')
- up_bias_grad: float32 [4096], P('mp')
- down_weight_grad: float32 [4096, 1024], P('mp')
- down_bias_grad: float32 [1024], replicated
- new_memory: bfloat16 [16, 512, 1024], P('dp', 'mp')
- new_compressed: bfloat16 [16, 512, 1024], P('dp', 'mp')
Inputs may be any that keep to these rules, and one draw needn't show every extreme that they name: The first valid_counts tokens of a segment are real, the rest padding.
All inputs are finite; a program needn't handle non-finite values.
Results may differ from a plain program's by a relative error of at most 0.015.
Values may be sent and summed in bfloat16 or wider, within the bound.
A program may use at most 192 MiB of HBM per device.

v0:
```python
import functools

import jax
import jax.numpy as jnp
from jax import lax
from jax.experimental import pallas as pl
from jax.experimental.pallas import tpu as pltpu
from jax.sharding import PartitionSpec as P

HEAD_DIM = 128
RATE = 3


def apply_layer_norm(rows):
    center = jnp.mean(rows, axis=-1, keepdims=True)
    centered = rows - center
    spread = jnp.mean(centered * centered, axis=-1, keepdims=True)
    inverse_deviation = lax.rsqrt(spread + 1e-05)
    return (centered * inverse_deviation, inverse_deviation)


def norm_backward_pass(input_gradient, standardized_rows, inverse_deviation, scale_factor):
    scaled_rows = input_gradient * scale_factor
    attention_norm_mean = jnp.mean(scaled_rows, axis=-1, keepdims=True)
    feedforward_norm_mean = jnp.mean(scaled_rows * standardized_rows, axis=-1, keepdims=True)
    return inverse_deviation * (
        scaled_rows - attention_norm_mean - standardized_rows * feedforward_norm_mean
    )


def squeeze_rows(old_comp, old_mem, fresh, valid_count, offset, own_rows, squeeze_weight):
    features = old_mem.shape[1]
    joined = jnp.concatenate([old_mem, fresh], axis=0)
    new_memory = lax.dynamic_slice_in_dim(joined, valid_count + offset, own_rows, 0)
    comp_len = old_comp.shape[0]
    evicted = valid_count // RATE
    first_row = evicted + offset
    window_start = jnp.maximum(first_row - comp_len, 0)
    padded = jnp.concatenate(
        [old_mem, jnp.zeros((RATE * own_rows, features), jnp.bfloat16)], axis=0
    )
    window = lax.dynamic_slice_in_dim(padded, window_start * RATE, RATE * own_rows, 0)
    squeezed = jnp.dot(
        window.reshape(own_rows, RATE * features),
        squeeze_weight,
        preferred_element_type=jnp.float32,
    ).astype(jnp.bfloat16)
    positions = first_row + jnp.arange(own_rows)
    from_old = jnp.take(old_comp, jnp.clip(positions, 0, comp_len - 1), axis=0)
    from_new = jnp.take(
        squeezed, jnp.clip(positions - comp_len - window_start, 0, own_rows - 1), axis=0
    )
    new_compressed = jnp.where((positions < comp_len)[:, None], from_old, from_new)
    return (new_memory, new_compressed)


def general_device(
    tokens,
    memory,
    compressed,
    valid_counts,
    attention_norm_gain,
    attention_norm_bias,
    query_projection,
    key_projection,
    value_projection,
    out_weight,
    feedforward_norm_gain,
    feedforward_norm_bias,
    up_weight,
    up_bias,
    down_weight,
    down_bias,
    squeeze_weight,
    cotangent,
):
    batch_segs, own_rows, features = tokens.shape
    offset = lax.axis_index("mp") * own_rows
    old_comp, old_mem, fresh = (
        lax.all_gather(compressed, "mp", axis=1, tiled=True),
        lax.all_gather(memory, "mp", axis=1, tiled=True),
        lax.all_gather(tokens, "mp", axis=1, tiled=True),
    )
    seg_len = fresh.shape[1]
    prior_rows = old_comp.shape[1] + old_mem.shape[1]
    context_tokens = jnp.concatenate([old_comp, old_mem, fresh], axis=1).astype(jnp.float32)
    ctx_len = context_tokens.shape[1]
    standardized_full, inverse_deviation_full = apply_layer_norm(context_tokens)
    normed_rows = (standardized_full * attention_norm_gain + attention_norm_bias).astype(
        jnp.bfloat16
    )
    token_rows_normed = normed_rows[:, prior_rows:]
    queries = jnp.einsum(
        "xhp,pj->xhj", token_rows_normed, query_projection, preferred_element_type=jnp.float32
    ).astype(jnp.bfloat16)
    key_rows = jnp.einsum(
        "xhp,pj->xhj", normed_rows, key_projection, preferred_element_type=jnp.float32
    ).astype(jnp.bfloat16)
    values = jnp.einsum(
        "xhp,pj->xhj", normed_rows, value_projection, preferred_element_type=jnp.float32
    ).astype(jnp.bfloat16)
    local_heads = query_projection.shape[1] // HEAD_DIM
    score_scale = HEAD_DIM ** (-0.5)

    def by_heads(matrix):
        return matrix.reshape(matrix.shape[0], matrix.shape[1], local_heads, HEAD_DIM)

    query_pos = jnp.arange(seg_len)[:, None]
    key_pos = jnp.arange(ctx_len)[None, :] - prior_rows
    allowed = (key_pos[None] < 0) | (key_pos <= query_pos)[None] & (
        key_pos[None] < valid_counts[:, None, None]
    )

    def scores_of(query_in, key_in):
        raw = (
            jnp.einsum(
                "gqhe,gkhe->ghqk",
                by_heads(query_in),
                by_heads(key_in),
                preferred_element_type=jnp.float32,
            )
            * score_scale
        )
        return jnp.where(allowed[:, None], raw, -1e30)

    scores = scores_of(queries, key_rows)
    peak_score = jnp.max(scores, axis=-1, keepdims=True)
    exponent = jnp.exp(scores - peak_score)
    exp_total = jnp.sum(exponent, axis=-1, keepdims=True)
    log_total = peak_score + jnp.log(exp_total)
    probs_low = (exponent / exp_total).astype(jnp.bfloat16)
    mixed_heads = jnp.einsum(
        "ghqk,gkhe->gqhe", probs_low, by_heads(values), preferred_element_type=jnp.float32
    ).astype(jnp.bfloat16)
    mixed_heads = mixed_heads.reshape(batch_segs, seg_len, local_heads * HEAD_DIM)
    partial_attn = jnp.einsum(
        "gsc,cd->gsd", mixed_heads, out_weight, preferred_element_type=jnp.float32
    )
    attention = lax.psum_scatter(partial_attn, "mp", scatter_dimension=1, tiled=True)
    residual_stream = tokens.astype(jnp.float32) + attention
    standardized_feedforward, inverse_deviation_feedforward = apply_layer_norm(residual_stream)
    feedforward_input = (
        standardized_feedforward * feedforward_norm_gain + feedforward_norm_bias
    ).astype(jnp.bfloat16)
    second_all = lax.all_gather(feedforward_input, "mp", axis=1, tiled=True)
    upper_in = (
        jnp.einsum("gsd,df->gsf", second_all, up_weight, preferred_element_type=jnp.float32)
        + up_bias
    )
    active, gelu_back = jax.vjp(jax.nn.gelu, upper_in)
    active_low = active.astype(jnp.bfloat16)
    partial_ffn = jnp.einsum(
        "gsf,fd->gsd", active_low, down_weight, preferred_element_type=jnp.float32
    )
    down_out = lax.psum_scatter(
        partial_ffn.astype(jnp.bfloat16), "mp", scatter_dimension=1, tiled=True
    ).astype(jnp.float32)
    output = (residual_stream + down_out + down_bias).astype(jnp.bfloat16)

    def update_one(comp_seg, mem_seg, fresh_seg, valid_count):
        return squeeze_rows(
            comp_seg, mem_seg, fresh_seg, valid_count, offset, own_rows, squeeze_weight
        )

    new_memory, new_compressed = jax.vmap(update_one)(old_comp, old_mem, fresh, valid_counts)
    output_gradient = cotangent.astype(jnp.float32)
    down_bias_grad = jnp.sum(output_gradient, axis=(0, 1))
    grad_all = lax.all_gather(cotangent, "mp", axis=1, tiled=True)
    down_weight_grad = jnp.einsum(
        "gsf,gsd->fd", active_low, grad_all, preferred_element_type=jnp.float32
    )
    grad_active = jnp.einsum(
        "gsd,fd->gsf", grad_all, down_weight, preferred_element_type=jnp.float32
    )
    grad_upper = gelu_back(grad_active)[0].astype(jnp.bfloat16)
    up_weight_grad = jnp.einsum(
        "gsd,gsf->df", second_all, grad_upper, preferred_element_type=jnp.float32
    )
    up_bias_grad = jnp.sum(grad_upper.astype(jnp.float32), axis=(0, 1))
    partial_second = jnp.einsum(
        "gsf,df->gsd", grad_upper, up_weight, preferred_element_type=jnp.float32
    )
    feedforward_gradient = lax.psum_scatter(partial_second, "mp", scatter_dimension=1, tiled=True)
    feedforward_gain_gradient = jnp.sum(
        feedforward_gradient * standardized_feedforward, axis=(0, 1)
    )
    second_bias_grad = jnp.sum(feedforward_gradient, axis=(0, 1))
    residual_gradient = output_gradient + norm_backward_pass(
        feedforward_gradient,
        standardized_feedforward,
        inverse_deviation_feedforward,
        feedforward_norm_gain,
    )
    grad_resid_all = lax.all_gather(
        residual_gradient.astype(jnp.bfloat16), "mp", axis=1, tiled=True
    )
    out_weight_grad = jnp.einsum(
        "gsc,gsd->cd", mixed_heads, grad_resid_all, preferred_element_type=jnp.float32
    )
    grad_mixed = jnp.einsum(
        "gsd,cd->gsc", grad_resid_all, out_weight, preferred_element_type=jnp.float32
    ).astype(jnp.bfloat16)
    probs_again = jnp.exp(scores_of(queries, key_rows) - log_total)
    grad_probs = jnp.einsum(
        "gqhe,gkhe->ghqk",
        by_heads(grad_mixed),
        by_heads(values),
        preferred_element_type=jnp.float32,
    )
    row_dot = jnp.sum(probs_again * grad_probs, axis=-1, keepdims=True)
    grad_scores = (probs_again * (grad_probs - row_dot)).astype(jnp.bfloat16)
    query_gradient = (
        score_scale
        * jnp.einsum(
            "ghqk,gkhe->gqhe", grad_scores, by_heads(key_rows), preferred_element_type=jnp.float32
        )
    ).astype(jnp.bfloat16)
    key_gradient = (
        score_scale
        * jnp.einsum(
            "ghqk,gqhe->gkhe", grad_scores, by_heads(queries), preferred_element_type=jnp.float32
        )
    ).astype(jnp.bfloat16)
    value_gradient = jnp.einsum(
        "ghqk,gqhe->gkhe",
        probs_again.astype(jnp.bfloat16),
        by_heads(grad_mixed),
        preferred_element_type=jnp.float32,
    ).astype(jnp.bfloat16)
    query_gradient = query_gradient.reshape(batch_segs, seg_len, -1)
    key_gradient = key_gradient.reshape(batch_segs, ctx_len, -1)
    value_gradient = value_gradient.reshape(batch_segs, ctx_len, -1)
    query_weight_grad = jnp.einsum(
        "nja,njr->ar", token_rows_normed, query_gradient, preferred_element_type=jnp.float32
    )
    key_weight_grad = jnp.einsum(
        "nja,njr->ar", normed_rows, key_gradient, preferred_element_type=jnp.float32
    )
    value_weight_grad = jnp.einsum(
        "nja,njr->ar", normed_rows, value_gradient, preferred_element_type=jnp.float32
    )
    partial_normed = jnp.einsum(
        "xmo,qo->xmq", key_gradient, key_projection, preferred_element_type=jnp.float32
    )
    partial_normed = partial_normed + jnp.einsum(
        "xmo,qo->xmq", value_gradient, value_projection, preferred_element_type=jnp.float32
    )
    partial_normed = partial_normed.at[:, prior_rows:].add(
        jnp.einsum(
            "xmo,qo->xmq", query_gradient, query_projection, preferred_element_type=jnp.float32
        )
    )
    partial_normed = partial_normed.reshape(batch_segs, 3, seg_len, features)
    normed_gradient = lax.psum_scatter(
        partial_normed.astype(jnp.bfloat16), "mp", scatter_dimension=2, tiled=True
    ).astype(jnp.float32)
    segment_context = jnp.stack([compressed, memory, tokens], axis=1).astype(jnp.float32)
    standardized_segment, inverse_deviation_segment = apply_layer_norm(segment_context)
    attention_gain_gradient = jnp.sum(normed_gradient * standardized_segment, axis=(0, 1, 2))
    first_bias_grad = jnp.sum(normed_gradient, axis=(0, 1, 2))
    tokens_grad = residual_gradient + norm_backward_pass(
        normed_gradient[:, 2],
        standardized_segment[:, 2],
        inverse_deviation_segment[:, 2],
        attention_norm_gain,
    )
    summed = (
        lax.psum(query_weight_grad.astype(jnp.bfloat16), "dp").astype(jnp.float32),
        lax.psum(key_weight_grad.astype(jnp.bfloat16), "dp").astype(jnp.float32),
        lax.psum(value_weight_grad.astype(jnp.bfloat16), "dp").astype(jnp.float32),
        lax.psum(out_weight_grad.astype(jnp.bfloat16), "dp").astype(jnp.float32),
        lax.psum(up_weight_grad.astype(jnp.bfloat16), "dp").astype(jnp.float32),
        lax.psum(up_bias_grad.astype(jnp.bfloat16), "dp").astype(jnp.float32),
        lax.psum(down_weight_grad.astype(jnp.bfloat16), "dp").astype(jnp.float32),
    )
    norms = lax.psum(
        (
            attention_gain_gradient,
            first_bias_grad,
            feedforward_gain_gradient,
            second_bias_grad,
            down_bias_grad,
        ),
        ("dp", "mp"),
    )
    return (
        output,
        tokens_grad,
        norms[0],
        norms[1],
        summed[0],
        summed[1],
        summed[2],
        summed[3],
        norms[2],
        norms[3],
        summed[4],
        summed[5],
        summed[6],
        norms[4],
        new_memory,
        new_compressed,
    )


BF = jnp.bfloat16
F32 = jnp.float32
MESH = pl.DeviceIdType.MESH
ANY = pl.BlockSpec(memory_space=pl.ANY)
VM = pl.BlockSpec(memory_space=pltpu.VMEM)
DMA = pltpu.SemaphoreType.DMA


def sds(shape, dtype):
    return jax.ShapeDtypeStruct(shape, dtype)


def where_am_i(chips, depth):
    dp = lax.axis_index("dp")
    return dp, lax.rem(dp, 2), dp // 2, lax.axis_index("mp")


def rcopy(src, dst, send, recv, device):
    return pltpu.make_async_remote_copy(
        src_ref=src,
        dst_ref=dst,
        send_sem=send,
        recv_sem=recv,
        device_id=device,
        device_id_type=MESH,
    )


def lcopy(src, dst, sem):
    return pltpu.make_async_copy(src, dst, sem)


def enter(partners):
    barrier = pltpu.get_barrier_semaphore()
    for p in partners:
        pl.semaphore_signal(barrier, inc=1, device_id=p, device_id_type=MESH)
    pl.semaphore_wait(barrier, len(partners))


def across(q, k):
    if k == 0:
        return q
    if k == 1:
        return q + 1 - 2 * lax.rem(q, 2)
    if k == 2:
        return lax.rem(q + 2, 4)
    return 3 - q


def layer_norm_rows(rows):
    center = jnp.mean(rows, axis=-1, keepdims=True)
    centered = rows - center
    spread = jnp.mean(centered * centered, axis=-1, keepdims=True)
    inv = lax.rsqrt(spread + 1e-05)
    return centered * inv, inv


class Slots:
    def __init__(self, ref):
        self.ref = ref
        self.used = 0

    def take(self, *shape):
        base = self.used
        size = 1
        for n in shape:
            size *= n
        self.used += size

        def at(*index):
            flat = 0
            for n, i in zip(shape, index):
                flat = flat * n + i
            return self.ref.at[base + flat]

        return at


def nt_dot(a, b):
    return lax.dot_general(a, b, (((1,), (1,)), ((), ())), preferred_element_type=F32)


def tn_dot(a, b):
    return lax.dot_general(a, b, (((0,), (0,)), ((), ())), preferred_element_type=F32)


def nn_dot(a, b):
    return jnp.dot(a, b, preferred_element_type=F32)


def one_hot(shape, offset):
    row = lax.broadcasted_iota(jnp.int32, shape, 0)
    col = lax.broadcasted_iota(jnp.int32, shape, 1)
    return jnp.where(col == row + offset, 1.0, 0.0).astype(BF)


FRONT_SEMS = 400


def front_kernel(Q, Z, comp, mem, tok, cot, wq, wk, wv, wo, up, down, ub, vc, sq, g1, b1, g2, b2,
                 tok_o, normed_o, q_o, k_o, v_o, probs_o, mixed_o, wq_o, wk_o, wv_o, wo_o,
                 resid_o, gresid_o, glow_o, gu_o, gd_o, down_o, small_o, nm_o, nc_o,
                 ctx, normed, wqs, wks, wvs, wos, qs, ks, vs, probs, mixed, phalf, got, resid, sec, cots, ups, downs,
                 ubs, vco, act, gup, gbuf, got1, send2, got2, low, nms, ncs, gus, gds, dns, sems):
    dp, c, q, z = where_am_i(Q, Z)
    sib = dp + 1 - 2 * c
    partners = [(sib, z)]
    for r in range(1, Z):
        for d in (dp, sib):
            partners.append((d, lax.rem(z + r, Z)))
    for k in range(1, Q):
        partners.append((2 * across(q, k) + c, z))
    enter(partners)
    B, R, D = tok.shape
    H = wq.shape[1]
    QR = D // Q
    OR = H // Q
    HR = R // 2
    S = R * Z
    N = S // 2
    E = up.shape[1] // (2 * Q)
    heads = B * H // HEAD_DIM
    mine = c == z // B
    jz = lax.rem(z, B)
    al = Slots(sems)

    def peer(k):
        return (2 * across(q, k) + c, z)

    wins = [wq, wk, wv, wo]
    wss = [wqs, wks, wvs, wos]

    def piece(a):
        if a < 3:
            return wins[a].at[pl.ds(q * QR, QR), :]
        return wo.at[pl.ds(q * OR, OR), :]

    def place(a, j, qq):
        if a < 3:
            return wss[a].at[pl.ds(pl.multiple_of(qq * QR, QR), QR), pl.ds(pl.multiple_of(j * H, H), H)]
        return wos.at[pl.ds(pl.multiple_of(j * H + qq * OR, OR), OR), :]

    def place_whole(a, j):
        if a < 3:
            return wss[a].at[:, pl.ds(pl.multiple_of(j * H, H), H)]
        return wos.at[pl.ds(pl.multiple_of(j * H, H), H), :]

    ws, wr = al.take(4, Z - 1), al.take(4, B)
    ps, pr = al.take(4, B, Q - 1), al.take(4, B, Q - 1)
    wl = al.take(4)

    def w_z(a, r):
        return rcopy(piece(a), place(a, jz, q), ws(a, r - 1), wr(a, jz), (dp, lax.rem(z + r, Z)))

    def w_arrive(a, j):
        return rcopy(place(a, j, q), place(a, j, q), ws(a, 0), wr(a, j), (dp, z))

    def w_p(a, j, k, qq):
        return rcopy(place(a, j, qq), place(a, j, qq), ps(a, j, k - 1), pr(a, j, k - 1), peer(k))

    def w_l(a):
        return lcopy(wins[a], place_whole(a, jz), wl(a))

    acts = [comp, mem, tok]
    cs, cr = al.take(3, B, 2), al.take(3, Z)
    fs, fr = al.take(3, Z), al.take(3, Z)
    cl = al.take(3)

    def c_rows(t, zs):
        return ctx.at[t, pl.ds(pl.multiple_of(zs * R, R), R), :]

    def c_half(t, zs, h):
        return ctx.at[t, pl.ds(pl.multiple_of(zs * R + HR * h, HR), HR), :]

    def c_l(t):
        return lcopy(acts[t].at[jz], c_rows(t, z), cl(t))

    def c_sib(t):
        return rcopy(acts[t].at[jz], c_rows(t, z), fs(t, z), fr(t, z), (sib, z))

    def c_z(t, s, h):
        return rcopy(acts[t].at[s, pl.ds(HR * h, HR), :], c_half(t, z, h), cs(t, s, h), cr(t, z), (2 * q + h, B * c + s))

    def c_arrive(t, zs):
        return rcopy(c_half(t, zs, c), c_half(t, zs, c), cs(t, 0, 0), cr(t, zs), (dp, z))

    def c_fwd(t, zs, half):
        return rcopy(c_half(t, zs, half), c_half(t, zs, half), fs(t, zs), fr(t, zs), (sib, z))

    us, ur, ul = al.take(Z - 1), al.take(Z - 1), al.take(1)
    vs_, vr_ = al.take(1), al.take(1)

    def u_z(r):
        return rcopy(ub.at[dp], ubs.at[r], us(r - 1), ur(r - 1), (dp, lax.rem(z + r, Z)))

    u_l = lcopy(ub.at[dp], ubs.at[0], ul(0))
    v_s = rcopy(vc, vco, vs_(0), vr_(0), (sib, z))

    ts, tr, tl = al.take(B), al.take(B), al.take(1)
    tps, tpr, tfs, tfr = al.take(Q), al.take(Q), al.take(Q), al.take(Q)

    def slot(ref, k, cc):
        return ref.at[pl.ds((2 * k + cc) * N, N), :]

    def t_z(s):
        return rcopy(cot.at[s], cots.at[pl.ds(pl.multiple_of(jz * R, R), R), :], ts(s), tr(jz), (2 * q + z // B, B * c + s))

    def t_l():
        return lcopy(cot.at[jz], cots.at[pl.ds(pl.multiple_of(jz * R, R), R), :], tl(0))

    def t_arrive(i):
        return rcopy(cots.at[pl.ds(i * R, R), :], cots.at[pl.ds(i * R, R), :], ts(0), tr(i), (dp, z))

    def t_p(k):
        return rcopy(slot(cots, 0, 0), slot(cots, k, 0), tps(k), tpr(k), peer(k))

    def t_f(k):
        return rcopy(slot(cots, k, 0), slot(cots, k, 1), tfs(k), tfr(k), (sib, z))

    xs, xr_, xl = al.take(2, Z), al.take(2, Z), al.take(2)

    def x_z(i, r):
        if i == 0:
            return rcopy(up.at[:, pl.ds(pl.multiple_of(dp * E, E), E)], ups.at[:, pl.ds(r * E, E)], xs(0, r), xr_(0, r),
                         (dp, lax.rem(z + r, Z)))
        return rcopy(down.at[pl.ds(pl.multiple_of(dp * E, E), E), :], downs.at[pl.ds(r * E, E), :], xs(1, r), xr_(1, r),
                     (dp, lax.rem(z + r, Z)))

    x_l = [lcopy(up.at[:, pl.ds(pl.multiple_of(dp * E, E), E)], ups.at[:, pl.ds(0, E)], xl(0)),
           lcopy(down.at[pl.ds(pl.multiple_of(dp * E, E), E), :], downs.at[pl.ds(0, E), :], xl(1))]

    @pl.when(mine)
    def _():
        for a in range(4):
            for r in range(1, Z):
                w_z(a, r).start()
        for a in range(4):
            w_l(a).start()
        for t in range(3):
            c_l(t).start()
            c_sib(t).start()
    for r in range(1, Z):
        u_z(r).start()
    v_s.start()
    u_l.start()
    for x in x_l:
        x.start()
    for j in range(B):
        @pl.when(B * c + j != z)
        def _():
            for a in range(4):
                w_arrive(a, j).wait_recv()
                for k in range(1, Q):
                    w_p(a, j, k, q).start()
    for s in range(B):
        @pl.when(B * c + s != z)
        def _():
            for t in range(3):
                for h in range(2):
                    c_z(t, s, h).start()

    def norm_block(t, zs):
        at = pl.ds(pl.multiple_of(zs * R, R), R)
        to = pl.ds(pl.multiple_of(t * S + zs * R, R), R)
        xhat, _ = layer_norm_rows(ctx[t, at, :].astype(F32))
        normed[to, :] = (xhat * g1[...] + b1[...]).astype(BF)

    @pl.when(mine)
    def _():
        for t in range(3):
            c_l(t).wait()

    @pl.when(jnp.logical_not(mine))
    def _():
        for t in range(3):
            rcopy(c_rows(t, z), c_rows(t, z), fs(t, z), fr(t, z), (sib, z)).wait_recv()

    def norm_own(t, carry):
        norm_block(t, z)
        return carry

    lax.fori_loop(0, 3, norm_own, 0)
    for r in range(1, Z):
        zs = lax.rem(z + r, Z)
        for t in range(3):
            c_arrive(t, zs).wait_recv()
            c_fwd(t, zs, c).start()
    for s in range(B):
        @pl.when(B * c + s != z)
        def _():
            for t in range(3):
                for h in range(2):
                    c_z(t, s, h).wait_send()
    for s in range(B):
        here = (B * c + s == z) & mine

        @pl.when(here)
        def _():
            t_l().start()

        @pl.when(jnp.logical_not(here))
        def _():
            t_z(s).start()
    for i in range(2):
        for r in range(1, Z):
            x_z(i, r).start()
    for r in range(1, Z):
        zs = lax.rem(z + r, Z)
        for t in range(3):
            c_fwd(t, zs, 1 - c).wait_recv()

        def norm_one(t, carry, zs=zs):
            norm_block(t, zs)
            return carry

        lax.fori_loop(0, 3, norm_one, 0)
    outs = al.take(16)
    copies = []

    def leave(src, dst):
        cp = lcopy(src, dst, outs(len(copies)))
        cp.start()
        copies.append(cp)

    leave(normed, normed_o)
    leave(ctx.at[2], tok_o)
    for j in range(B):
        @pl.when(B * c + j != z)
        def _():
            for a in range(4):
                for k in range(1, Q):
                    w_p(a, j, k, across(q, k)).wait_recv()

    @pl.when(mine)
    def _():
        for a in range(4):
            w_l(a).wait()
    for a in range(4):
        leave(wss[a], (wq_o, wk_o, wv_o, wo_o)[a])

    T = 256

    def project(i, carry):
        at = pl.ds(pl.multiple_of(i * T, T), T)
        ks[at, :] = nn_dot(normed[at, :], wks[...]).astype(BF)
        vs[at, :] = nn_dot(normed[at, :], wvs[...]).astype(BF)
        return carry

    lax.fori_loop(0, 3 * S // T, project, 0)

    def project_q(i, carry):
        at = pl.ds(pl.multiple_of(i * T, T), T)
        qs[at, :] = nn_dot(normed[pl.ds(pl.multiple_of(2 * S + i * T, T), T), :], wqs[...]).astype(BF)
        return carry

    lax.fori_loop(0, S // T, project_q, 0)
    leave(qs, q_o)
    leave(ks, k_o)
    leave(vs, v_o)

    v_s.wait()
    counts = jnp.where(mine, vc[jz], vco[jz])
    count = counts[0:1, 0:1]
    scale = HEAD_DIM ** (-0.5)
    P2 = 2 * S
    pouts = al.take(2, heads)

    def attend(half, tag):
        r0 = pl.multiple_of(half * N, N)

        def head(h, carry):
            hd = pl.ds(pl.multiple_of(h * HEAD_DIM, HEAD_DIM), HEAD_DIM)
            qh = qs[pl.ds(r0, N), hd]
            s1 = nt_dot(qh, ks[pl.ds(0, P2), hd])
            s2 = nt_dot(qh, ks[pl.ds(P2, S), hd])
            row = lax.broadcasted_iota(jnp.int32, (N, S), 0) + half * N
            col = lax.broadcasted_iota(jnp.int32, (N, S), 1)
            s2 = jnp.where((col <= row) & (col < count), s2, -1e30)
            top = jnp.maximum(jnp.max(s1, axis=-1, keepdims=True), jnp.max(s2, axis=-1, keepdims=True))
            p1 = jnp.exp((s1 - top) * scale)
            p2 = jnp.exp((s2 - top) * scale)
            inv = 1.0 / (jnp.sum(p1, axis=-1, keepdims=True) + jnp.sum(p2, axis=-1, keepdims=True))
            p1 = (p1 * inv).astype(BF)
            p2 = (p2 * inv).astype(BF)
            probs[h, pl.ds(r0, N), pl.ds(0, P2)] = p1
            probs[h, pl.ds(r0, N), pl.ds(P2, S)] = p2
            lcopy(probs.at[h, pl.ds(r0, N), :], probs_o.at[h, pl.ds(r0, N), :], pouts(tag, h)).start()
            mix = nn_dot(p1, vs[pl.ds(0, P2), hd]) + nn_dot(p2, vs[pl.ds(P2, S), hd])
            mixed[pl.ds(r0, N), hd] = mix.astype(BF)
            return carry

        lax.fori_loop(0, heads, head, 0)

    hs, hr = al.take(1), al.take(1)
    h_x = rcopy(phalf, got, hs(0), hr(0), (sib, z))
    attend(1 - c, 0)
    phalf[...] = nn_dot(mixed[pl.ds(pl.multiple_of((1 - c) * N, N), N), :], wos[...])
    h_x.start()
    for i in range(B):
        @pl.when(jnp.logical_not((B * c + i == z) & mine))
        def _():
            t_arrive(i).wait_recv()

        @pl.when((B * c + i == z) & mine)
        def _():
            t_l().wait()
    for k in range(1, Q):
        t_p(k).start()
    t_f(0).start()
    attend(c, 1)
    leave(mixed, mixed_o)
    own_part = nn_dot(mixed[pl.ds(pl.multiple_of(c * N, N), N), :], wos[...])
    h_x.wait_recv()
    resid[...] = ctx[2, pl.ds(pl.multiple_of(c * N, N), N), :].astype(F32) + (own_part + got[...])
    leave(resid, resid_o)
    xhat2, _ = layer_norm_rows(resid[...])
    sec[pl.ds(0, N), :] = (xhat2 * g2[...] + b2[...]).astype(BF)

    as_, ar, afs, afr = al.take(Q), al.take(Q), al.take(Q), al.take(Q)

    def a_p(k):
        return rcopy(slot(sec, 0, 0), slot(sec, k, 0), as_(k), ar(k), peer(k))

    def a_f(k):
        return rcopy(slot(sec, k, 0), slot(sec, k, 1), afs(k), afr(k), (sib, z))

    for k in range(1, Q):
        t_p(k).wait_recv()
        t_f(k).start()
    for k in range(1, Q - 1):
        a_p(k).start()
    a_f(0).start()
    sqc = al.take(RATE)
    sqs = [dns.at[pl.ds(0, D), :], dns.at[pl.ds(D, D), :], gbuf.at[pl.ds(D, D), :]]
    sq_x = [lcopy(sq.at[pl.ds(r * D, D), :], sqs[r], sqc(r)) for r in range(RATE)]
    for x in sq_x:
        x.start()
    for r in range(1, Z):
        u_z(r).wait()
        for i in range(2):
            x_z(i, r).wait_recv()
    u_l.wait()
    for x in x_l:
        x.wait()
    ss, sr = al.take(Q), al.take(Q)
    gps, gpr = al.take(Q), al.take(Q)

    def s_x(k):
        return rcopy(slot(gbuf, k, 1), got1.at[k], ss(k), sr(k), (sib, z))

    def p_x(k):
        return rcopy(send2.at[k - 1], got2.at[k - 1], gps(k), gpr(k), peer(k))

    bias_row = jnp.concatenate([ubs[r] for r in range(Z)], axis=1)
    small_o[...] = jnp.zeros_like(small_o)

    def forward_block(b, carry):
        at = pl.ds(pl.multiple_of(b * N, N), N)
        x = nn_dot(sec[at, :], ups[...]) + bias_row
        ga = nt_dot(cots[at, :], downs[...])
        x2 = x * x
        root = 0.7978845608028654
        th = jnp.tanh(root * (x + 0.044715 * (x2 * x)))
        act[at, :] = (0.5 * x * (1.0 + th)).astype(BF)
        slope = 0.5 * (1.0 + th) + 0.5 * x * (1.0 - th * th) * (root * (1.0 + 0.134145 * x2))
        gu = (ga * slope).astype(BF)
        gup[at, :] = gu
        small_o[2:3, pl.ds(0, Z * E)] = small_o[2:3, pl.ds(0, Z * E)] + jnp.sum(gu.astype(F32), axis=0, keepdims=True)
        gbuf[at, :] = nt_dot(gu, ups[...]).astype(BF)
        return carry

    def feed(k):
        lax.fori_loop(2 * k, 2 * k + 2, forward_block, 0)
        s_x(k).start()

    def combine(k):
        s_x(k).wait_recv()
        send2[k - 1] = (gbuf[pl.ds(2 * k * N, N), :].astype(F32) + got1[k].astype(F32)).astype(BF)
        p_x(k).start()

    t_f(0).wait_recv()
    a_f(0).wait_recv()
    feed(0)

    groups = S // RATE
    squeezed = None
    for r in range(RATE):
        sq_x[r].wait()
        row = lax.broadcasted_iota(jnp.int32, (ncs.shape[0], S), 0)
        col = lax.broadcasted_iota(jnp.int32, (ncs.shape[0], S), 1)
        pick = jnp.where((col == row * RATE + r) & (row < groups), 1.0, 0.0).astype(BF)
        picked = nn_dot(pick, ctx[1]).astype(BF)
        term = nn_dot(picked, sqs[r][...])
        squeezed = term if squeezed is None else squeezed + term
    ncs[...] = squeezed.astype(BF)
    shift = count + c * N
    new_mem = nn_dot(one_hot((N, S), shift), ctx[1]) + nn_dot(one_hot((N, S), shift - S), ctx[2])
    nms[...] = new_mem.astype(BF)
    third = lax.shift_right_logical(count * 21846, 16)
    shift = third + c * N
    new_comp = nn_dot(one_hot((N, S), shift), ctx[0]) + nn_dot(one_hot((N, ncs.shape[0]), shift - S), ncs[...])
    ncs[pl.ds(0, N), :] = new_comp.astype(BF)
    per = N // R
    ms, mr, ml = al.take(2, 2), al.take(2, B), al.take(2)
    rows_in = [nms, ncs]
    rows_out = [nm_o, nc_o]

    def row_x(i, p):
        return rcopy(rows_in[i].at[pl.ds(p * R, R), :], rows_out[i].at[jz], ms(i, p), mr(i, jz), (2 * q + z // B, c * per + p))

    def row_l(i, p):
        return lcopy(rows_in[i].at[pl.ds(p * R, R), :], rows_out[i].at[jz], ml(i))

    for p in range(per):
        here = (c * per + p == z) & mine

        @pl.when(here)
        def _():
            for i in range(2):
                row_l(i, p).start()

        @pl.when(jnp.logical_not(here))
        def _():
            for i in range(2):
                row_x(i, p).start()

    for k in range(1, Q):
        a_p(k).wait_recv()
        if k == Q - 2:
            a_p(Q - 1).start()
        a_f(k).start()
        t_f(k).wait_recv()
        a_f(k).wait_recv()
        feed(k)
        if k > 1:
            combine(k - 1)
    combine(Q - 1)

    def up_grad(i, carry):
        at = pl.ds(pl.multiple_of(i * T, T), T)
        gus[at, :] = tn_dot(sec[:, at], gup[...]).astype(BF)
        return carry

    lax.fori_loop(0, D // T, up_grad, 0)
    leave(gus, gu_o)

    def down_grad(i, carry):
        at = pl.ds(pl.multiple_of(i * T, T), T)
        gds[at, :] = tn_dot(act[:, at], cots[...]).astype(BF)
        return carry

    lax.fori_loop(0, Z * E // T, down_grad, 0)
    leave(gds, gd_o)

    def down_rows(b, carry):
        at = pl.ds(pl.multiple_of(b * N, N), N)
        dns[at, :] = nn_dot(act[at, :], downs[...]).astype(BF)
        return carry

    lax.fori_loop(0, 2 * Q, down_rows, 0)
    leave(dns, down_o)

    s_x(0).wait_recv()
    for k in range(1, Q):
        p_x(k).wait_recv()
    C = 64

    def back_rows(i, carry):
        at = pl.ds(pl.multiple_of(i * C, C), C)
        gs = gbuf[at, :].astype(F32) + got1[0, at, :].astype(F32)
        for k in range(1, Q):
            gs = gs + got2[k - 1, at, :].astype(F32)
        xhat, inv = layer_norm_rows(resid[at, :])
        small_o[0:1, :] = small_o[0:1, :] + jnp.sum(gs * xhat, axis=0, keepdims=True)
        small_o[1:2, :] = small_o[1:2, :] + jnp.sum(gs, axis=0, keepdims=True)
        e = gs * g2[...]
        m1 = jnp.mean(e, axis=-1, keepdims=True)
        m2 = jnp.mean(e * xhat, axis=-1, keepdims=True)
        gr = cots[at, :].astype(F32) + inv * (e - m1 - xhat * m2)
        got[at, :] = gr
        low[at, :] = gr.astype(BF)
        return carry

    lax.fori_loop(0, N // C, back_rows, 0)
    leave(got, gresid_o)
    ls_, lr_, ll_ = al.take(1), al.take(1), al.take(1)
    mine_rows = glow_o.at[pl.ds(pl.multiple_of(c * N, N), N), :]
    far = rcopy(low, mine_rows, ls_(0), lr_(0), (sib, z))
    near = lcopy(low, mine_rows, ll_(0))
    far.start()
    near.start()

    for cp in copies:
        cp.wait()
    for h in range(heads):
        for half, tag in ((1 - c, 0), (c, 1)):
            rows = pl.ds(pl.multiple_of(half * N, N), N)
            lcopy(probs.at[h, rows, :], probs_o.at[h, rows, :], pouts(tag, h)).wait()

    @pl.when(mine)
    def _():
        for a in range(4):
            for r in range(1, Z):
                w_z(a, r).wait_send()
        for t in range(3):
            c_sib(t).wait_send()
    for j in range(B):
        @pl.when(B * c + j != z)
        def _():
            for a in range(4):
                for k in range(1, Q):
                    w_p(a, j, k, q).wait_send()
    for r in range(1, Z):
        for t in range(3):
            c_fwd(t, lax.rem(z + r, Z), c).wait_send()
        for i in range(2):
            x_z(i, r).wait_send()
    for s in range(B):
        @pl.when(jnp.logical_not((B * c + s == z) & mine))
        def _():
            t_z(s).wait_send()
    for k in range(1, Q):
        t_p(k).wait_send()
        a_p(k).wait_send()
        p_x(k).wait_send()
    for k in range(Q):
        t_f(k).wait_send()
        a_f(k).wait_send()
        s_x(k).wait_send()
    h_x.wait_send()
    for p in range(per):
        here = (c * per + p == z) & mine

        @pl.when(here)
        def _():
            for i in range(2):
                row_l(i, p).wait()

        @pl.when(jnp.logical_not(here))
        def _():
            for i in range(2):
                row_x(i, p).wait_send()
    for s in range(B):
        @pl.when(jnp.logical_not((B * c + s == z) & mine))
        def _():
            for i in range(2):
                rcopy(rows_out[i].at[s], rows_out[i].at[s], ms(i, 0), mr(i, s), (dp, z)).wait_recv()
    near.wait()
    far.wait()
    assert al.used <= FRONT_SEMS


def front(Q, Z, comp, mem, tok, cot, wq, wk, wv, wo, up, down, ub, vc, sq, g1, b1, g2, b2):
    B, R, D = tok.shape
    H = wq.shape[1]
    S = R * Z
    N = S // 2
    W = B * H
    heads = W // HEAD_DIM
    F = up.shape[1] // 2 // Q * Z
    rows = 2 * Q * N
    vm = pltpu.VMEM
    return pl.pallas_call(
        functools.partial(front_kernel, Q, Z),
        out_shape=[
            sds((S, D), BF), sds((3 * S, D), BF), sds((S, W), BF), sds((3 * S, W), BF), sds((3 * S, W), BF),
            sds((heads, S, 3 * S), BF), sds((S, W), BF), sds((D, W), BF), sds((D, W), BF), sds((D, W), BF), sds((W, D), BF),
            sds((N, D), F32), sds((N, D), F32), sds((S, D), BF), sds((D, F), BF), sds((F, D), BF), sds((rows, D), BF),
            sds((8, D), F32), sds((B, R, D), BF), sds((B, R, D), BF),
        ],
        in_specs=[ANY] * 11 + [VM] + [ANY] + [VM] * 4,
        out_specs=[ANY] * 17 + [VM] + [ANY] * 2,
        scratch_shapes=[
            vm((3, S, D), BF), vm((3 * S, D), BF), vm((D, W), BF), vm((D, W), BF), vm((D, W), BF), vm((W, D), BF),
            vm((S, W), BF), vm((3 * S, W), BF), vm((3 * S, W), BF), vm((heads, S, 3 * S), BF), vm((S, W), BF),
            vm((N, D), F32), vm((N, D), F32), vm((N, D), F32), vm((rows, D), BF), vm((rows, D), BF), vm((D, F), BF), vm((F, D), BF),
            vm((Z, 1, F // Z), F32), vm(vc.shape, jnp.int32), vm((rows, F), BF), vm((rows, F), BF), vm((rows, D), BF),
            vm((Q, N, D), BF), vm((Q - 1, N, D), BF), vm((Q - 1, N, D), BF), vm((N, D), BF),
            vm((N, D), BF), vm((N, D), BF), vm((D, F), BF), vm((F, D), BF), vm((rows, D), BF),
            DMA((FRONT_SEMS,)),
        ],
        compiler_params=pltpu.CompilerParams(collective_id=1, has_side_effects=True, vmem_limit_bytes=63 << 20),
        name="front",
    )(comp, mem, tok, cot, wq, wk, wv, wo, up, down, ub, vc, sq, g1, b1, g2, b2)


class PlaneSum:
    def __init__(self, al, peer, blk, rows, h, g):
        self.peer, self.blk, self.half, self.rows, self.h, self.g = peer, blk, rows // 2, rows, h, g
        self.hs, self.hr, self.gs, self.gr = al.take(2), al.take(2), al.take(2), al.take(2)

    def h_x(self, i):
        return rcopy(self.blk(3, i * self.half, self.half), self.h.at[i], self.hs(i), self.hr(i), self.peer(i + 1))

    def g_x(self, i):
        return rcopy(self.blk(i + 1, 0, self.rows), self.g.at[i], self.gs(i), self.gr(i), self.peer(i + 1))

    def start(self):
        for i in range(2):
            self.h_x(i).start()

    def middle(self):
        for i in range(2):
            self.h_x(i).wait_recv()
            mine = self.blk(2 - i, i * self.half, self.half)
            mine[...] = (mine[...].astype(F32) + self.h[i].astype(F32)).astype(BF)
            self.g_x(1 - i).start()

    def total(self):
        for i in range(2):
            self.g_x(i).wait_recv()
        own = self.blk(0, 0, self.rows)
        return own[...].astype(F32) + (self.g[0].astype(F32) + self.g[1].astype(F32))

    def drain(self):
        for i in range(2):
            self.h_x(i).wait_send()
            self.g_x(i).wait_send()


class PlaneGather:
    def __init__(self, al, peer, sib, loc, rows, own=None):
        self.peer, self.sib, self.loc, self.half, self.rows = peer, sib, loc, rows // 2, rows
        self.own = own
        self.as_, self.ar, self.hs, self.hr = al.take(2), al.take(2), al.take(2), al.take(2)
        self.fs, self.fr = al.take(4), al.take(4)

    def a_x(self, i, k=0):
        src = self.loc(0, 0, self.rows) if self.own is None else self.own
        return rcopy(src, self.loc(k, 0, self.rows), self.as_(i), self.ar(i), self.peer(i + 1))

    def h_x(self, i, k=None):
        k = 2 - (1 - i) if k is None else k
        rows = self.loc(k, i * self.half, self.half)
        return rcopy(rows, rows, self.hs(i), self.hr(i), self.peer(2 - i))

    def f_x(self, k, other=None):
        src = self.loc(k, 0, self.rows)
        if k == 0 and self.own is not None:
            src = self.own
        dst = self.loc(k, 0, self.rows) if other is None else other(k, 0, self.rows)
        return rcopy(src, dst, self.fs(k), self.fr(k), self.sib)

    def start(self):
        for i in range(2):
            self.a_x(i).start()
        self.f_x(0).start()

    def middle(self):
        for i in range(2):
            rcopy(self.loc(i + 1, 0, self.rows), self.loc(i + 1, 0, self.rows), self.as_(i), self.ar(i), self.peer(1)).wait_recv()
            self.h_x(i).start()
            self.f_x(i + 1).start()

    def last(self):
        for i in range(2):
            self.h_x(i, 3).wait_recv()
        self.f_x(3).start()

    def drain(self):
        for i in range(2):
            self.a_x(i).wait_send()
            self.h_x(i).wait_send()
        for k in range(4):
            self.f_x(k).wait_send()

    def arrivals(self, other):
        for k in range(4):
            rcopy(other(k, 0, self.rows), other(k, 0, self.rows), self.fs(k), self.fr(k), self.sib).wait_recv()


BACK_SEMS = 300


def back_kernel(Q, Z, B, tok, normed_i, q_i, k_i, v_i, probs_i, mixed_i, wq_i, wk_i, wv_i, wo_i, resid_i, gresid_i, glow_i,
                gu, gd, down_i, ffs, cot, g1, b1, db,
                aw, ago, afu, afd, aub, small_o, out_o, tg_o,
                normed, qs, ks, vs, probs, mixed, wqs, wks, wvs, wos, toks, resid, gresid, glow, gms,
                xu, xd, xb, fus, fds, fbs, dgot, dnb, dh, dg, gkv, gqs, gos, gwb, gh, gg, oh, og,
                wdone, odone, zb, zo, wfin, ofin, ghalf, ggot, cots, arow, sums, sgot, srow, pgot, zgot, outs, tgs, sems):
    dp, c, q, z = where_am_i(Q, Z)
    sib = (dp + 1 - 2 * c, z)
    partners = [sib]
    for r in range(1, Z):
        for d in (dp, dp + 1 - 2 * c):
            partners.append((d, lax.rem(z + r, Z)))

    def peer(k):
        return (2 * across(q, k) + c, z)

    for k in range(1, Q):
        partners.append(peer(k))
    enter(partners)
    S, D = glow.shape
    N = S // 2
    W = qs.shape[1]
    H = W // B
    F = gd.shape[0]
    E = F // Z
    R = S // Z
    heads = W // HEAD_DIM
    hj = H // HEAD_DIM
    mine = c == z // B
    jz = lax.rem(z, B)
    al = Slots(sems)

    def up_to_z(r):
        return (dp, lax.rem(z + Z - r, Z))

    xs, xr = al.take(3, Z), al.take(3, Z)

    def x_z(i, r):
        if i == 0:
            return rcopy(gu.at[:, pl.ds(r * E, E)], xu.at[r], xs(0, r), xr(0, r), up_to_z(r))
        if i == 1:
            return rcopy(gd.at[pl.ds(r * E, E), :], xd.at[r], xs(1, r), xr(1, r), up_to_z(r))
        return rcopy(ffs.at[pl.ds(2, 1), pl.ds(r * E, E)], xb.at[r], xs(2, r), xr(2, r), up_to_z(r))

    ss, sr = al.take(Q), al.take(Q)

    def d_x(k):
        return rcopy(down_i.at[pl.ds((2 * k + 1) * N, N), :], dgot.at[k], ss(k), sr(k), sib)

    ld = al.take(30)
    pairs = [(wo_i, wos), (glow_i, glow), (mixed_i, mixed), (probs_i, probs), (v_i, vs), (k_i, ks), (q_i, qs),
             (normed_i, normed), (wq_i, wqs), (wk_i, wks), (wv_i, wvs), (gresid_i, gresid), (resid_i, resid),
             (tok.at[pl.ds(pl.multiple_of(c * N, N), N), :], toks), (cot, cots),
             (gu.at[:, pl.ds(0, E)], xu.at[0]), (gd.at[pl.ds(0, E), :], xd.at[0])]
    pairs += [(down_i.at[pl.ds(2 * k * N, N), :], dnb.at[k]) for k in range(Q)]
    loads = [lcopy(src, dst, ld(i)) for i, (src, dst) in enumerate(pairs)]
    for x in loads[:3]:
        x.start()
    for k in (3, 1, 2, 0):
        d_x(k).start()
    for x in loads[3:]:
        x.start()
    for r in range(1, Z):
        for i in range(3):
            x_z(i, r).start()

    for x in loads[:3]:
        x.wait()
    T = 256

    def mix_rows(i, carry):
        at = pl.ds(pl.multiple_of(i * T, T), T)
        gms[at, :] = nt_dot(glow[at, :], wos[...]).astype(BF)
        gos[at, :] = tn_dot(mixed[:, at], glow[...]).astype(BF)
        return carry

    lax.fori_loop(0, S // T, mix_rows, 0)
    OR = H // Q
    M = D // Q

    def o_blk(j):
        def blk(k, lo, n):
            return gos.at[pl.ds(pl.multiple_of(j * H + across(q, k) * OR + lo, n), n), :]
        return blk

    def w_blk(j):
        def blk(k, lo, n):
            return gwb.at[j, pl.ds(pl.multiple_of(across(q, k) * M + lo, n), n), :]
        return blk

    osum = [PlaneSum(al, peer, o_blk(j), OR, oh.at[j], og.at[j]) for j in range(B)]
    wsum = [PlaneSum(al, peer, w_blk(j), M, gh.at[j], gg.at[j]) for j in range(B)]
    dsum = PlaneSum(al, peer, lambda k, lo, n: dnb.at[k, pl.ds(lo, n), :], N, dh, dg)
    for x in osum:
        x.start()
    sums[...] = jnp.zeros_like(sums)
    arow[...] = jnp.zeros_like(arow)
    scale = HEAD_DIM ** (-0.5)

    def head(h, hh):
        hd = pl.ds(h * HEAD_DIM, HEAD_DIM)
        ko = pl.ds(hh * HEAD_DIM, HEAD_DIM)
        vo = pl.ds(H + hh * HEAD_DIM, HEAD_DIM)
        p = probs[h]
        gm = gms[:, hd]
        gp = nt_dot(gm, vs[:, hd])
        delta = jnp.sum(gm.astype(F32) * mixed[:, hd].astype(F32), axis=-1, keepdims=True)
        gs = (p.astype(F32) * (gp - delta)).astype(BF)
        gqs[:, hd] = (scale * nn_dot(gs, ks[:, hd])).astype(BF)
        gkv[:, ko] = (scale * tn_dot(gs, qs[:, hd])).astype(BF)
        gkv[:, vo] = tn_dot(p, gm).astype(BF)

    def split_rows(v):
        hi = v.astype(BF)
        rest = v - hi.astype(F32)
        mid = rest.astype(BF)
        low = (rest - mid.astype(F32)).astype(BF)
        return jnp.concatenate([hi, mid, low, jnp.zeros((5, v.shape[1]), BF)], axis=0)

    def weights(j):
        js = pl.ds(j * H, H)

        def rows(i, carry):
            at = pl.ds(pl.multiple_of(i * T, T), T)
            kv = tn_dot(normed[:, at], gkv[...])
            gq = tn_dot(normed[pl.ds(2 * S, S), at], gqs[:, js])
            gwb[j, at, pl.ds(0, 2 * H)] = kv.astype(BF)
            gwb[j, at, pl.ds(2 * H, H)] = gq.astype(BF)
            t = (kv[:, :H] * wks[at, js].astype(F32) + kv[:, H:] * wvs[at, js].astype(F32) + gq * wqs[at, js].astype(F32))
            arow[at, :] = arow[at, :] + jnp.broadcast_to(jnp.sum(t, axis=-1, keepdims=True), (T, 128))
            return carry

        lax.fori_loop(0, D // T, rows, 0)
        wsum[j].start()
        skv = split_rows(jnp.sum(gkv[...].astype(F32), axis=0, keepdims=True))
        sq_ = split_rows(jnp.sum(gqs[:, js].astype(F32), axis=0, keepdims=True))
        b = nt_dot(skv[:, :H], wks[:, js]) + nt_dot(skv[:, H:], wvs[:, js]) + nt_dot(sq_, wqs[:, js])
        sums[1:2, :] = sums[1:2, :] + jnp.sum(b, axis=0, keepdims=True)

    for x in loads[3:7]:
        x.wait()
    for h in range(hj):
        head(h, h)
    for x in osum:
        x.middle()
    for x in loads[17:]:
        x.wait()
    for k in (3, 1, 2, 0):
        d_x(k).wait_recv()
        dnb[k] = (dnb[k].astype(F32) + dgot[k].astype(F32)).astype(BF)
    for x in loads[7:11]:
        x.wait()
    H2 = pl.ds(2 * S, S)

    def token_rows(j, half):
        js = pl.ds(j * H, H)
        rows = pl.ds(pl.multiple_of(half * N, N), N)
        krows = pl.ds(pl.multiple_of(2 * S + half * N, N), N)
        return (nt_dot(gkv[krows, pl.ds(0, H)], wks[:, js]) + nt_dot(gkv[krows, pl.ds(H, H)], wvs[:, js])
                + nt_dot(gqs[rows, js], wqs[:, js]))

    weights(0)
    ghalf[...] = token_rows(0, 1 - c)
    srow[...] = token_rows(0, c)
    dsum.start()
    for h in range(hj, 2 * hj):
        head(h, h - hj)
    wsum[0].middle()
    weights(1)
    dsum.middle()
    ghalf[...] = ghalf[...] + token_rows(1, 1 - c)
    ts_, tr_ = al.take(1), al.take(1)
    t_x = rcopy(ghalf, ggot, ts_(0), tr_(0), sib)
    t_x.start()
    srow[...] = srow[...] + token_rows(1, c)

    for x in loads[11:17]:
        x.wait()
    acol = jnp.swapaxes(arow[...], 0, 1)[0:1, :]
    bsum = sums[1:2, :]
    sums[0:1, :] = (acol - b1[...] * bsum) / g1[...]
    sums[2:3, :] = ffs[0:1, :]
    sums[3:4, :] = ffs[1:2, :]
    sums[4:5, :] = jnp.sum(cots[...].astype(F32), axis=(0, 1)).reshape(1, D)
    n1, n2 = al.take(1), al.take(1)
    v_x = rcopy(sums, sgot, n1(0), n2(0), sib)
    v_x.start()
    osums = []
    ozs, ozr = al.take(2, B), al.take(2, Z)

    def z_x(i, j):
        src, dst = ((wdone, zb), (odone, zo))[i]
        return rcopy(src.at[j], dst.at[z], ozs(i, j), ozr(i, z), (dp, B * c + j))

    def z_arrive(i, zz):
        dst = (zb, zo)[i]
        return rcopy(dst.at[zz], dst.at[zz], ozs(i, 0), ozr(i, zz), (dp, z))

    def to_plane(i, j):
        ((wdone, odone)[i])[j] = ((wsum, osum)[i])[j].total().astype(BF)

        @pl.when(B * c + j != z)
        def _():
            z_x(i, j).start()

    wsum[1].middle()
    for j in range(B):
        to_plane(1, j)
    t_x.wait_recv()
    C = 64

    def norm_rows(i, carry):
        at = pl.ds(pl.multiple_of(i * C, C), C)
        gn = srow[at, :] + ggot[at, :]
        xhat, inv = layer_norm_rows(toks[at, :].astype(F32))
        e = gn * g1[...]
        m1 = jnp.mean(e, axis=-1, keepdims=True)
        m2 = jnp.mean(e * xhat, axis=-1, keepdims=True)
        tgs[at, :] = (gresid[at, :] + inv * (e - m1 - xhat * m2)).astype(BF)
        return carry

    lax.fori_loop(0, N // C, norm_rows, 0)
    per = N // R
    rs, rr, rl = al.take(2, 2), al.take(2, B), al.take(2)
    rows_in = [tgs, outs]
    rows_out = [tg_o, out_o]

    def row_x(i, p):
        return rcopy(rows_in[i].at[pl.ds(p * R, R), :], rows_out[i].at[jz], rs(i, p), rr(i, jz), (2 * q + z // B, c * per + p))

    def row_l(i, p):
        return lcopy(rows_in[i].at[pl.ds(p * R, R), :], rows_out[i].at[jz], rl(i))

    def send_rows(i):
        for p in range(per):
            here = (c * per + p == z) & mine

            @pl.when(here)
            def _():
                row_l(i, p).start()

            @pl.when(jnp.logical_not(here))
            def _():
                row_x(i, p).start()

    send_rows(0)
    for r in range(1, Z):
        for i in range(3):
            x_z(i, r).wait_recv()
    fu, fd, fb = xu[0].astype(F32), xd[0].astype(F32), ffs[2:3, 0:E]
    for r in range(1, Z):
        fu = fu + xu[r].astype(F32)
        fd = fd + xd[r].astype(F32)
        fb = fb + xb[r]
    fus[...] = fu.astype(BF)
    fds[...] = fd.astype(BF)
    fbs[...] = fb

    def dev(k, core):
        return 2 * across(q, k) + core

    def u_loc(core):
        def loc(k, lo, n):
            return afu.at[pl.ds(lo, n), pl.ds(pl.multiple_of(dev(k, core) * E, E), E)]
        return loc

    def d_loc(core):
        def loc(k, lo, n):
            return afd.at[pl.ds(pl.multiple_of(dev(k, core) * E + lo, n), n), :]
        return loc

    ugat = PlaneGather(al, peer, sib, u_loc(c), D, own=fus)
    dgat = PlaneGather(al, peer, sib, d_loc(c), E, own=fds)
    fl = al.take(3)
    f_l = [lcopy(fus, u_loc(c)(0, 0, D), fl(0)), lcopy(fds, d_loc(c)(0, 0, E), fl(1))]
    bs, br, bfs, bfr = al.take(Q), al.take(Q), al.take(Q), al.take(Q)

    def b_x(k):
        return rcopy(fbs, aub.at[dp], bs(k), br(k), peer(k))

    def b_arrive(k):
        return rcopy(aub.at[dev(k, c)], aub.at[dev(k, c)], bs(k), br(k), peer(k))

    def b_f(k):
        src = fbs if k == 0 else aub.at[dev(k, c)]
        return rcopy(src, aub.at[dev(k, c)], bfs(k), bfr(k), sib)

    b_l = lcopy(fbs, aub.at[dp], fl(2))
    ugat.start()
    dgat.start()
    for x in f_l:
        x.start()
    b_l.start()
    for k in range(1, Q):
        b_x(k).start()
    b_f(0).start()
    v_x.wait()
    srow[0:8, :] = sums[...] + sgot[...]
    pgot[q] = srow[0:8, :]
    vps, vpr, vzs, vzr = al.take(Q), al.take(Q), al.take(Z), al.take(Z)

    def vp_x(k):
        return rcopy(srow.at[pl.ds(0, 8), :], pgot.at[q], vps(k), vpr(k), peer(k))

    def vp_arrive(k):
        return rcopy(pgot.at[across(q, k)], pgot.at[across(q, k)], vps(k), vpr(k), peer(k))

    def vz_x(r):
        return rcopy(srow.at[pl.ds(8, 8), :], zgot.at[z], vzs(r), vzr(r), (dp, lax.rem(z + r, Z)))

    def vz_arrive(r):
        zz = lax.rem(z + Z - r, Z)
        return rcopy(zgot.at[zz], zgot.at[zz], vzs(r), vzr(r), (dp, z))

    for k in range(1, Q):
        vp_x(k).start()
    for i in range(2):
        pass
    outs[...] = (resid[...] + dsum.total() + db[...]).astype(BF)
    send_rows(1)
    to_plane(0, 0)
    for k in range(1, Q):
        vp_arrive(k).wait_recv()
    psum = pgot[0]
    for k in range(1, Q):
        psum = psum + pgot[k]
    srow[8:16, :] = psum
    zgot[z] = psum
    for r in range(1, Z):
        vz_x(r).start()
    to_plane(0, 1)

    def a_loc(ref, n_rows):
        def loc(k, lo, n):
            return ref.at[pl.ds(pl.multiple_of(across(q, k) * n_rows + lo, n), n), :]
        return loc

    wgat = PlaneGather(al, peer, sib, a_loc(aw, M), M, own=wfin)
    ogat = PlaneGather(al, peer, sib, a_loc(ago, OR), OR, own=ofin)
    gl = al.take(2)
    g_l = [lcopy(wfin, a_loc(aw, M)(0, 0, M), gl(0)), lcopy(ofin, a_loc(ago, OR)(0, 0, OR), gl(1))]

    @pl.when(mine)
    def _():
        for i, (fin, done, buf, gat) in ((1, (ofin, odone, zo, ogat)), (0, (wfin, wdone, zb, wgat))):
            for zz in range(Z):
                @pl.when(zz != z)
                def _():
                    z_arrive(i, zz).wait_recv()
            buf[z] = done[jz]
            t = buf[0].astype(F32)
            for zz in range(1, Z):
                t = t + buf[zz].astype(F32)
            fin[...] = t.astype(BF)
            gat.start()
            g_l[1 if i == 1 else 0].start()
    for gat in (ugat, dgat):
        gat.middle()
    for k in range(1, Q):
        b_arrive(k).wait_recv()
        b_f(k).start()
    for r in range(1, Z):
        vz_arrive(r).wait_recv()
    zsum = zgot[0]
    for zz in range(1, Z):
        zsum = zsum + zgot[zz]
    small_o[...] = zsum

    @pl.when(mine)
    def _():
        for gat in (ogat, wgat):
            gat.middle()
    for gat in (ugat, dgat):
        gat.last()

    @pl.when(mine)
    def _():
        for gat in (ogat, wgat):
            gat.last()
    ugat.arrivals(u_loc(1 - c))
    dgat.arrivals(d_loc(1 - c))

    @pl.when(jnp.logical_not(mine))
    def _():
        ogat.arrivals(a_loc(ago, OR))
        wgat.arrivals(a_loc(aw, M))

    for k in range(Q):
        rcopy(aub.at[dev(k, 1 - c)], aub.at[dev(k, 1 - c)], bfs(k), bfr(k), sib).wait_recv()
        b_f(k).wait_send()
        d_x(k).wait_send()
    for k in range(1, Q):
        b_x(k).wait_send()
        vp_x(k).wait_send()
    b_l.wait()
    for x in f_l:
        x.wait()
    for r in range(1, Z):
        vz_x(r).wait_send()
        for i in range(3):
            x_z(i, r).wait_send()
    for x in osum + wsum + [dsum, ugat, dgat]:
        x.drain()

    @pl.when(mine)
    def _():
        for x in (ogat, wgat):
            x.drain()
        for x in g_l:
            x.wait()
    t_x.wait_send()
    for j in range(B):
        @pl.when(B * c + j != z)
        def _():
            for i in range(2):
                z_x(i, j).wait_send()
    for p in range(per):
        here = (c * per + p == z) & mine

        @pl.when(here)
        def _():
            for i in range(2):
                row_l(i, p).wait()

        @pl.when(jnp.logical_not(here))
        def _():
            for i in range(2):
                row_x(i, p).wait_send()
    for s in range(B):
        @pl.when(jnp.logical_not((B * c + s == z) & mine))
        def _():
            for i in range(2):
                rcopy(rows_out[i].at[s], rows_out[i].at[s], rs(i, 0), rr(i, s), (dp, z)).wait_recv()
    assert al.used <= BACK_SEMS


def back(Q, Z, B, tok, normed, q_, k_, v_, probs, mixed, wq, wk, wv, wo, resid, gresid, glow, gu, gd, down, ffs, cot, g1, b1, db):
    S, D = glow.shape
    N, R = S // 2, S // Z
    W = q_.shape[1]
    H = W // B
    F = gd.shape[0]
    E = F // Z
    heads = W // HEAD_DIM
    M, OR = D // Q, H // Q
    vm = pltpu.VMEM
    return pl.pallas_call(
        functools.partial(back_kernel, Q, Z, B),
        out_shape=[
            sds((D, 3 * H), BF), sds((H, D), BF), sds((D, 2 * Q * E), BF), sds((2 * Q * E, D), BF), sds((2 * Q, 1, E), F32),
            sds((8, D), F32), sds((B, R, D), BF), sds((B, R, D), BF),
        ],
        in_specs=[ANY] * 17 + [VM] + [ANY] + [VM] * 3,
        out_specs=[ANY] * 5 + [VM] + [ANY] * 2,
        scratch_shapes=[
            vm((3 * S, D), BF), vm((S, W), BF), vm((3 * S, W), BF), vm((3 * S, W), BF), vm((heads, S, 3 * S), BF), vm((S, W), BF),
            vm((D, W), BF), vm((D, W), BF), vm((D, W), BF), vm((W, D), BF),
            vm((N, D), BF), vm((N, D), F32), vm((N, D), F32), vm((S, D), BF), vm((S, W), BF),
            vm((Z, D, E), BF), vm((Z, E, D), BF), vm((Z, 1, E), F32), vm((D, E), BF), vm((E, D), BF), vm((1, E), F32),
            vm((Q, N, D), BF), vm((Q, N, D), BF), vm((2, N // 2, D), BF), vm((2, N, D), BF),
            vm((3 * S, 2 * H), BF), vm((S, W), BF), vm((W, D), BF), vm((B, D, 3 * H), BF),
            vm((B, 2, M // 2, 3 * H), BF), vm((B, 2, M, 3 * H), BF), vm((B, 2, OR // 2, D), BF), vm((B, 2, OR, D), BF),
            vm((B, M, 3 * H), BF), vm((B, OR, D), BF), vm((Z, M, 3 * H), BF), vm((Z, OR, D), BF), vm((M, 3 * H), BF), vm((OR, D), BF),
            vm((N, D), F32), vm((N, D), F32), vm(cot.shape, BF), vm((D, 128), F32),
            vm((8, D), F32), vm((8, D), F32), vm((N, D), F32), vm((Q, 8, D), F32), vm((Z, 8, D), F32), vm((N, D), BF), vm((N, D), BF),
            DMA((BACK_SEMS,)),
        ],
        compiler_params=pltpu.CompilerParams(collective_id=2, has_side_effects=True, vmem_limit_bytes=63 << 20),
        name="back",
    )(tok, normed, q_, k_, v_, probs, mixed, wq, wk, wv, wo, resid, gresid, glow, gu, gd, down, ffs, cot, g1, b1, db)


def chip_device(Q, Z, tokens, memory, compressed, valid_counts, attention_norm_gain, attention_norm_bias,
                query_projection, key_projection, value_projection, out_weight, feedforward_norm_gain,
                feedforward_norm_bias, up_weight, up_bias, down_weight, down_bias, squeeze_weight, cotangent):
    B, R, D = tokens.shape
    H = query_projection.shape[1]
    FL = up_weight.shape[1]
    E = FL // (2 * Q)
    (tok_all, normed, q_, k_, v_, probs, mixed, wqg, wkg, wvg, wog, resid, g_resid, g_low, up_low, down_g_low, down,
     ff_small, o_nm, o_nc) = front(
        Q, Z, compressed, memory, tokens, cotangent, query_projection, key_projection, value_projection, out_weight,
        up_weight, down_weight, up_bias.reshape(2 * Q, 1, E), jnp.broadcast_to(valid_counts[:, None, None], (B, 8, 128)),
        squeeze_weight, attention_norm_gain.reshape(1, D), attention_norm_bias.reshape(1, D),
        feedforward_norm_gain.reshape(1, D), feedforward_norm_bias.reshape(1, D),
    )
    aw, ago, afu, afd, aub, small, o_out, o_tg = back(
        Q, Z, B, tok_all, normed, q_, k_, v_, probs, mixed, wqg, wkg, wvg, wog, resid, g_resid, g_low, up_low, down_g_low, down,
        ff_small, cotangent, attention_norm_gain.reshape(1, D), attention_norm_bias.reshape(1, D), down_bias.reshape(1, D),
    )
    aw = aw.astype(F32)
    return (
        o_out, o_tg.astype(F32), small[0], small[1], aw[:, 2 * H:], aw[:, :H], aw[:, H:2 * H], ago.astype(F32),
        small[2], small[3], afu.astype(F32), aub.reshape(FL), afd.astype(F32), small[4], o_nm, o_nc,
    )


def solution(mesh):
    in_specs = (
        P("dp", "mp", None),
        P("dp", "mp", None),
        P("dp", "mp", None),
        P("dp"),
        P(),
        P(),
        P(None, "mp"),
        P(None, "mp"),
        P(None, "mp"),
        P("mp", None),
        P(),
        P(),
        P(None, "mp"),
        P("mp"),
        P("mp", None),
        P(),
        P(),
        P("dp", "mp", None),
    )
    out_specs = (
        P("dp", "mp", None),
        P("dp", "mp", None),
        P(),
        P(),
        P(None, "mp"),
        P(None, "mp"),
        P(None, "mp"),
        P("mp", None),
        P(),
        P(),
        P(None, "mp"),
        P("mp"),
        P("mp", None),
        P(),
        P("dp", "mp", None),
        P("dp", "mp", None),
    )
    Q, Z = mesh.shape["dp"] // 2, mesh.shape["mp"]

    def per_device(*args):
        B, R, D = args[0].shape
        H, FL = args[6].shape[1], args[12].shape[1]
        whole = Q == 4 and B == 2 and 2 * B == Z and H % HEAD_DIM == 0 and D % (16 * Q) == 0 and H % (16 * Q) == 0
        if whole and R % 32 == 0 and FL % (256 * Q) == 0:
            return chip_device(Q, Z, *args)
        return general_device(*args)

    return jax.shard_map(
        per_device, mesh=mesh, in_specs=in_specs, out_specs=out_specs, check_vma=False
    )
```

profile of v0, /device:TPU:9, one launch (start us, length us, event | category | flops | bytes accessed | tf_op | source)
XLA Modules:
  0.0 321.3 jit_solution(16345163608392640377)
XLA Ops:
  0.6 1.3 broadcast_in_dim.2.vc
  2.0 185.5 %front.1 = (bf16[512,1024]{1,0:T(8,128)(2,1)}, bf16[1536,1024]{1,0:T(8,128)(2,1)}, bf16[512,512]{1,0:T(8,128)(2,1)}, bf16[1536,512]{1,0:T(8,128)(2,1)}, bf16[153...) custom-call(bf16[2,128,1024]{2,1,0:T(8,128)(2,1)} %comp.1, ...), custom_call_target="tpu_custom_call" | custom-call | tf_op jit(solution)/shard_map/front/pallas_call | solution.py:968
  187.5 117.2 %back.1 = (bf16[1024,768]{1,0:T(8,128)(2,1)}, bf16[256,1024]{1,0:T(8,128)(2,1)}, bf16[1024,1024]{1,0:T(8,128)(2,1)}, bf16[1024,1024]{1,0:T(8,128)(2,1)}, f32[8,1...) custom-call(bf16[512,1024]{1,0:T(8,128)(2,1)} %get-tuple-element.44.tok, ...), custom_call_target="tpu_custom_call" | custom-call | tf_op jit(solution)/shard_map/back/pallas_call | solution.py:1526
  304.7 0.0 copy-start
  304.7 1.6 fusion.1
  306.3 2.1 convert_element_type.15
  308.5 2.1 convert_element_type.17
  310.6 0.0 copy-done
  310.6 0.0 copy-start.2
  310.6 1.7 fusion
  312.3 1.0 copy-done.2
  313.3 0.0 copy-start.1
  313.3 2.5 convert_element_type.18
  315.8 0.0 copy-done.1
  315.8 0.0 copy-start.5
  315.8 0.0 copy-start.6
  315.8 0.0 copy-start.4
  315.8 2.5 convert_element_type.19
  318.3 0.0 copy-done.5
  318.3 0.0 copy-start.3
  318.3 0.8 copy.38
  319.1 0.0 copy-done.6
  319.1 0.6 copy.39
  319.7 0.0 copy-done.4
  319.7 0.8 copy.40
  320.5 0.0 copy-done.3
  320.5 0.8 copy.41
Async XLA Ops:
  304.7 5.9 %copy-start = (bf16[1024,768]{1,0:T(8,128)(2,1)S(1)}, bf16[1024,768]{1,0:T(8,128)(2,1)}, u32[]{:S(2)}) copy-start(bf16[1024,768]{1,0:T(8,128)(2,1)} %get-tuple-element.65) | copy-start | bytes 4718596
  310.6 2.7 copy-start.2
  313.3 2.5 copy-start.1
  315.8 2.5 copy-start.5
  315.8 3.3 %copy-start.6 = (f32[8,1,128]{2,1,0:T(1,128)S(1)}, f32[8,1,128]{2,1,0:T(1,128)}, u32[]{:S(2)}) copy-start(f32[8,1,128]{2,1,0:T(1,128)} %get-tuple-element.68) | copy-start | bytes 12292
  315.8 3.9 %copy-start.4 = (bf16[2,128,1024]{2,1,0:T(8,128)(2,1)S(1)}, bf16[2,128,1024]{2,1,0:T(8,128)(2,1)}, u32[]{:S(2)}) copy-start(bf16[2,128,1024]{2,1,0:T(8,128)(2,1)} %get-tuple-element.110) | copy-start | bytes 1572868
  318.3 2.2 copy-start.3
where the time goes:
time: 322 us; the launch traced here: 321 us
  Pallas kernels  303 us (94%)
  other arithmetic  9.21 us (3%)
  local copies, waits for them, and re-layouts  8.66 us (3%)
    pallas_call x1, Pallas kernels, front(): pl.pallas_call(functools.partial(front_kernel, Q, Z), out_shape=[sds((S,...  185 us
    pallas_call x1, Pallas kernels, back(): pl.pallas_call(functools.partial(back_kernel, Q, Z, B), out_shape=[sds((D...  117 us

commit v1 on v0

--- a/solution.py
+++ b/solution.py
@@ -399,6 +399,94 @@
     return jnp.where(col == row + offset, 1.0, 0.0).astype(BF)
 
 
+class PlaneSum:
+    def __init__(self, al, peer, blk, rows, h, g):
+        self.peer, self.blk, self.half, self.rows, self.h, self.g = peer, blk, rows // 2, rows, h, g
+        self.hs, self.hr, self.gs, self.gr = al.take(2), al.take(2), al.take(2), al.take(2)
+
+    def h_x(self, i):
+        return rcopy(self.blk(3, i * self.half, self.half), self.h.at[i], self.hs(i), self.hr(i), self.peer(i + 1))
+
+    def g_x(self, i):
+        return rcopy(self.blk(i + 1, 0, self.rows), self.g.at[i], self.gs(i), self.gr(i), self.peer(i + 1))
+
+    def start(self):
+        for i in range(2):
+            self.h_x(i).start()
+
+    def middle(self):
+        for i in range(2):
+            self.h_x(i).wait_recv()
+            mine = self.blk(2 - i, i * self.half, self.half)
+            mine[...] = (mine[...].astype(F32) + self.h[i].astype(F32)).astype(BF)
+            self.g_x(1 - i).start()
+
+    def arrive(self):
+        for i in range(2):
+            self.g_x(i).wait_recv()
+
+    def total(self):
+        self.arrive()
+        own = self.blk(0, 0, self.rows)
+        return own[...].astype(F32) + (self.g[0].astype(F32) + self.g[1].astype(F32))
+
+    def drain(self):
+        for i in range(2):
+            self.h_x(i).wait_send()
+            self.g_x(i).wait_send()
+
+
+class PlaneGather:
+    def __init__(self, al, peer, sib, loc, rows, own=None):
+        self.peer, self.sib, self.loc, self.half, self.rows = peer, sib, loc, rows // 2, rows
+        self.own = own
+        self.as_, self.ar, self.hs, self.hr = al.take(2), al.take(2), al.take(2), al.take(2)
+        self.fs, self.fr = al.take(4), al.take(4)
+
+    def a_x(self, i, k=0):
+        src = self.loc(0, 0, self.rows) if self.own is None else self.own
+        return rcopy(src, self.loc(k, 0, self.rows), self.as_(i), self.ar(i), self.peer(i + 1))
+
+    def h_x(self, i, k=None):
+        k = 2 - (1 - i) if k is None else k
+        rows = self.loc(k, i * self.half, self.half)
+        return rcopy(rows, rows, self.hs(i), self.hr(i), self.peer(2 - i))
+
+    def f_x(self, k, other=None):
+        src = self.loc(k, 0, self.rows)
+        if k == 0 and self.own is not None:
+            src = self.own
+        dst = self.loc(k, 0, self.rows) if other is None else other(k, 0, self.rows)
+        return rcopy(src, dst, self.fs(k), self.fr(k), self.sib)
+
+    def start(self):
+        for i in range(2):
+            self.a_x(i).start()
+        self.f_x(0).start()
+
+    def middle(self):
+        for i in range(2):
+            rcopy(self.loc(i + 1, 0, self.rows), self.loc(i + 1, 0, self.rows), self.as_(i), self.ar(i), self.peer(1)).wait_recv()
+            self.h_x(i).start()
+            self.f_x(i + 1).start()
+
+    def last(self):
+        for i in range(2):
+            self.h_x(i, 3).wait_recv()
+        self.f_x(3).start()
+
+    def drain(self):
+        for i in range(2):
+            self.a_x(i).wait_send()
+            self.h_x(i).wait_send()
+        for k in range(4):
+            self.f_x(k).wait_send()
+
+    def arrivals(self, other):
+        for k in range(4):
+            rcopy(other(k, 0, self.rows), other(k, 0, self.rows), self.fs(k), self.fr(k), self.sib).wait_recv()
+
+
 FRONT_SEMS = 400
 
 
@@ -406,7 +494,7 @@
                  tok_o, normed_o, q_o, k_o, v_o, probs_o, mixed_o, wq_o, wk_o, wv_o, wo_o,
                  resid_o, gresid_o, glow_o, gu_o, gd_o, down_o, small_o, nm_o, nc_o,
                  ctx, normed, wqs, wks, wvs, wos, qs, ks, vs, probs, mixed, phalf, got, resid, sec, cots, ups, downs,
-                 ubs, vco, act, gup, gbuf, got1, send2, got2, low, nms, ncs, gus, gds, dns, sems):
+                 ubs, vco, act, gup, gbuf, got1, gh, gg, low, nms, ncs, gus, gds, dns, sems):
     dp, c, q, z = where_am_i(Q, Z)
     sib = dp + 1 - 2 * c
     partners = [(sib, z)]
@@ -502,25 +590,30 @@
     v_s = rcopy(vc, vco, vs_(0), vr_(0), (sib, z))
 
     ts, tr, tl = al.take(B), al.take(B), al.take(1)
-    tps, tpr, tfs, tfr = al.take(Q), al.take(Q), al.take(Q), al.take(Q)
-
-    def slot(ref, k, cc):
-        return ref.at[pl.ds((2 * k + cc) * N, N), :]
+
+    def dev(k, core):
+        return 2 * across(q, k) + core
+
+    def t_rows(d, i):
+        return cots.at[pl.ds(pl.multiple_of(d * N + i * R, R), R), :]
 
     def t_z(s):
-        return rcopy(cot.at[s], cots.at[pl.ds(pl.multiple_of(jz * R, R), R), :], ts(s), tr(jz), (2 * q + z // B, B * c + s))
+        to = 2 * q + z // B
+        return rcopy(cot.at[s], t_rows(to, jz), ts(s), tr(jz), (to, B * c + s))
 
     def t_l():
-        return lcopy(cot.at[jz], cots.at[pl.ds(pl.multiple_of(jz * R, R), R), :], tl(0))
+        return lcopy(cot.at[jz], t_rows(dp, jz), tl(0))
 
     def t_arrive(i):
-        return rcopy(cots.at[pl.ds(i * R, R), :], cots.at[pl.ds(i * R, R), :], ts(0), tr(i), (dp, z))
-
-    def t_p(k):
-        return rcopy(slot(cots, 0, 0), slot(cots, k, 0), tps(k), tpr(k), peer(k))
-
-    def t_f(k):
-        return rcopy(slot(cots, k, 0), slot(cots, k, 1), tfs(k), tfr(k), (sib, z))
+        return rcopy(t_rows(dp, i), t_rows(dp, i), ts(0), tr(i), (dp, z))
+
+    def rows_at(ref, core):
+        def loc(k, lo, n):
+            return ref.at[pl.ds(pl.multiple_of(dev(k, core) * N + lo, n), n), :]
+        return loc
+
+    tgat = PlaneGather(al, peer, (sib, z), rows_at(cots, c), N)
+    agat = PlaneGather(al, peer, (sib, z), rows_at(sec, c), N)
 
     xs, xr_, xl = al.take(2, Z), al.take(2, Z), al.take(2)
 
@@ -606,9 +699,6 @@
         @pl.when(jnp.logical_not(here))
         def _():
             t_z(s).start()
-    for i in range(2):
-        for r in range(1, Z):
-            x_z(i, r).start()
     for r in range(1, Z):
         zs = lax.rem(z + r, Z)
         for t in range(3):
@@ -659,6 +749,8 @@
         return carry
 
     lax.fori_loop(0, S // T, project_q, 0)
+    for r in range(1, Z):
+        x_z(0, r).start()
     leave(qs, q_o)
     leave(ks, k_o)
     leave(vs, v_o)
@@ -701,6 +793,8 @@
     attend(1 - c, 0)
     phalf[...] = nn_dot(mixed[pl.ds(pl.multiple_of((1 - c) * N, N), N), :], wos[...])
     h_x.start()
+    for r in range(1, Z):
+        x_z(1, r).start()
     for i in range(B):
         @pl.when(jnp.logical_not((B * c + i == z) & mine))
         def _():
@@ -709,9 +803,7 @@
         @pl.when((B * c + i == z) & mine)
         def _():
             t_l().wait()
-    for k in range(1, Q):
-        t_p(k).start()
-    t_f(0).start()
+    tgat.start()
     attend(c, 1)
     leave(mixed, mixed_o)
     own_part = nn_dot(mixed[pl.ds(pl.multiple_of(c * N, N), N), :], wos[...])
@@ -719,47 +811,23 @@
     resid[...] = ctx[2, pl.ds(pl.multiple_of(c * N, N), N), :].astype(F32) + (own_part + got[...])
     leave(resid, resid_o)
     xhat2, _ = layer_norm_rows(resid[...])
-    sec[pl.ds(0, N), :] = (xhat2 * g2[...] + b2[...]).astype(BF)
-
-    as_, ar, afs, afr = al.take(Q), al.take(Q), al.take(Q), al.take(Q)
-
-    def a_p(k):
-        return rcopy(slot(sec, 0, 0), slot(sec, k, 0), as_(k), ar(k), peer(k))
-
-    def a_f(k):
-        return rcopy(slot(sec, k, 0), slot(sec, k, 1), afs(k), afr(k), (sib, z))
-
-    for k in range(1, Q):
-        t_p(k).wait_recv()
-        t_f(k).start()
-    for k in range(1, Q - 1):
-        a_p(k).start()
-    a_f(0).start()
+    sec[pl.ds(pl.multiple_of(dp * N, N), N), :] = (xhat2 * g2[...] + b2[...]).astype(BF)
+
+    agat.start()
     sqc = al.take(RATE)
     sqs = [dns.at[pl.ds(0, D), :], dns.at[pl.ds(D, D), :], gbuf.at[pl.ds(D, D), :]]
     sq_x = [lcopy(sq.at[pl.ds(r * D, D), :], sqs[r], sqc(r)) for r in range(RATE)]
     for x in sq_x:
         x.start()
-    for r in range(1, Z):
-        u_z(r).wait()
-        for i in range(2):
-            x_z(i, r).wait_recv()
-    u_l.wait()
-    for x in x_l:
-        x.wait()
     ss, sr = al.take(Q), al.take(Q)
-    gps, gpr = al.take(Q), al.take(Q)
 
     def s_x(k):
-        return rcopy(slot(gbuf, k, 1), got1.at[k], ss(k), sr(k), (sib, z))
-
-    def p_x(k):
-        return rcopy(send2.at[k - 1], got2.at[k - 1], gps(k), gpr(k), peer(k))
-
-    bias_row = jnp.concatenate([ubs[r] for r in range(Z)], axis=1)
+        return rcopy(rows_at(gbuf, 1 - c)(k, 0, N), got1.at[k], ss(k), sr(k), (sib, z))
+
+    gsum = PlaneSum(al, peer, rows_at(gbuf, c), N, gh, gg)
     small_o[...] = jnp.zeros_like(small_o)
 
-    def forward_block(b, carry):
+    def forward_block(b, bias_row):
         at = pl.ds(pl.multiple_of(b * N, N), N)
         x = nn_dot(sec[at, :], ups[...]) + bias_row
         ga = nt_dot(cots[at, :], downs[...])
@@ -772,20 +840,16 @@
         gup[at, :] = gu
         small_o[2:3, pl.ds(0, Z * E)] = small_o[2:3, pl.ds(0, Z * E)] + jnp.sum(gu.astype(F32), axis=0, keepdims=True)
         gbuf[at, :] = nt_dot(gu, ups[...]).astype(BF)
-        return carry
-
-    def feed(k):
-        lax.fori_loop(2 * k, 2 * k + 2, forward_block, 0)
+        return bias_row
+
+    def feed(k, bias_row):
+        lax.fori_loop(dev(k, 0), dev(k, 0) + 2, forward_block, bias_row)
         s_x(k).start()
 
     def combine(k):
         s_x(k).wait_recv()
-        send2[k - 1] = (gbuf[pl.ds(2 * k * N, N), :].astype(F32) + got1[k].astype(F32)).astype(BF)
-        p_x(k).start()
-
-    t_f(0).wait_recv()
-    a_f(0).wait_recv()
-    feed(0)
+        rows = rows_at(gbuf, c)(k, 0, N)
+        rows[...] = (rows[...].astype(F32) + got1[k].astype(F32)).astype(BF)
 
     groups = S // RATE
     squeezed = None
@@ -816,6 +880,19 @@
     def row_l(i, p):
         return lcopy(rows_in[i].at[pl.ds(p * R, R), :], rows_out[i].at[jz], ml(i))
 
+    tgat.middle()
+    agat.middle()
+    tgat.last()
+    agat.last()
+    for r in range(1, Z):
+        u_z(r).wait()
+        for i in range(2):
+            x_z(i, r).wait_recv()
+    u_l.wait()
+    for x in x_l:
+        x.wait()
+    tgat.arrivals(rows_at(cots, 1 - c))
+    agat.arrivals(rows_at(sec, 1 - c))
     for p in range(per):
         here = (c * per + p == z) & mine
 
@@ -829,17 +906,16 @@
             for i in range(2):
                 row_x(i, p).start()
 
-    for k in range(1, Q):
-        a_p(k).wait_recv()
-        if k == Q - 2:
-            a_p(Q - 1).start()
-        a_f(k).start()
-        t_f(k).wait_recv()
-        a_f(k).wait_recv()
-        feed(k)
-        if k > 1:
-            combine(k - 1)
-    combine(Q - 1)
+    bias = jnp.concatenate([ubs[r] for r in range(Z)], axis=1)
+    feed(3, bias)
+    feed(1, bias)
+    combine(3)
+    gsum.start()
+    feed(2, bias)
+    combine(1)
+    feed(0, bias)
+    combine(2)
+    gsum.middle()
 
     def up_grad(i, carry):
         at = pl.ds(pl.multiple_of(i * T, T), T)
@@ -865,23 +941,21 @@
     lax.fori_loop(0, 2 * Q, down_rows, 0)
     leave(dns, down_o)
 
-    s_x(0).wait_recv()
-    for k in range(1, Q):
-        p_x(k).wait_recv()
+    combine(0)
+    gsum.arrive()
     C = 64
 
     def back_rows(i, carry):
         at = pl.ds(pl.multiple_of(i * C, C), C)
-        gs = gbuf[at, :].astype(F32) + got1[0, at, :].astype(F32)
-        for k in range(1, Q):
-            gs = gs + got2[k - 1, at, :].astype(F32)
+        own = pl.ds(pl.multiple_of(dp * N + i * C, C), C)
+        gs = gbuf[own, :].astype(F32) + (gg[0, at, :].astype(F32) + gg[1, at, :].astype(F32))
         xhat, inv = layer_norm_rows(resid[at, :])
         small_o[0:1, :] = small_o[0:1, :] + jnp.sum(gs * xhat, axis=0, keepdims=True)
         small_o[1:2, :] = small_o[1:2, :] + jnp.sum(gs, axis=0, keepdims=True)
         e = gs * g2[...]
         m1 = jnp.mean(e, axis=-1, keepdims=True)
         m2 = jnp.mean(e * xhat, axis=-1, keepdims=True)
-        gr = cots[at, :].astype(F32) + inv * (e - m1 - xhat * m2)
+        gr = cots[own, :].astype(F32) + inv * (e - m1 - xhat * m2)
         got[at, :] = gr
         low[at, :] = gr.astype(BF)
         return carry
@@ -924,13 +998,9 @@
         @pl.when(jnp.logical_not((B * c + s == z) & mine))
         def _():
             t_z(s).wait_send()
-    for k in range(1, Q):
-        t_p(k).wait_send()
-        a_p(k).wait_send()
-        p_x(k).wait_send()
+    for x in (tgat, agat, gsum):
+        x.drain()
     for k in range(Q):
-        t_f(k).wait_send()
-        a_f(k).wait_send()
         s_x(k).wait_send()
     h_x.wait_send()
     for p in range(per):
@@ -980,98 +1050,13 @@
             vm((S, W), BF), vm((3 * S, W), BF), vm((3 * S, W), BF), vm((heads, S, 3 * S), BF), vm((S, W), BF),
             vm((N, D), F32), vm((N, D), F32), vm((N, D), F32), vm((rows, D), BF), vm((rows, D), BF), vm((D, F), BF), vm((F, D), BF),
             vm((Z, 1, F // Z), F32), vm(vc.shape, jnp.int32), vm((rows, F), BF), vm((rows, F), BF), vm((rows, D), BF),
-            vm((Q, N, D), BF), vm((Q - 1, N, D), BF), vm((Q - 1, N, D), BF), vm((N, D), BF),
+            vm((Q, N, D), BF), vm((2, N // 2, D), BF), vm((2, N, D), BF), vm((N, D), BF),
             vm((N, D), BF), vm((N, D), BF), vm((D, F), BF), vm((F, D), BF), vm((rows, D), BF),
             DMA((FRONT_SEMS,)),
         ],
         compiler_params=pltpu.CompilerParams(collective_id=1, has_side_effects=True, vmem_limit_bytes=63 << 20),
         name="front",
     )(comp, mem, tok, cot, wq, wk, wv, wo, up, down, ub, vc, sq, g1, b1, g2, b2)
-
-
-class PlaneSum:
-    def __init__(self, al, peer, blk, rows, h, g):
-        self.peer, self.blk, self.half, self.rows, self.h, self.g = peer, blk, rows // 2, rows, h, g
-        self.hs, self.hr, self.gs, self.gr = al.take(2), al.take(2), al.take(2), al.take(2)
-
-    def h_x(self, i):
-        return rcopy(self.blk(3, i * self.half, self.half), self.h.at[i], self.hs(i), self.hr(i), self.peer(i + 1))
-
-    def g_x(self, i):
-        return rcopy(self.blk(i + 1, 0, self.rows), self.g.at[i], self.gs(i), self.gr(i), self.peer(i + 1))
-
-    def start(self):
-        for i in range(2):
-            self.h_x(i).start()
-
-    def middle(self):
-        for i in range(2):
-            self.h_x(i).wait_recv()
-            mine = self.blk(2 - i, i * self.half, self.half)
-            mine[...] = (mine[...].astype(F32) + self.h[i].astype(F32)).astype(BF)
-            self.g_x(1 - i).start()
-
-    def total(self):
-        for i in range(2):
-            self.g_x(i).wait_recv()
-        own = self.blk(0, 0, self.rows)
-        return own[...].astype(F32) + (self.g[0].astype(F32) + self.g[1].astype(F32))
-
-    def drain(self):
-        for i in range(2):
-            self.h_x(i).wait_send()
-            self.g_x(i).wait_send()
-
-
-class PlaneGather:
-    def __init__(self, al, peer, sib, loc, rows, own=None):
-        self.peer, self.sib, self.loc, self.half, self.rows = peer, sib, loc, rows // 2, rows
-        self.own = own
-        self.as_, self.ar, self.hs, self.hr = al.take(2), al.take(2), al.take(2), al.take(2)
-        self.fs, self.fr = al.take(4), al.take(4)
-
-    def a_x(self, i, k=0):
-        src = self.loc(0, 0, self.rows) if self.own is None else self.own
-        return rcopy(src, self.loc(k, 0, self.rows), self.as_(i), self.ar(i), self.peer(i + 1))
-
-    def h_x(self, i, k=None):
-        k = 2 - (1 - i) if k is None else k
-        rows = self.loc(k, i * self.half, self.half)
-        return rcopy(rows, rows, self.hs(i), self.hr(i), self.peer(2 - i))
-
-    def f_x(self, k, other=None):
-        src = self.loc(k, 0, self.rows)
-        if k == 0 and self.own is not None:
-            src = self.own
-        dst = self.loc(k, 0, self.rows) if other is None else other(k, 0, self.rows)
-        return rcopy(src, dst, self.fs(k), self.fr(k), self.sib)
-
-    def start(self):
-        for i in range(2):
-            self.a_x(i).start()
-        self.f_x(0).start()
-
-    def middle(self):
-        for i in range(2):
-            rcopy(self.loc(i + 1, 0, self.rows), self.loc(i + 1, 0, self.rows), self.as_(i), self.ar(i), self.peer(1)).wait_recv()
-            self.h_x(i).start()
-            self.f_x(i + 1).start()
-
-    def last(self):
-        for i in range(2):
-            self.h_x(i, 3).wait_recv()
-        self.f_x(3).start()
-
-    def drain(self):
-        for i in range(2):
-            self.a_x(i).wait_send()
-            self.h_x(i).wait_send()
-        for k in range(4):
-            self.f_x(k).wait_send()
-
-    def arrivals(self, other):
-        for k in range(4):
-            rcopy(other(k, 0, self.rows), other(k, 0, self.rows), self.fs(k), self.fr(k), self.sib).wait_recv()
 
 
 BACK_SEMS = 300
@@ -1109,6 +1094,9 @@
     jz = lax.rem(z, B)
     al = Slots(sems)
 
+    def dev(k, core):
+        return 2 * across(q, k) + core
+
     def up_to_z(r):
         return (dp, lax.rem(z + Z - r, Z))
 
@@ -1124,20 +1112,20 @@
     ss, sr = al.take(Q), al.take(Q)
 
     def d_x(k):
-        return rcopy(down_i.at[pl.ds((2 * k + 1) * N, N), :], dgot.at[k], ss(k), sr(k), sib)
+        return rcopy(down_i.at[pl.ds(pl.multiple_of(dev(k, 1 - c) * N, N), N), :], dgot.at[k], ss(k), sr(k), sib)
 
     ld = al.take(30)
     pairs = [(wo_i, wos), (glow_i, glow), (mixed_i, mixed), (probs_i, probs), (v_i, vs), (k_i, ks), (q_i, qs),
              (normed_i, normed), (wq_i, wqs), (wk_i, wks), (wv_i, wvs), (gresid_i, gresid), (resid_i, resid),
              (tok.at[pl.ds(pl.multiple_of(c * N, N), N), :], toks), (cot, cots),
              (gu.at[:, pl.ds(0, E)], xu.at[0]), (gd.at[pl.ds(0, E), :], xd.at[0])]
-    pairs += [(down_i.at[pl.ds(2 * k * N, N), :], dnb.at[k]) for k in range(Q)]
+    pairs += [(down_i.at[pl.ds(pl.multiple_of(dev(k, c) * N, N), N), :], dnb.at[k]) for k in range(Q)]
     loads = [lcopy(src, dst, ld(i)) for i, (src, dst) in enumerate(pairs)]
-    for x in loads[:3]:
+    for x in loads[:3] + loads[17:]:
         x.start()
     for k in (3, 1, 2, 0):
         d_x(k).start()
-    for x in loads[3:]:
+    for x in loads[3:17]:
         x.start()
     for r in range(1, Z):
         for i in range(3):
@@ -1172,6 +1160,13 @@
     dsum = PlaneSum(al, peer, lambda k, lo, n: dnb.at[k, pl.ds(lo, n), :], N, dh, dg)
     for x in osum:
         x.start()
+    for x in loads[17:]:
+        x.wait()
+    for k in (3, 1, 2, 0):
+        d_x(k).wait_recv()
+        dnb[k] = (dnb[k].astype(F32) + dgot[k].astype(F32)).astype(BF)
+        if k == 3:
+            dsum.start()
     sums[...] = jnp.zeros_like(sums)
     arow[...] = jnp.zeros_like(arow)
     scale = HEAD_DIM ** (-0.5)
@@ -1220,13 +1215,6 @@
         x.wait()
     for h in range(hj):
         head(h, h)
-    for x in osum:
-        x.middle()
-    for x in loads[17:]:
-        x.wait()
-    for k in (3, 1, 2, 0):
-        d_x(k).wait_recv()
-        dnb[k] = (dnb[k].astype(F32) + dgot[k].astype(F32)).astype(BF)
     for x in loads[7:11]:
         x.wait()
     H2 = pl.ds(2 * S, S)
@@ -1238,15 +1226,16 @@
         return (nt_dot(gkv[krows, pl.ds(0, H)], wks[:, js]) + nt_dot(gkv[krows, pl.ds(H, H)], wvs[:, js])
                 + nt_dot(gqs[rows, js], wqs[:, js]))
 
+    for x in osum:
+        x.middle()
     weights(0)
+    dsum.middle()
     ghalf[...] = token_rows(0, 1 - c)
     srow[...] = token_rows(0, c)
-    dsum.start()
     for h in range(hj, 2 * hj):
         head(h, h - hj)
     wsum[0].middle()
     weights(1)
-    dsum.middle()
     ghalf[...] = ghalf[...] + token_rows(1, 1 - c)
     ts_, tr_ = al.take(1), al.take(1)
     t_x = rcopy(ghalf, ggot, ts_(0), tr_(0), sib)
@@ -1334,9 +1323,6 @@
     fus[...] = fu.astype(BF)
     fds[...] = fd.astype(BF)
     fbs[...] = fb
-
-    def dev(k, core):
-        return 2 * across(q, k) + core
 
     def u_loc(core):
         def loc(k, lo, n):

time: 322 us -> 303 us (0.941)
  Pallas kernels: 303 us -> 284 us
    pallas_call x1, Pallas kernels: 185 us -> 153 us  [front(): pl.pallas_call(functools.partial(front_kernel, Q, Z), out_shape=[sds((S,...]
    pallas_call x1, Pallas kernels: 117 us -> 131 us  [back(): pl.pallas_call(functools.partial(back_kernel, Q, Z, B), out_shape=[sds((D...]
where the time goes in v1:
time: 303 us; the launch traced here: 302 us
  Pallas kernels  284 us (94%)
  other arithmetic  9.21 us (3%)
  local copies, waits for them, and re-layouts  8.66 us (3%)
    pallas_call x1, Pallas kernels, front(): pl.pallas_call(functools.partial(front_kernel, Q, Z), out_shape=[sds((S,...  153 us
    pallas_call x1, Pallas kernels, back(): pl.pallas_call(functools.partial(back_kernel, Q, Z, B), out_shape=[sds((D...  131 us

profile of v1, /device:TPU:9, one launch (start us, length us, event | category | flops | bytes accessed | tf_op | source)
XLA Modules:
  0.0 302.4 jit_solution(15825728713188712152)
XLA Ops:
  0.6 1.3 broadcast_in_dim.2.vc
  2.0 153.2 %front.1 = (bf16[512,1024]{1,0:T(8,128)(2,1)}, bf16[1536,1024]{1,0:T(8,128)(2,1)}, bf16[512,512]{1,0:T(8,128)(2,1)}, bf16[1536,512]{1,0:T(8,128)(2,1)}, bf16[153...) custom-call(bf16[2,128,1024]{2,1,0:T(8,128)(2,1)} %comp.1, ...), custom_call_target="tpu_custom_call" | custom-call | tf_op jit(solution)/shard_map/front/pallas_call | solution.py:1038
  155.2 130.6 %back.1 = (bf16[1024,768]{1,0:T(8,128)(2,1)}, bf16[256,1024]{1,0:T(8,128)(2,1)}, bf16[1024,1024]{1,0:T(8,128)(2,1)}, bf16[1024,1024]{1,0:T(8,128)(2,1)}, f32[8,1...) custom-call(bf16[512,1024]{1,0:T(8,128)(2,1)} %get-tuple-element.44.tok, ...), custom_call_target="tpu_custom_call" | custom-call | tf_op jit(solution)/shard_map/back/pallas_call | solution.py:1512
  285.8 0.0 copy-start
  285.8 1.6 fusion.1
  287.4 2.1 convert_element_type.15
  289.5 2.1 convert_element_type.17
  291.7 0.0 copy-done
  291.7 0.0 copy-start.2
  291.7 1.7 fusion
  293.4 1.0 copy-done.2
  294.4 0.0 copy-start.1
  294.4 2.5 convert_element_type.18
  296.9 0.0 copy-done.1
  296.9 0.0 copy-start.5
  296.9 0.0 copy-start.6
  296.9 0.0 copy-start.4
  296.9 2.5 convert_element_type.19
  299.4 0.0 copy-done.5
  299.4 0.0 copy-start.3
  299.4 0.8 copy.38
  300.2 0.0 copy-done.6
  300.2 0.6 copy.39
  300.8 0.0 copy-done.4
  300.8 0.8 copy.40
  301.6 0.0 copy-done.3
  301.6 0.8 copy.41
Async XLA Ops:
  285.8 5.9 %copy-start = (bf16[1024,768]{1,0:T(8,128)(2,1)S(1)}, bf16[1024,768]{1,0:T(8,128)(2,1)}, u32[]{:S(2)}) copy-start(bf16[1024,768]{1,0:T(8,128)(2,1)} %get-tuple-element.65) | copy-start | bytes 4718596
  291.7 2.7 copy-start.2
  294.4 2.5 copy-start.1
  296.9 2.5 copy-start.5
  296.9 3.3 %copy-start.6 = (f32[8,1,128]{2,1,0:T(1,128)S(1)}, f32[8,1,128]{2,1,0:T(1,128)}, u32[]{:S(2)}) copy-start(f32[8,1,128]{2,1,0:T(1,128)} %get-tuple-element.68) | copy-start | bytes 12292
  296.9 3.9 %copy-start.4 = (bf16[2,128,1024]{2,1,0:T(8,128)(2,1)S(1)}, bf16[2,128,1024]{2,1,0:T(8,128)(2,1)}, u32[]{:S(2)}) copy-start(bf16[2,128,1024]{2,1,0:T(8,128)(2,1)} %get-tuple-element.110) | copy-start | bytes 1572868
  299.4 2.2 copy-start.3

commit v2 on v1

--- a/solution.py
+++ b/solution.py
@@ -399,16 +399,25 @@
     return jnp.where(col == row + offset, 1.0, 0.0).astype(BF)
 
 
+def stack(ref, offset, rows, width=None):
+    width = ref.shape[-1] if width is None else width
+
+    def view(i):
+        return ref.at[pl.ds(pl.multiple_of(offset + i * rows, rows), rows), pl.ds(0, width)]
+
+    return view
+
+
 class PlaneSum:
     def __init__(self, al, peer, blk, rows, h, g):
         self.peer, self.blk, self.half, self.rows, self.h, self.g = peer, blk, rows // 2, rows, h, g
         self.hs, self.hr, self.gs, self.gr = al.take(2), al.take(2), al.take(2), al.take(2)
 
     def h_x(self, i):
-        return rcopy(self.blk(3, i * self.half, self.half), self.h.at[i], self.hs(i), self.hr(i), self.peer(i + 1))
+        return rcopy(self.blk(3, i * self.half, self.half), self.h(i), self.hs(i), self.hr(i), self.peer(i + 1))
 
     def g_x(self, i):
-        return rcopy(self.blk(i + 1, 0, self.rows), self.g.at[i], self.gs(i), self.gr(i), self.peer(i + 1))
+        return rcopy(self.blk(i + 1, 0, self.rows), self.g(i), self.gs(i), self.gr(i), self.peer(i + 1))
 
     def start(self):
         for i in range(2):
@@ -418,7 +427,7 @@
         for i in range(2):
             self.h_x(i).wait_recv()
             mine = self.blk(2 - i, i * self.half, self.half)
-            mine[...] = (mine[...].astype(F32) + self.h[i].astype(F32)).astype(BF)
+            mine[...] = (mine[...].astype(F32) + self.h(i)[...].astype(F32)).astype(BF)
             self.g_x(1 - i).start()
 
     def arrive(self):
@@ -428,7 +437,7 @@
     def total(self):
         self.arrive()
         own = self.blk(0, 0, self.rows)
-        return own[...].astype(F32) + (self.g[0].astype(F32) + self.g[1].astype(F32))
+        return own[...].astype(F32) + (self.g(0)[...].astype(F32) + self.g(1)[...].astype(F32))
 
     def drain(self):
         for i in range(2):
@@ -487,19 +496,20 @@
             rcopy(other(k, 0, self.rows), other(k, 0, self.rows), self.fs(k), self.fr(k), self.sib).wait_recv()
 
 
-FRONT_SEMS = 400
-
-
-def front_kernel(Q, Z, comp, mem, tok, cot, wq, wk, wv, wo, up, down, ub, vc, sq, g1, b1, g2, b2,
-                 tok_o, normed_o, q_o, k_o, v_o, probs_o, mixed_o, wq_o, wk_o, wv_o, wo_o,
-                 resid_o, gresid_o, glow_o, gu_o, gd_o, down_o, small_o, nm_o, nc_o,
+LAYER_SEMS = 600
+
+
+def layer_kernel(Q, Z, comp, mem, tok, cot, wq, wk, wv, wo, up, down, ub, vc, sq, g1, b1, g2, b2, db,
+                 aw, ago, afu, afd, aub, small_o, out_o, tg_o, nm_o, nc_o,
                  ctx, normed, wqs, wks, wvs, wos, qs, ks, vs, probs, mixed, phalf, got, resid, sec, cots, ups, downs,
-                 ubs, vco, act, gup, gbuf, got1, gh, gg, low, nms, ncs, gus, gds, dns, sems):
+                 ubs, vco, act, gup, gbuf, got1, gh, gg, glow, nms, ncs, gus, gds, dgot, dh, dg, ggot, srow,
+                 xu, xd, xb, fbs, arow, ffs, sums, sgot, pgot, zgot, sems, ready):
     dp, c, q, z = where_am_i(Q, Z)
-    sib = dp + 1 - 2 * c
-    partners = [(sib, z)]
+    sd = dp + 1 - 2 * c
+    sib = (sd, z)
+    partners = [sib]
     for r in range(1, Z):
-        for d in (dp, sib):
+        for d in (dp, sd):
             partners.append((d, lax.rem(z + r, Z)))
     for k in range(1, Q):
         partners.append((2 * across(q, k) + c, z))
@@ -569,7 +579,7 @@
         return lcopy(acts[t].at[jz], c_rows(t, z), cl(t))
 
     def c_sib(t):
-        return rcopy(acts[t].at[jz], c_rows(t, z), fs(t, z), fr(t, z), (sib, z))
+        return rcopy(acts[t].at[jz], c_rows(t, z), fs(t, z), fr(t, z), sib)
 
     def c_z(t, s, h):
         return rcopy(acts[t].at[s, pl.ds(HR * h, HR), :], c_half(t, z, h), cs(t, s, h), cr(t, z), (2 * q + h, B * c + s))
@@ -578,7 +588,7 @@
         return rcopy(c_half(t, zs, c), c_half(t, zs, c), cs(t, 0, 0), cr(t, zs), (dp, z))
 
     def c_fwd(t, zs, half):
-        return rcopy(c_half(t, zs, half), c_half(t, zs, half), fs(t, zs), fr(t, zs), (sib, z))
+        return rcopy(c_half(t, zs, half), c_half(t, zs, half), fs(t, zs), fr(t, zs), sib)
 
     us, ur, ul = al.take(Z - 1), al.take(Z - 1), al.take(1)
     vs_, vr_ = al.take(1), al.take(1)
@@ -587,7 +597,7 @@
         return rcopy(ub.at[dp], ubs.at[r], us(r - 1), ur(r - 1), (dp, lax.rem(z + r, Z)))
 
     u_l = lcopy(ub.at[dp], ubs.at[0], ul(0))
-    v_s = rcopy(vc, vco, vs_(0), vr_(0), (sib, z))
+    v_s = rcopy(vc, vco, vs_(0), vr_(0), sib)
 
     ts, tr, tl = al.take(B), al.take(B), al.take(1)
 
@@ -612,21 +622,74 @@
             return ref.at[pl.ds(pl.multiple_of(dev(k, core) * N + lo, n), n), :]
         return loc
 
-    tgat = PlaneGather(al, peer, (sib, z), rows_at(cots, c), N)
-    agat = PlaneGather(al, peer, (sib, z), rows_at(sec, c), N)
-
-    xs, xr_, xl = al.take(2, Z), al.take(2, Z), al.take(2)
+    tgat = PlaneGather(al, peer, sib, rows_at(cots, c), N)
+    agat = PlaneGather(al, peer, sib, rows_at(sec, c), N)
+
+    xs, xr_, xl, xf = al.take(2, Z), al.take(2, Z), al.take(2), al.take(2, 2)
+    is_end = lax.rem(z, Z - 1) == 0
+
+    def x_place(i, r):
+        if i == 0:
+            return ups.at[:, pl.ds(r * E, E)]
+        return downs.at[pl.ds(r * E, E), :]
 
     def x_z(i, r):
-        if i == 0:
-            return rcopy(up.at[:, pl.ds(pl.multiple_of(dp * E, E), E)], ups.at[:, pl.ds(r * E, E)], xs(0, r), xr_(0, r),
-                         (dp, lax.rem(z + r, Z)))
-        return rcopy(down.at[pl.ds(pl.multiple_of(dp * E, E), E), :], downs.at[pl.ds(r * E, E), :], xs(1, r), xr_(1, r),
-                     (dp, lax.rem(z + r, Z)))
+        src = up.at[:, pl.ds(pl.multiple_of(dp * E, E), E)] if i == 0 else down.at[pl.ds(pl.multiple_of(dp * E, E), E), :]
+        return rcopy(src, x_place(i, r), xs(i, r), xr_(i, r), (dp, lax.rem(z + r, Z)))
+
+    def x_direct(r):
+        return (z < Z - 1, is_end, z > 0)[r - 1]
+
+    def x_start(i):
+        for r in range(1, Z):
+            @pl.when(x_direct(r))
+            def _():
+                x_z(i, r).start()
+
+    onward = ((2, 3, ((2, 3), (1, 2)), 3), (1, 0, ((2, 1), (3, 2)), 1))
+
+    def x_onward(i, n, to, a, b):
+        return rcopy(x_place(i, a), x_place(i, b), xf(i, n), xr_(i, b), (dp, to))
+
+    def x_forward(i):
+        for at, to, pairs, rest in onward:
+            @pl.when(z == at)
+            def _():
+                for n, (a, b) in enumerate(pairs):
+                    x_z(i, a).wait_recv()
+                    x_onward(i, n, to, a, b).start()
+
+    def x_rest(i):
+        for at, to, pairs, rest in onward:
+            @pl.when(z == at)
+            def _():
+                x_z(i, rest).wait_recv()
+
+        @pl.when(is_end)
+        def _():
+            for r in range(1, Z):
+                x_z(i, r).wait_recv()
+
+    def x_drain(i):
+        for r in range(1, Z):
+            @pl.when(x_direct(r))
+            def _():
+                x_z(i, r).wait_send()
+        for at, to, pairs, rest in onward:
+            @pl.when(z == at)
+            def _():
+                for n, (a, b) in enumerate(pairs):
+                    x_onward(i, n, to, a, b).wait_send()
 
     x_l = [lcopy(up.at[:, pl.ds(pl.multiple_of(dp * E, E), E)], ups.at[:, pl.ds(0, E)], xl(0)),
            lcopy(down.at[pl.ds(pl.multiple_of(dp * E, E), E), :], downs.at[pl.ds(0, E), :], xl(1))]
 
+    c_sem = al.take(B)
+    c_in = [lcopy(cot.at[i], nms.at[pl.ds(i * R, R), :], c_sem(i)) for i in range(B)]
+
+    for x in c_in:
+        x.start()
+    sums[...] = jnp.zeros_like(sums)
     @pl.when(mine)
     def _():
         for a in range(4):
@@ -671,13 +734,16 @@
     @pl.when(jnp.logical_not(mine))
     def _():
         for t in range(3):
-            rcopy(c_rows(t, z), c_rows(t, z), fs(t, z), fr(t, z), (sib, z)).wait_recv()
+            rcopy(c_rows(t, z), c_rows(t, z), fs(t, z), fr(t, z), sib).wait_recv()
 
     def norm_own(t, carry):
         norm_block(t, z)
         return carry
 
     lax.fori_loop(0, 3, norm_own, 0)
+    for x in c_in:
+        x.wait()
+    sums[4:5, :] = jnp.sum(nms[...].astype(F32), axis=0, keepdims=True)
     for r in range(1, Z):
         zs = lax.rem(z + r, Z)
         for t in range(3):
@@ -709,16 +775,6 @@
             return carry
 
         lax.fori_loop(0, 3, norm_one, 0)
-    outs = al.take(16)
-    copies = []
-
-    def leave(src, dst):
-        cp = lcopy(src, dst, outs(len(copies)))
-        cp.start()
-        copies.append(cp)
-
-    leave(normed, normed_o)
-    leave(ctx.at[2], tok_o)
     for j in range(B):
         @pl.when(B * c + j != z)
         def _():
@@ -730,8 +786,6 @@
     def _():
         for a in range(4):
             w_l(a).wait()
-    for a in range(4):
-        leave(wss[a], (wq_o, wk_o, wv_o, wo_o)[a])
 
     T = 256
 
@@ -749,18 +803,13 @@
         return carry
 
     lax.fori_loop(0, S // T, project_q, 0)
-    for r in range(1, Z):
-        x_z(0, r).start()
-    leave(qs, q_o)
-    leave(ks, k_o)
-    leave(vs, v_o)
+    x_start(0)
 
     v_s.wait()
     counts = jnp.where(mine, vc[jz], vco[jz])
     count = counts[0:1, 0:1]
     scale = HEAD_DIM ** (-0.5)
     P2 = 2 * S
-    pouts = al.take(2, heads)
 
     def attend(half, tag):
         r0 = pl.multiple_of(half * N, N)
@@ -781,7 +830,6 @@
             p2 = (p2 * inv).astype(BF)
             probs[h, pl.ds(r0, N), pl.ds(0, P2)] = p1
             probs[h, pl.ds(r0, N), pl.ds(P2, S)] = p2
-            lcopy(probs.at[h, pl.ds(r0, N), :], probs_o.at[h, pl.ds(r0, N), :], pouts(tag, h)).start()
             mix = nn_dot(p1, vs[pl.ds(0, P2), hd]) + nn_dot(p2, vs[pl.ds(P2, S), hd])
             mixed[pl.ds(r0, N), hd] = mix.astype(BF)
             return carry
@@ -789,12 +837,11 @@
         lax.fori_loop(0, heads, head, 0)
 
     hs, hr = al.take(1), al.take(1)
-    h_x = rcopy(phalf, got, hs(0), hr(0), (sib, z))
+    h_x = rcopy(phalf, got, hs(0), hr(0), sib)
     attend(1 - c, 0)
     phalf[...] = nn_dot(mixed[pl.ds(pl.multiple_of((1 - c) * N, N), N), :], wos[...])
     h_x.start()
-    for r in range(1, Z):
-        x_z(1, r).start()
+    x_start(1)
     for i in range(B):
         @pl.when(jnp.logical_not((B * c + i == z) & mine))
         def _():
@@ -805,27 +852,25 @@
             t_l().wait()
     tgat.start()
     attend(c, 1)
-    leave(mixed, mixed_o)
     own_part = nn_dot(mixed[pl.ds(pl.multiple_of(c * N, N), N), :], wos[...])
     h_x.wait_recv()
     resid[...] = ctx[2, pl.ds(pl.multiple_of(c * N, N), N), :].astype(F32) + (own_part + got[...])
-    leave(resid, resid_o)
     xhat2, _ = layer_norm_rows(resid[...])
     sec[pl.ds(pl.multiple_of(dp * N, N), N), :] = (xhat2 * g2[...] + b2[...]).astype(BF)
 
     agat.start()
     sqc = al.take(RATE)
-    sqs = [dns.at[pl.ds(0, D), :], dns.at[pl.ds(D, D), :], gbuf.at[pl.ds(D, D), :]]
+    sqs = [gbuf.at[pl.ds(0, D), :], gbuf.at[pl.ds(D, D), :], dgot]
     sq_x = [lcopy(sq.at[pl.ds(r * D, D), :], sqs[r], sqc(r)) for r in range(RATE)]
     for x in sq_x:
         x.start()
     ss, sr = al.take(Q), al.take(Q)
 
     def s_x(k):
-        return rcopy(rows_at(gbuf, 1 - c)(k, 0, N), got1.at[k], ss(k), sr(k), (sib, z))
-
-    gsum = PlaneSum(al, peer, rows_at(gbuf, c), N, gh, gg)
-    small_o[...] = jnp.zeros_like(small_o)
+        return rcopy(rows_at(gbuf, 1 - c)(k, 0, N), stack(got1, 0, N)(k), ss(k), sr(k), sib)
+
+    gsum = PlaneSum(al, peer, rows_at(gbuf, c), N, stack(gh, 0, N // 2), stack(gg, 0, N))
+    ffs[...] = jnp.zeros_like(ffs)
 
     def forward_block(b, bias_row):
         at = pl.ds(pl.multiple_of(b * N, N), N)
@@ -838,7 +883,7 @@
         slope = 0.5 * (1.0 + th) + 0.5 * x * (1.0 - th * th) * (root * (1.0 + 0.134145 * x2))
         gu = (ga * slope).astype(BF)
         gup[at, :] = gu
-        small_o[2:3, pl.ds(0, Z * E)] = small_o[2:3, pl.ds(0, Z * E)] + jnp.sum(gu.astype(F32), axis=0, keepdims=True)
+        ffs[2:3, pl.ds(0, Z * E)] = ffs[2:3, pl.ds(0, Z * E)] + jnp.sum(gu.astype(F32), axis=0, keepdims=True)
         gbuf[at, :] = nt_dot(gu, ups[...]).astype(BF)
         return bias_row
 
@@ -849,7 +894,7 @@
     def combine(k):
         s_x(k).wait_recv()
         rows = rows_at(gbuf, c)(k, 0, N)
-        rows[...] = (rows[...].astype(F32) + got1[k].astype(F32)).astype(BF)
+        rows[...] = (rows[...].astype(F32) + stack(got1, 0, N)(k)[...].astype(F32)).astype(BF)
 
     groups = S // RATE
     squeezed = None
@@ -871,23 +916,25 @@
     ncs[pl.ds(0, N), :] = new_comp.astype(BF)
     per = N // R
     ms, mr, ml = al.take(2, 2), al.take(2, B), al.take(2)
-    rows_in = [nms, ncs]
-    rows_out = [nm_o, nc_o]
-
-    def row_x(i, p):
-        return rcopy(rows_in[i].at[pl.ds(p * R, R), :], rows_out[i].at[jz], ms(i, p), mr(i, jz), (2 * q + z // B, c * per + p))
-
-    def row_l(i, p):
-        return lcopy(rows_in[i].at[pl.ds(p * R, R), :], rows_out[i].at[jz], ml(i))
-
+    kept_in = [nms, ncs]
+    kept_out = [nm_o, nc_o]
+
+    def keep_x(i, p):
+        return rcopy(kept_in[i].at[pl.ds(p * R, R), :], kept_out[i].at[jz], ms(i, p), mr(i, jz), (2 * q + z // B, c * per + p))
+
+    def keep_l(i, p):
+        return lcopy(kept_in[i].at[pl.ds(p * R, R), :], kept_out[i].at[jz], ml(i))
+
+    x_forward(0)
     tgat.middle()
     agat.middle()
     tgat.last()
+    x_forward(1)
     agat.last()
     for r in range(1, Z):
         u_z(r).wait()
-        for i in range(2):
-            x_z(i, r).wait_recv()
+    for i in range(2):
+        x_rest(i)
     u_l.wait()
     for x in x_l:
         x.wait()
@@ -899,12 +946,12 @@
         @pl.when(here)
         def _():
             for i in range(2):
-                row_l(i, p).start()
+                keep_l(i, p).start()
 
         @pl.when(jnp.logical_not(here))
         def _():
             for i in range(2):
-                row_x(i, p).start()
+                keep_x(i, p).start()
 
     bias = jnp.concatenate([ubs[r] for r in range(Z)], axis=1)
     feed(3, bias)
@@ -923,7 +970,85 @@
         return carry
 
     lax.fori_loop(0, D // T, up_grad, 0)
-    leave(gus, gu_o)
+    ys, yr = al.take(2, 6), al.take(2, 4)
+    near_r, near_z = 3 - 2 * lax.rem(z, 2), z + 1 - 2 * lax.rem(z, 2)
+
+    def y_own(i, r):
+        if i == 0:
+            return gus.at[:, pl.ds(pl.multiple_of(r * E, E), E)]
+        return gds.at[pl.ds(pl.multiple_of(r * E, E), E), :]
+
+    def y_buf(i, n):
+        return (xu, xd)[i].at[n]
+
+    def y_near(i):
+        return rcopy(y_own(i, near_r), y_buf(i, 0), ys(i, 0), yr(i, 0), (dp, near_z))
+
+    def y_hand(i, n):
+        r = 2 if n == 0 else 1 + 2 * (z // 3)
+        return rcopy(y_own(i, r), y_buf(i, 2 + n), ys(i, 2 + n), yr(i, 2 + n), (dp, 1 + z // 3))
+
+    def y_far(i, n):
+        r = 5 - 2 * z if n == 0 else 2
+        return rcopy(y_own(i, r), y_buf(i, 1), ys(i, 4 + n), yr(i, 1), (dp, lax.rem(z + Z - r, Z)))
+
+    def y_start(i):
+        @pl.when(is_end)
+        def _():
+            for n in range(2):
+                y_hand(i, n).start()
+        y_near(i).start()
+
+    def y_middle(i):
+        @pl.when(jnp.logical_not(is_end))
+        def _():
+            for n in range(2):
+                rcopy(y_buf(i, 2 + n), y_buf(i, 2 + n), ys(i, 2 + n), yr(i, 2 + n), (dp, z)).wait_recv()
+                mine_ = y_own(i, 5 - 2 * z if n == 0 else 2)
+                mine_[...] = (mine_[...].astype(F32) + y_buf(i, 2 + n)[...].astype(F32)).astype(BF)
+                y_far(i, n).start()
+
+    def y_arrive(i):
+        for n in range(2):
+            rcopy(y_buf(i, n), y_buf(i, n), ys(i, 0), yr(i, n), (dp, z)).wait_recv()
+
+    def y_drain(i):
+        y_near(i).wait_send()
+
+        @pl.when(is_end)
+        def _():
+            for n in range(2):
+                y_hand(i, n).wait_send()
+
+        @pl.when(jnp.logical_not(is_end))
+        def _():
+            for n in range(2):
+                y_far(i, n).wait_send()
+
+    ubs_, ubr = al.take(Z), al.take(Z)
+
+    def ub_x(r):
+        return rcopy(ffs.at[pl.ds(2, 1), pl.ds(r * E, E)], xb.at[r], ubs_(r), ubr(r), (dp, lax.rem(z + Z - r, Z)))
+
+    y_start(0)
+    for r in range(1, Z):
+        ub_x(r).start()
+    agat.drain()
+
+    def down_rows(b, carry):
+        at = pl.ds(pl.multiple_of(b * N, N), N)
+        sec[at, :] = nn_dot(act[at, :], downs[...]).astype(BF)
+        return carry
+
+    lax.fori_loop(0, 2 * Q, down_rows, 0)
+    dss, dsr = al.take(Q), al.take(Q)
+
+    def d_x(k):
+        return rcopy(rows_at(sec, 1 - c)(k, 0, N), stack(dgot, 0, N)(k), dss(k), dsr(k), sib)
+
+    dsum = PlaneSum(al, peer, rows_at(sec, c), N, stack(dh, 0, N // 2), stack(dg, 0, N))
+    for k in (3, 1, 2, 0):
+        d_x(k).start()
 
     def down_grad(i, carry):
         at = pl.ds(pl.multiple_of(i * T, T), T)
@@ -931,15 +1056,14 @@
         return carry
 
     lax.fori_loop(0, Z * E // T, down_grad, 0)
-    leave(gds, gd_o)
-
-    def down_rows(b, carry):
-        at = pl.ds(pl.multiple_of(b * N, N), N)
-        dns[at, :] = nn_dot(act[at, :], downs[...]).astype(BF)
-        return carry
-
-    lax.fori_loop(0, 2 * Q, down_rows, 0)
-    leave(dns, down_o)
+
+    y_start(1)
+    for k in (3, 1, 2, 0):
+        d_x(k).wait_recv()
+        rows = rows_at(sec, c)(k, 0, N)
+        rows[...] = (rows[...].astype(F32) + stack(dgot, 0, N)(k)[...].astype(F32)).astype(BF)
+        if k == 3:
+            dsum.start()
 
     combine(0)
     gsum.arrive()
@@ -948,192 +1072,56 @@
     def back_rows(i, carry):
         at = pl.ds(pl.multiple_of(i * C, C), C)
         own = pl.ds(pl.multiple_of(dp * N + i * C, C), C)
-        gs = gbuf[own, :].astype(F32) + (gg[0, at, :].astype(F32) + gg[1, at, :].astype(F32))
+        gs = gbuf[own, :].astype(F32) + (gg[at, :].astype(F32) + gg[pl.ds(pl.multiple_of(N + i * C, C), C), :].astype(F32))
         xhat, inv = layer_norm_rows(resid[at, :])
-        small_o[0:1, :] = small_o[0:1, :] + jnp.sum(gs * xhat, axis=0, keepdims=True)
-        small_o[1:2, :] = small_o[1:2, :] + jnp.sum(gs, axis=0, keepdims=True)
+        ffs[0:1, :] = ffs[0:1, :] + jnp.sum(gs * xhat, axis=0, keepdims=True)
+        ffs[1:2, :] = ffs[1:2, :] + jnp.sum(gs, axis=0, keepdims=True)
         e = gs * g2[...]
         m1 = jnp.mean(e, axis=-1, keepdims=True)
         m2 = jnp.mean(e * xhat, axis=-1, keepdims=True)
         gr = cots[own, :].astype(F32) + inv * (e - m1 - xhat * m2)
         got[at, :] = gr
-        low[at, :] = gr.astype(BF)
+        glow[pl.ds(pl.multiple_of(c * N + i * C, C), C), :] = gr.astype(BF)
         return carry
 
     lax.fori_loop(0, N // C, back_rows, 0)
-    leave(got, gresid_o)
-    ls_, lr_, ll_ = al.take(1), al.take(1), al.take(1)
-    mine_rows = glow_o.at[pl.ds(pl.multiple_of(c * N, N), N), :]
-    far = rcopy(low, mine_rows, ls_(0), lr_(0), (sib, z))
-    near = lcopy(low, mine_rows, ll_(0))
-    far.start()
-    near.start()
-
-    for cp in copies:
-        cp.wait()
-    for h in range(heads):
-        for half, tag in ((1 - c, 0), (c, 1)):
-            rows = pl.ds(pl.multiple_of(half * N, N), N)
-            lcopy(probs.at[h, rows, :], probs_o.at[h, rows, :], pouts(tag, h)).wait()
-
-    @pl.when(mine)
-    def _():
-        for a in range(4):
-            for r in range(1, Z):
-                w_z(a, r).wait_send()
-        for t in range(3):
-            c_sib(t).wait_send()
-    for j in range(B):
-        @pl.when(B * c + j != z)
-        def _():
-            for a in range(4):
-                for k in range(1, Q):
-                    w_p(a, j, k, q).wait_send()
-    for r in range(1, Z):
-        for t in range(3):
-            c_fwd(t, lax.rem(z + r, Z), c).wait_send()
-        for i in range(2):
-            x_z(i, r).wait_send()
-    for s in range(B):
-        @pl.when(jnp.logical_not((B * c + s == z) & mine))
-        def _():
-            t_z(s).wait_send()
-    for x in (tgat, agat, gsum):
+    ls_, lr_ = al.take(1), al.take(1)
+
+    def far_x(half):
+        rows = glow.at[pl.ds(pl.multiple_of(half * N, N), N), :]
+        return rcopy(rows, rows, ls_(0), lr_(0), sib)
+
+    far_x(c).start()
+    for x in (tgat, gsum):
         x.drain()
     for k in range(Q):
         s_x(k).wait_send()
     h_x.wait_send()
-    for p in range(per):
-        here = (c * per + p == z) & mine
-
-        @pl.when(here)
-        def _():
-            for i in range(2):
-                row_l(i, p).wait()
-
-        @pl.when(jnp.logical_not(here))
-        def _():
-            for i in range(2):
-                row_x(i, p).wait_send()
-    for s in range(B):
-        @pl.when(jnp.logical_not((B * c + s == z) & mine))
-        def _():
-            for i in range(2):
-                rcopy(rows_out[i].at[s], rows_out[i].at[s], ms(i, 0), mr(i, s), (dp, z)).wait_recv()
-    near.wait()
-    far.wait()
-    assert al.used <= FRONT_SEMS
-
-
-def front(Q, Z, comp, mem, tok, cot, wq, wk, wv, wo, up, down, ub, vc, sq, g1, b1, g2, b2):
-    B, R, D = tok.shape
-    H = wq.shape[1]
-    S = R * Z
-    N = S // 2
+
+    @pl.when(mine)
+    def _():
+        for t in range(3):
+            c_sib(t).wait_send()
+    for r in range(1, Z):
+        for t in range(3):
+            c_fwd(t, lax.rem(z + r, Z), c).wait_send()
+    for i in range(2):
+        x_drain(i)
+    for p in partners:
+        pl.semaphore_signal(ready, inc=1, device_id=p, device_id_type=MESH)
+    far_x(1 - c).wait_recv()
+
     W = B * H
-    heads = W // HEAD_DIM
-    F = up.shape[1] // 2 // Q * Z
-    rows = 2 * Q * N
-    vm = pltpu.VMEM
-    return pl.pallas_call(
-        functools.partial(front_kernel, Q, Z),
-        out_shape=[
-            sds((S, D), BF), sds((3 * S, D), BF), sds((S, W), BF), sds((3 * S, W), BF), sds((3 * S, W), BF),
-            sds((heads, S, 3 * S), BF), sds((S, W), BF), sds((D, W), BF), sds((D, W), BF), sds((D, W), BF), sds((W, D), BF),
-            sds((N, D), F32), sds((N, D), F32), sds((S, D), BF), sds((D, F), BF), sds((F, D), BF), sds((rows, D), BF),
-            sds((8, D), F32), sds((B, R, D), BF), sds((B, R, D), BF),
-        ],
-        in_specs=[ANY] * 11 + [VM] + [ANY] + [VM] * 4,
-        out_specs=[ANY] * 17 + [VM] + [ANY] * 2,
-        scratch_shapes=[
-            vm((3, S, D), BF), vm((3 * S, D), BF), vm((D, W), BF), vm((D, W), BF), vm((D, W), BF), vm((W, D), BF),
-            vm((S, W), BF), vm((3 * S, W), BF), vm((3 * S, W), BF), vm((heads, S, 3 * S), BF), vm((S, W), BF),
-            vm((N, D), F32), vm((N, D), F32), vm((N, D), F32), vm((rows, D), BF), vm((rows, D), BF), vm((D, F), BF), vm((F, D), BF),
-            vm((Z, 1, F // Z), F32), vm(vc.shape, jnp.int32), vm((rows, F), BF), vm((rows, F), BF), vm((rows, D), BF),
-            vm((Q, N, D), BF), vm((2, N // 2, D), BF), vm((2, N, D), BF), vm((N, D), BF),
-            vm((N, D), BF), vm((N, D), BF), vm((D, F), BF), vm((F, D), BF), vm((rows, D), BF),
-            DMA((FRONT_SEMS,)),
-        ],
-        compiler_params=pltpu.CompilerParams(collective_id=1, has_side_effects=True, vmem_limit_bytes=63 << 20),
-        name="front",
-    )(comp, mem, tok, cot, wq, wk, wv, wo, up, down, ub, vc, sq, g1, b1, g2, b2)
-
-
-BACK_SEMS = 300
-
-
-def back_kernel(Q, Z, B, tok, normed_i, q_i, k_i, v_i, probs_i, mixed_i, wq_i, wk_i, wv_i, wo_i, resid_i, gresid_i, glow_i,
-                gu, gd, down_i, ffs, cot, g1, b1, db,
-                aw, ago, afu, afd, aub, small_o, out_o, tg_o,
-                normed, qs, ks, vs, probs, mixed, wqs, wks, wvs, wos, toks, resid, gresid, glow, gms,
-                xu, xd, xb, fus, fds, fbs, dgot, dnb, dh, dg, gkv, gqs, gos, gwb, gh, gg, oh, og,
-                wdone, odone, zb, zo, wfin, ofin, ghalf, ggot, cots, arow, sums, sgot, srow, pgot, zgot, outs, tgs, sems):
-    dp, c, q, z = where_am_i(Q, Z)
-    sib = (dp + 1 - 2 * c, z)
-    partners = [sib]
-    for r in range(1, Z):
-        for d in (dp, dp + 1 - 2 * c):
-            partners.append((d, lax.rem(z + r, Z)))
-
-    def peer(k):
-        return (2 * across(q, k) + c, z)
-
-    for k in range(1, Q):
-        partners.append(peer(k))
-    enter(partners)
-    S, D = glow.shape
-    N = S // 2
-    W = qs.shape[1]
-    H = W // B
-    F = gd.shape[0]
-    E = F // Z
-    R = S // Z
-    heads = W // HEAD_DIM
     hj = H // HEAD_DIM
-    mine = c == z // B
-    jz = lax.rem(z, B)
-    al = Slots(sems)
-
-    def dev(k, core):
-        return 2 * across(q, k) + core
-
-    def up_to_z(r):
-        return (dp, lax.rem(z + Z - r, Z))
-
-    xs, xr = al.take(3, Z), al.take(3, Z)
-
-    def x_z(i, r):
-        if i == 0:
-            return rcopy(gu.at[:, pl.ds(r * E, E)], xu.at[r], xs(0, r), xr(0, r), up_to_z(r))
-        if i == 1:
-            return rcopy(gd.at[pl.ds(r * E, E), :], xd.at[r], xs(1, r), xr(1, r), up_to_z(r))
-        return rcopy(ffs.at[pl.ds(2, 1), pl.ds(r * E, E)], xb.at[r], xs(2, r), xr(2, r), up_to_z(r))
-
-    ss, sr = al.take(Q), al.take(Q)
-
-    def d_x(k):
-        return rcopy(down_i.at[pl.ds(pl.multiple_of(dev(k, 1 - c) * N, N), N), :], dgot.at[k], ss(k), sr(k), sib)
-
-    ld = al.take(30)
-    pairs = [(wo_i, wos), (glow_i, glow), (mixed_i, mixed), (probs_i, probs), (v_i, vs), (k_i, ks), (q_i, qs),
-             (normed_i, normed), (wq_i, wqs), (wk_i, wks), (wv_i, wvs), (gresid_i, gresid), (resid_i, resid),
-             (tok.at[pl.ds(pl.multiple_of(c * N, N), N), :], toks), (cot, cots),
-             (gu.at[:, pl.ds(0, E)], xu.at[0]), (gd.at[pl.ds(0, E), :], xd.at[0])]
-    pairs += [(down_i.at[pl.ds(pl.multiple_of(dev(k, c) * N, N), N), :], dnb.at[k]) for k in range(Q)]
-    loads = [lcopy(src, dst, ld(i)) for i, (src, dst) in enumerate(pairs)]
-    for x in loads[:3] + loads[17:]:
-        x.start()
-    for k in (3, 1, 2, 0):
-        d_x(k).start()
-    for x in loads[3:17]:
-        x.start()
-    for r in range(1, Z):
-        for i in range(3):
-            x_z(i, r).start()
-
-    for x in loads[:3]:
-        x.wait()
-    T = 256
+    M = D // Q
+    gms, gqs, gkv = gup.at[pl.ds(0, S), :], gup.at[pl.ds(S, S), :], act.at[pl.ds(0, 3 * S), :]
+    gos = gbuf.at[pl.ds(0, W), :]
+    tgs, outs = ctx.at[0, pl.ds(0, N), :], ctx.at[0, pl.ds(N, N), :]
+    small1 = ctx.at[1]
+    odone = stack(small1, 2 * S // 2 - B * OR, OR)
+    wdone = stack(downs, 0, M, 3 * H)
+    zb, zo = stack(got1, 0, M, 3 * H), stack(gg, 0, OR)
+    wfin, ofin = gg.at[pl.ds(N, M), pl.ds(0, 3 * H)], gh.at[pl.ds(0, OR), :]
 
     def mix_rows(i, carry):
         at = pl.ds(pl.multiple_of(i * T, T), T)
@@ -1142,8 +1130,6 @@
         return carry
 
     lax.fori_loop(0, S // T, mix_rows, 0)
-    OR = H // Q
-    M = D // Q
 
     def o_blk(j):
         def blk(k, lo, n):
@@ -1152,26 +1138,22 @@
 
     def w_blk(j):
         def blk(k, lo, n):
-            return gwb.at[j, pl.ds(pl.multiple_of(across(q, k) * M + lo, n), n), :]
+            return cots.at[pl.ds(pl.multiple_of(j * D + across(q, k) * M + lo, n), n), pl.ds(0, 3 * H)]
         return blk
 
-    osum = [PlaneSum(al, peer, o_blk(j), OR, oh.at[j], og.at[j]) for j in range(B)]
-    wsum = [PlaneSum(al, peer, w_blk(j), M, gh.at[j], gg.at[j]) for j in range(B)]
-    dsum = PlaneSum(al, peer, lambda k, lo, n: dnb.at[k, pl.ds(lo, n), :], N, dh, dg)
+    osum = [
+        PlaneSum(al, peer, o_blk(j), OR, stack(small1, j * OR, OR // 2), stack(small1, B * OR + 2 * j * OR, OR)) for j in range(B)
+    ]
+    wsum = [
+        PlaneSum(al, peer, w_blk(j), M, stack(gbuf, W + 2 * B * M + j * M, M // 2, 3 * H), stack(gbuf, W + 2 * j * M, M, 3 * H))
+        for j in range(B)
+    ]
+    pl.semaphore_wait(ready, len(partners))
     for x in osum:
         x.start()
-    for x in loads[17:]:
-        x.wait()
-    for k in (3, 1, 2, 0):
-        d_x(k).wait_recv()
-        dnb[k] = (dnb[k].astype(F32) + dgot[k].astype(F32)).astype(BF)
-        if k == 3:
-            dsum.start()
-    sums[...] = jnp.zeros_like(sums)
     arow[...] = jnp.zeros_like(arow)
-    scale = HEAD_DIM ** (-0.5)
-
-    def head(h, hh):
+
+    def back_head(h, hh):
         hd = pl.ds(h * HEAD_DIM, HEAD_DIM)
         ko = pl.ds(hh * HEAD_DIM, HEAD_DIM)
         vo = pl.ds(H + hh * HEAD_DIM, HEAD_DIM)
@@ -1198,8 +1180,9 @@
             at = pl.ds(pl.multiple_of(i * T, T), T)
             kv = tn_dot(normed[:, at], gkv[...])
             gq = tn_dot(normed[pl.ds(2 * S, S), at], gqs[:, js])
-            gwb[j, at, pl.ds(0, 2 * H)] = kv.astype(BF)
-            gwb[j, at, pl.ds(2 * H, H)] = gq.astype(BF)
+            to = pl.ds(pl.multiple_of(j * D + i * T, T), T)
+            cots[to, pl.ds(0, 2 * H)] = kv.astype(BF)
+            cots[to, pl.ds(2 * H, H)] = gq.astype(BF)
             t = (kv[:, :H] * wks[at, js].astype(F32) + kv[:, H:] * wvs[at, js].astype(F32) + gq * wqs[at, js].astype(F32))
             arow[at, :] = arow[at, :] + jnp.broadcast_to(jnp.sum(t, axis=-1, keepdims=True), (T, 128))
             return carry
@@ -1211,13 +1194,8 @@
         b = nt_dot(skv[:, :H], wks[:, js]) + nt_dot(skv[:, H:], wvs[:, js]) + nt_dot(sq_, wqs[:, js])
         sums[1:2, :] = sums[1:2, :] + jnp.sum(b, axis=0, keepdims=True)
 
-    for x in loads[3:7]:
-        x.wait()
     for h in range(hj):
-        head(h, h)
-    for x in loads[7:11]:
-        x.wait()
-    H2 = pl.ds(2 * S, S)
+        back_head(h, h)
 
     def token_rows(j, half):
         js = pl.ds(j * H, H)
@@ -1230,42 +1208,40 @@
         x.middle()
     weights(0)
     dsum.middle()
-    ghalf[...] = token_rows(0, 1 - c)
+    y_middle(0)
+    phalf[...] = token_rows(0, 1 - c)
     srow[...] = token_rows(0, c)
     for h in range(hj, 2 * hj):
-        head(h, h - hj)
+        back_head(h, h - hj)
     wsum[0].middle()
+    y_middle(1)
     weights(1)
-    ghalf[...] = ghalf[...] + token_rows(1, 1 - c)
+    phalf[...] = phalf[...] + token_rows(1, 1 - c)
     ts_, tr_ = al.take(1), al.take(1)
-    t_x = rcopy(ghalf, ggot, ts_(0), tr_(0), sib)
+    t_x = rcopy(phalf, ggot, ts_(0), tr_(0), sib)
     t_x.start()
     srow[...] = srow[...] + token_rows(1, c)
 
-    for x in loads[11:17]:
-        x.wait()
     acol = jnp.swapaxes(arow[...], 0, 1)[0:1, :]
     bsum = sums[1:2, :]
     sums[0:1, :] = (acol - b1[...] * bsum) / g1[...]
     sums[2:3, :] = ffs[0:1, :]
     sums[3:4, :] = ffs[1:2, :]
-    sums[4:5, :] = jnp.sum(cots[...].astype(F32), axis=(0, 1)).reshape(1, D)
     n1, n2 = al.take(1), al.take(1)
     v_x = rcopy(sums, sgot, n1(0), n2(0), sib)
     v_x.start()
-    osums = []
     ozs, ozr = al.take(2, B), al.take(2, Z)
 
     def z_x(i, j):
         src, dst = ((wdone, zb), (odone, zo))[i]
-        return rcopy(src.at[j], dst.at[z], ozs(i, j), ozr(i, z), (dp, B * c + j))
+        return rcopy(src(j), dst(z), ozs(i, j), ozr(i, z), (dp, B * c + j))
 
     def z_arrive(i, zz):
         dst = (zb, zo)[i]
-        return rcopy(dst.at[zz], dst.at[zz], ozs(i, 0), ozr(i, zz), (dp, z))
+        return rcopy(dst(zz), dst(zz), ozs(i, 0), ozr(i, zz), (dp, z))
 
     def to_plane(i, j):
-        ((wdone, odone)[i])[j] = ((wsum, osum)[i])[j].total().astype(BF)
+        (wdone, odone)[i](j)[...] = (wsum, osum)[i][j].total().astype(BF)
 
         @pl.when(B * c + j != z)
         def _():
@@ -1275,20 +1251,17 @@
     for j in range(B):
         to_plane(1, j)
     t_x.wait_recv()
-    C = 64
-
     def norm_rows(i, carry):
         at = pl.ds(pl.multiple_of(i * C, C), C)
         gn = srow[at, :] + ggot[at, :]
-        xhat, inv = layer_norm_rows(toks[at, :].astype(F32))
+        xhat, inv = layer_norm_rows(ctx[2, pl.ds(pl.multiple_of(c * N + i * C, C), C), :].astype(F32))
         e = gn * g1[...]
         m1 = jnp.mean(e, axis=-1, keepdims=True)
         m2 = jnp.mean(e * xhat, axis=-1, keepdims=True)
-        tgs[at, :] = (gresid[at, :] + inv * (e - m1 - xhat * m2)).astype(BF)
+        tgs[at, :] = (got[at, :] + inv * (e - m1 - xhat * m2)).astype(BF)
         return carry
 
     lax.fori_loop(0, N // C, norm_rows, 0)
-    per = N // R
     rs, rr, rl = al.take(2, 2), al.take(2, B), al.take(2)
     rows_in = [tgs, outs]
     rows_out = [tg_o, out_o]
@@ -1312,14 +1285,15 @@
                 row_x(i, p).start()
 
     send_rows(0)
+    for i in range(2):
+        y_arrive(i)
+    fu = y_own(0, 0)[...].astype(F32) + (xu[0].astype(F32) + xu[1].astype(F32))
+    fd = y_own(1, 0)[...].astype(F32) + (xd[0].astype(F32) + xd[1].astype(F32))
+    fb = ffs[2:3, 0:E]
     for r in range(1, Z):
-        for i in range(3):
-            x_z(i, r).wait_recv()
-    fu, fd, fb = xu[0].astype(F32), xd[0].astype(F32), ffs[2:3, 0:E]
-    for r in range(1, Z):
-        fu = fu + xu[r].astype(F32)
-        fd = fd + xd[r].astype(F32)
+        ub_x(r).wait_recv()
         fb = fb + xb[r]
+    fus, fds = xu.at[2], xd.at[2]
     fus[...] = fu.astype(BF)
     fds[...] = fd.astype(BF)
     fbs[...] = fb
@@ -1379,8 +1353,6 @@
 
     for k in range(1, Q):
         vp_x(k).start()
-    for i in range(2):
-        pass
     outs[...] = (resid[...] + dsum.total() + db[...]).astype(BF)
     send_rows(1)
     to_plane(0, 0)
@@ -1412,10 +1384,10 @@
                 @pl.when(zz != z)
                 def _():
                     z_arrive(i, zz).wait_recv()
-            buf[z] = done[jz]
-            t = buf[0].astype(F32)
+            buf(z)[...] = done(jz)[...]
+            t = buf(0)[...].astype(F32)
             for zz in range(1, Z):
-                t = t + buf[zz].astype(F32)
+                t = t + buf(zz)[...].astype(F32)
             fin[...] = t.astype(BF)
             gat.start()
             g_l[1 if i == 1 else 0].start()
@@ -1462,8 +1434,9 @@
         x.wait()
     for r in range(1, Z):
         vz_x(r).wait_send()
-        for i in range(3):
-            x_z(i, r).wait_send()
+        ub_x(r).wait_send()
+    for i in range(2):
+        y_drain(i)
     for x in osum + wsum + [dsum, ugat, dgat]:
         x.drain()
 
@@ -1496,43 +1469,78 @@
         def _():
             for i in range(2):
                 rcopy(rows_out[i].at[s], rows_out[i].at[s], rs(i, 0), rr(i, s), (dp, z)).wait_recv()
-    assert al.used <= BACK_SEMS
-
-
-def back(Q, Z, B, tok, normed, q_, k_, v_, probs, mixed, wq, wk, wv, wo, resid, gresid, glow, gu, gd, down, ffs, cot, g1, b1, db):
-    S, D = glow.shape
-    N, R = S // 2, S // Z
-    W = q_.shape[1]
-    H = W // B
-    F = gd.shape[0]
-    E = F // Z
+    far_x(c).wait_send()
+
+    @pl.when(mine)
+    def _():
+        for a in range(4):
+            for r in range(1, Z):
+                w_z(a, r).wait_send()
+    for j in range(B):
+        @pl.when(B * c + j != z)
+        def _():
+            for a in range(4):
+                for k in range(1, Q):
+                    w_p(a, j, k, q).wait_send()
+    for s in range(B):
+        @pl.when(jnp.logical_not((B * c + s == z) & mine))
+        def _():
+            t_z(s).wait_send()
+    for p in range(per):
+        here = (c * per + p == z) & mine
+
+        @pl.when(here)
+        def _():
+            for i in range(2):
+                keep_l(i, p).wait()
+
+        @pl.when(jnp.logical_not(here))
+        def _():
+            for i in range(2):
+                keep_x(i, p).wait_send()
+    for s in range(B):
+        @pl.when(jnp.logical_not((B * c + s == z) & mine))
+        def _():
+            for i in range(2):
+                rcopy(kept_out[i].at[s], kept_out[i].at[s], ms(i, 0), mr(i, s), (dp, z)).wait_recv()
+    assert al.used <= LAYER_SEMS
+
+
+def layer(Q, Z, comp, mem, tok, cot, wq, wk, wv, wo, up, down, ub, vc, sq, g1, b1, g2, b2, db):
+    B, R, D = tok.shape
+    H = wq.shape[1]
+    S = R * Z
+    N = S // 2
+    W = B * H
     heads = W // HEAD_DIM
-    M, OR = D // Q, H // Q
+    E = up.shape[1] // (2 * Q)
+    F = E * Z
+    rows = 2 * Q * N
     vm = pltpu.VMEM
     return pl.pallas_call(
-        functools.partial(back_kernel, Q, Z, B),
+        functools.partial(layer_kernel, Q, Z),
         out_shape=[
             sds((D, 3 * H), BF), sds((H, D), BF), sds((D, 2 * Q * E), BF), sds((2 * Q * E, D), BF), sds((2 * Q, 1, E), F32),
-            sds((8, D), F32), sds((B, R, D), BF), sds((B, R, D), BF),
+            sds((8, D), F32), sds((B, R, D), BF), sds((B, R, D), BF), sds((B, R, D), BF), sds((B, R, D), BF),
         ],
-        in_specs=[ANY] * 17 + [VM] + [ANY] + [VM] * 3,
-        out_specs=[ANY] * 5 + [VM] + [ANY] * 2,
+        in_specs=[ANY] * 11 + [VM] + [ANY] + [VM] * 5,
+        out_specs=[ANY] * 5 + [VM] + [ANY] * 4,
         scratch_shapes=[
-            vm((3 * S, D), BF), vm((S, W), BF), vm((3 * S, W), BF), vm((3 * S, W), BF), vm((heads, S, 3 * S), BF), vm((S, W), BF),
-            vm((D, W), BF), vm((D, W), BF), vm((D, W), BF), vm((W, D), BF),
-            vm((N, D), BF), vm((N, D), F32), vm((N, D), F32), vm((S, D), BF), vm((S, W), BF),
-            vm((Z, D, E), BF), vm((Z, E, D), BF), vm((Z, 1, E), F32), vm((D, E), BF), vm((E, D), BF), vm((1, E), F32),
-            vm((Q, N, D), BF), vm((Q, N, D), BF), vm((2, N // 2, D), BF), vm((2, N, D), BF),
-            vm((3 * S, 2 * H), BF), vm((S, W), BF), vm((W, D), BF), vm((B, D, 3 * H), BF),
-            vm((B, 2, M // 2, 3 * H), BF), vm((B, 2, M, 3 * H), BF), vm((B, 2, OR // 2, D), BF), vm((B, 2, OR, D), BF),
-            vm((B, M, 3 * H), BF), vm((B, OR, D), BF), vm((Z, M, 3 * H), BF), vm((Z, OR, D), BF), vm((M, 3 * H), BF), vm((OR, D), BF),
-            vm((N, D), F32), vm((N, D), F32), vm(cot.shape, BF), vm((D, 128), F32),
-            vm((8, D), F32), vm((8, D), F32), vm((N, D), F32), vm((Q, 8, D), F32), vm((Z, 8, D), F32), vm((N, D), BF), vm((N, D), BF),
-            DMA((BACK_SEMS,)),
+            vm((3, S, D), BF), vm((3 * S, D), BF), vm((D, W), BF), vm((D, W), BF), vm((D, W), BF), vm((W, D), BF),
+            vm((S, W), BF), vm((3 * S, W), BF), vm((3 * S, W), BF), vm((heads, S, 3 * S), BF), vm((S, W), BF),
+            vm((N, D), F32), vm((N, D), F32), vm((N, D), F32), vm((rows, D), BF), vm((rows, D), BF), vm((D, F), BF), vm((F, D), BF),
+            vm((Z, 1, E), F32), vm(vc.shape, jnp.int32), vm((rows, F), BF), vm((rows, F), BF), vm((rows, D), BF),
+            vm((Q * N, D), BF), vm((N, D), BF), vm((2 * N, D), BF), vm((S, D), BF),
+            vm((N, D), BF), vm((N, D), BF), vm((D, F), BF), vm((F, D), BF), vm((Q * N, D), BF), vm((N, D), BF), vm((2 * N, D), BF),
+            vm((N, D), F32), vm((N, D), F32),
+            vm((4, D, E), BF), vm((4, E, D), BF), vm((Z, 1, E), F32), vm((1, E), F32),
+            vm((D, 128), F32), vm((8, D), F32), vm((8, D), F32), vm((8, D), F32),
+            vm((Q, 8, D), F32), vm((Z, 8, D), F32),
+            DMA((LAYER_SEMS,)), pltpu.SemaphoreType.REGULAR,
         ],
-        compiler_params=pltpu.CompilerParams(collective_id=2, has_side_effects=True, vmem_limit_bytes=63 << 20),
-        name="back",
-    )(tok, normed, q_, k_, v_, probs, mixed, wq, wk, wv, wo, resid, gresid, glow, gu, gd, down, ffs, cot, g1, b1, db)
+        compiler_params=pltpu.CompilerParams(collective_id=1, has_side_effects=True, vmem_limit_bytes=63 << 20),
+        name="layer",
+    )(comp, mem, tok, cot, wq, wk, wv, wo, up, down, ub, vc, sq, g1, b1, g2, b2, db)
 
 
 def chip_device(Q, Z, tokens, memory, compressed, valid_counts, attention_norm_gain, attention_norm_bias,
@@ -1542,16 +1550,11 @@
     H = query_projection.shape[1]
     FL = up_weight.shape[1]
     E = FL // (2 * Q)
-    (tok_all, normed, q_, k_, v_, probs, mixed, wqg, wkg, wvg, wog, resid, g_resid, g_low, up_low, down_g_low, down,
-     ff_small, o_nm, o_nc) = front(
+    aw, ago, afu, afd, aub, small, o_out, o_tg, o_nm, o_nc = layer(
         Q, Z, compressed, memory, tokens, cotangent, query_projection, key_projection, value_projection, out_weight,
         up_weight, down_weight, up_bias.reshape(2 * Q, 1, E), jnp.broadcast_to(valid_counts[:, None, None], (B, 8, 128)),
         squeeze_weight, attention_norm_gain.reshape(1, D), attention_norm_bias.reshape(1, D),
-        feedforward_norm_gain.reshape(1, D), feedforward_norm_bias.reshape(1, D),
-    )
-    aw, ago, afu, afd, aub, small, o_out, o_tg = back(
-        Q, Z, B, tok_all, normed, q_, k_, v_, probs, mixed, wqg, wkg, wvg, wog, resid, g_resid, g_low, up_low, down_g_low, down,
-        ff_small, cotangent, attention_norm_gain.reshape(1, D), attention_norm_bias.reshape(1, D), down_bias.reshape(1, D),
+        feedforward_norm_gain.reshape(1, D), feedforward_norm_bias.reshape(1, D), down_bias.reshape(1, D),
     )
     aw = aw.astype(F32)
     return (

time: 303 us -> 287 us (0.947)
  Pallas kernels: 284 us -> 270 us
    pallas_call x2 -> x1, Pallas kernels: 284 us -> 270 us  [layer(): pl.pallas_call(functools.partial(layer_kernel, Q, Z), out_shape=[sds((D,...]
where the time goes in v2:
time: 287 us
  Pallas kernels  270 us (94%)
  local copies, waits for them, and re-layouts  9.21 us (3%)
  other arithmetic  7.12 us (2%)
    pallas_call x1, Pallas kernels, layer(): pl.pallas_call(functools.partial(layer_kernel, Q, Z), out_shape=[sds((D,...  270 us

profile of v2, /device:TPU:9, one launch (start us, length us, event | category | flops | bytes accessed | tf_op | source)
XLA Modules:
  0.0 286.5 jit_solution(10137530992408572621)
XLA Ops:
  0.6 1.3 broadcast_in_dim.2.vc
  2.0 269.5 %layer.1 = (bf16[1024,768]{1,0:T(8,128)(2,1)}, bf16[256,1024]{1,0:T(8,128)(2,1)}, bf16[1024,1024]{1,0:T(8,128)(2,1)}, bf16[1024,1024]{1,0:T(8,128)(2,1)}, f32[8,...) custom-call(bf16[2,128,1024]{2,1,0:T(8,128)(2,1)} %comp.1, ...), custom_call_target="tpu_custom_call" | custom-call | tf_op jit(solution)/shard_map/layer/pallas_call | solution.py:1520
  271.5 1.6 fusion.1
  273.1 0.0 copy-start.1
  273.1 3.3 %fusion = (f32[1024,256]{1,0:T(8,128)}, f32[1024,256]{1,0:T(8,128)}, f32[1024,256]{1,0:T(8,128)}) fusion(bf16[1024,768]{1,0:T(8,128)(2,1)} %get-tuple-element.29), kind=kLoop, calls=%fused_computation | loop fusion | bytes 6291456 | tf_op jit(solution)/shard_map/slice | solution.py:1561
  276.4 0.0 copy-done.1
  276.4 0.0 copy-start
  276.4 2.5 convert_element_type.18
  278.9 0.0 copy-done
  278.9 0.0 copy-start.3
  278.9 0.0 copy-start.2
  278.9 2.5 convert_element_type.19
  281.4 0.0 copy-start.6
  281.4 0.0 copy-done.3
  281.4 0.0 copy-start.7
  281.4 0.0 copy-start.5
  281.4 1.1 convert_element_type.15
  282.5 0.0 copy-start.4
  282.5 0.0 copy-done.2
  282.5 1.1 convert_element_type.17
  283.5 0.0 copy-done.6
  283.6 0.8 copy.38
  284.3 0.0 copy-done.7
  284.3 0.6 copy.39
  284.9 0.0 copy-done.5
  284.9 0.8 copy.40
  285.7 0.0 copy-done.4
  285.7 0.8 copy.41
Async XLA Ops:
  273.1 3.3 %copy-start.1 = (bf16[1024,1024]{1,0:T(8,128)(2,1)S(1)}, bf16[1024,1024]{1,0:T(8,128)(2,1)}, u32[]{:S(2)}) copy-start(bf16[1024,1024]{1,0:T(8,128)(2,1)} %get-tuple-element.31) | copy-start | bytes 6291460
  276.4 2.5 copy-start
  278.9 2.5 copy-start.3
  278.9 3.6 %copy-start.2 = (bf16[256,1024]{1,0:T(8,128)(2,1)S(1)}, bf16[256,1024]{1,0:T(8,128)(2,1)}, u32[]{:S(2)}) copy-start(bf16[256,1024]{1,0:T(8,128)(2,1)} %get-tuple-element.30) | copy-start | bytes 1572868
  281.4 2.2 copy-start.6
  281.4 3.0 %copy-start.7 = (f32[8,1,128]{2,1,0:T(1,128)S(1)}, f32[8,1,128]{2,1,0:T(1,128)}, u32[]{:S(2)}) copy-start(f32[8,1,128]{2,1,0:T(1,128)} %get-tuple-element.32) | copy-start | bytes 12292
  281.4 3.6 %copy-start.5 = (bf16[2,128,1024]{2,1,0:T(8,128)(2,1)S(1)}, bf16[2,128,1024]{2,1,0:T(8,128)(2,1)}, u32[]{:S(2)}) copy-start(bf16[2,128,1024]{2,1,0:T(8,128)(2,1)} %get-tuple-element.74) | copy-start | bytes 1572868
  282.5 3.3 %copy-start.4 = (bf16[2,128,1024]{2,1,0:T(8,128)(2,1)S(1)}, bf16[2,128,1024]{2,1,0:T(8,128)(2,1)}, u32[]{:S(2)}) copy-start(bf16[2,128,1024]{2,1,0:T(8,128)(2,1)} %get-tuple-element.75) | copy-start | bytes 1572868

commit v3 on v2

--- a/solution.py
+++ b/solution.py
@@ -350,6 +350,12 @@
     if k == 2:
         return lax.rem(q + 2, 4)
     return 3 - q
+
+
+def across_by(q, i):
+    x, y = lax.rem(q, 2), q // 2
+    dx, dy = 1 - lax.rem(i, 2), 1 - i // 2
+    return (x + dx - 2 * x * dx) + 2 * (y + dy - 2 * y * dy)
 
 
 def layer_norm_rows(rows):
@@ -555,11 +561,22 @@
     def w_z(a, r):
         return rcopy(piece(a), place(a, jz, q), ws(a, r - 1), wr(a, jz), (dp, lax.rem(z + r, Z)))
 
+    def w_direct(r):
+        zt = lax.rem(z + r, Z)
+        return jnp.logical_not((lax.rem(zt, Z - 1) == 0) & (zt // B != z // B))
+
+    wf = al.take(4, B)
+
+    def w_onward(a, j):
+        return rcopy(place(a, j, q), place(a, j, q), wf(a, j), wr(a, j), (dp, (Z - 1) * (1 - c)))
+
     def w_arrive(a, j):
         return rcopy(place(a, j, q), place(a, j, q), ws(a, 0), wr(a, j), (dp, z))
 
     def w_p(a, j, k, qq):
         return rcopy(place(a, j, qq), place(a, j, qq), ps(a, j, k - 1), pr(a, j, k - 1), peer(k))
+
+    relay = z == 2 - c
 
     def w_l(a):
         return lcopy(wins[a], place_whole(a, jz), wl(a))
@@ -692,9 +709,11 @@
     sums[...] = jnp.zeros_like(sums)
     @pl.when(mine)
     def _():
-        for a in range(4):
-            for r in range(1, Z):
-                w_z(a, r).start()
+        for r in range(1, Z):
+            @pl.when(w_direct(r))
+            def _():
+                for a in range(4):
+                    w_z(a, r).start()
         for a in range(4):
             w_l(a).start()
         for t in range(3):
@@ -711,6 +730,10 @@
         def _():
             for a in range(4):
                 w_arrive(a, j).wait_recv()
+
+                @pl.when(relay)
+                def _():
+                    w_onward(a, j).start()
                 for k in range(1, Q):
                     w_p(a, j, k, q).start()
     for s in range(B):
@@ -765,6 +788,7 @@
         @pl.when(jnp.logical_not(here))
         def _():
             t_z(s).start()
+    x_start(0)
     for r in range(1, Z):
         zs = lax.rem(z + r, Z)
         for t in range(3):
@@ -803,7 +827,7 @@
         return carry
 
     lax.fori_loop(0, S // T, project_q, 0)
-    x_start(0)
+    x_start(1)
 
     v_s.wait()
     counts = jnp.where(mine, vc[jz], vco[jz])
@@ -841,7 +865,6 @@
     attend(1 - c, 0)
     phalf[...] = nn_dot(mixed[pl.ds(pl.multiple_of((1 - c) * N, N), N), :], wos[...])
     h_x.start()
-    x_start(1)
     for i in range(B):
         @pl.when(jnp.logical_not((B * c + i == z) & mine))
         def _():
@@ -853,6 +876,7 @@
     tgat.start()
     attend(c, 1)
     own_part = nn_dot(mixed[pl.ds(pl.multiple_of(c * N, N), N), :], wos[...])
+    x_forward(0)
     h_x.wait_recv()
     resid[...] = ctx[2, pl.ds(pl.multiple_of(c * N, N), N), :].astype(F32) + (own_part + got[...])
     xhat2, _ = layer_norm_rows(resid[...])
@@ -872,24 +896,38 @@
     gsum = PlaneSum(al, peer, rows_at(gbuf, c), N, stack(gh, 0, N // 2), stack(gg, 0, N))
     ffs[...] = jnp.zeros_like(ffs)
 
-    def forward_block(b, bias_row):
+    def slope_at(b):
+        return (b // 4, pl.ds(pl.multiple_of(lax.rem(b // 2, 2) * N, N), N), pl.ds(pl.multiple_of(lax.rem(b, 2) * Z * E, Z * E), Z * E))
+
+    def up_block(b, bias_row):
         at = pl.ds(pl.multiple_of(b * N, N), N)
         x = nn_dot(sec[at, :], ups[...]) + bias_row
-        ga = nt_dot(cots[at, :], downs[...])
         x2 = x * x
         root = 0.7978845608028654
         th = jnp.tanh(root * (x + 0.044715 * (x2 * x)))
         act[at, :] = (0.5 * x * (1.0 + th)).astype(BF)
         slope = 0.5 * (1.0 + th) + 0.5 * x * (1.0 - th * th) * (root * (1.0 + 0.134145 * x2))
-        gu = (ga * slope).astype(BF)
+        ctx[slope_at(b)] = slope.astype(BF)
+        return bias_row
+
+    def back_block(b):
+        at = pl.ds(pl.multiple_of(b * N, N), N)
+        ga = nt_dot(cots[at, :], downs[...])
+        gu = (ga * ctx[slope_at(b)].astype(F32)).astype(BF)
         gup[at, :] = gu
         ffs[2:3, pl.ds(0, Z * E)] = ffs[2:3, pl.ds(0, Z * E)] + jnp.sum(gu.astype(F32), axis=0, keepdims=True)
         gbuf[at, :] = nt_dot(gu, ups[...]).astype(BF)
-        return bias_row
-
-    def feed(k, bias_row):
-        lax.fori_loop(dev(k, 0), dev(k, 0) + 2, forward_block, bias_row)
-        s_x(k).start()
+
+    def feed(k):
+        def half(i, carry):
+            back_block(dev(k, 1 - c) + i * (2 * c - 1))
+
+            @pl.when(i == 0)
+            def _():
+                s_x(k).start()
+            return carry
+
+        lax.fori_loop(0, 2, half, 0)
 
     def combine(k):
         s_x(k).wait_recv()
@@ -925,21 +963,29 @@
     def keep_l(i, p):
         return lcopy(kept_in[i].at[pl.ds(p * R, R), :], kept_out[i].at[jz], ml(i))
 
-    x_forward(0)
+    x_forward(1)
     tgat.middle()
     agat.middle()
     tgat.last()
-    x_forward(1)
     agat.last()
     for r in range(1, Z):
         u_z(r).wait()
-    for i in range(2):
-        x_rest(i)
     u_l.wait()
+
+    @pl.when(mine)
+    def _():
+        for t in range(3):
+            c_sib(t).wait_send()
+    for r in range(1, Z):
+        for t in range(3):
+            c_fwd(t, lax.rem(z + r, Z), c).wait_send()
+    x_rest(0)
     for x in x_l:
         x.wait()
+    agat.arrivals(rows_at(sec, 1 - c))
+    lax.fori_loop(0, 2 * Q, up_block, jnp.concatenate([ubs[r] for r in range(Z)], axis=1))
+    x_rest(1)
     tgat.arrivals(rows_at(cots, 1 - c))
-    agat.arrivals(rows_at(sec, 1 - c))
     for p in range(per):
         here = (c * per + p == z) & mine
 
@@ -953,16 +999,16 @@
             for i in range(2):
                 keep_x(i, p).start()
 
-    bias = jnp.concatenate([ubs[r] for r in range(Z)], axis=1)
-    feed(3, bias)
-    feed(1, bias)
+
+    feed(3)
     combine(3)
     gsum.start()
-    feed(2, bias)
+    feed(1)
+    feed(2)
     combine(1)
-    feed(0, bias)
     combine(2)
     gsum.middle()
+    feed(0)
 
     def up_grad(i, carry):
         at = pl.ds(pl.multiple_of(i * T, T), T)
@@ -1062,11 +1108,9 @@
         d_x(k).wait_recv()
         rows = rows_at(sec, c)(k, 0, N)
         rows[...] = (rows[...].astype(F32) + stack(dgot, 0, N)(k)[...].astype(F32)).astype(BF)
-        if k == 3:
-            dsum.start()
-
     combine(0)
     gsum.arrive()
+    dsum.start()
     C = 64
 
     def back_rows(i, carry):
@@ -1097,14 +1141,6 @@
     for k in range(Q):
         s_x(k).wait_send()
     h_x.wait_send()
-
-    @pl.when(mine)
-    def _():
-        for t in range(3):
-            c_sib(t).wait_send()
-    for r in range(1, Z):
-        for t in range(3):
-            c_fwd(t, lax.rem(z + r, Z), c).wait_send()
     for i in range(2):
         x_drain(i)
     for p in partners:
@@ -1119,8 +1155,7 @@
     tgs, outs = ctx.at[0, pl.ds(0, N), :], ctx.at[0, pl.ds(N, N), :]
     small1 = ctx.at[1]
     odone = stack(small1, 2 * S // 2 - B * OR, OR)
-    wdone = stack(downs, 0, M, 3 * H)
-    zb, zo = stack(got1, 0, M, 3 * H), stack(gg, 0, OR)
+    zo = stack(gg, 0, OR)
     wfin, ofin = gg.at[pl.ds(N, M), pl.ds(0, 3 * H)], gh.at[pl.ds(0, OR), :]
 
     def mix_rows(i, carry):
@@ -1136,16 +1171,24 @@
             return gos.at[pl.ds(pl.multiple_of(j * H + across(q, k) * OR + lo, n), n), :]
         return blk
 
-    def w_blk(j):
+    M2 = M // 2
+
+    def w_blk(j, half):
         def blk(k, lo, n):
-            return cots.at[pl.ds(pl.multiple_of(j * D + across(q, k) * M + lo, n), n), pl.ds(0, 3 * H)]
+            return cots.at[pl.ds(pl.multiple_of(j * D + across(q, k) * M + half * M2 + lo, n), n), pl.ds(0, 3 * H)]
         return blk
 
     osum = [
         PlaneSum(al, peer, o_blk(j), OR, stack(small1, j * OR, OR // 2), stack(small1, B * OR + 2 * j * OR, OR)) for j in range(B)
     ]
     wsum = [
-        PlaneSum(al, peer, w_blk(j), M, stack(gbuf, W + 2 * B * M + j * M, M // 2, 3 * H), stack(gbuf, W + 2 * j * M, M, 3 * H))
+        [
+            PlaneSum(
+                al, peer, w_blk(j, half), M2,
+                stack(gbuf, W + 2 * B * M + j * M + half * M2, M2 // 2, 3 * H), stack(gbuf, W + 2 * j * M + half * M, M2, 3 * H),
+            )
+            for half in range(2)
+        ]
         for j in range(B)
     ]
     pl.semaphore_wait(ready, len(partners))
@@ -1177,18 +1220,23 @@
         js = pl.ds(j * H, H)
 
         def rows(i, carry):
-            at = pl.ds(pl.multiple_of(i * T, T), T)
+            to_chip = across_by(q, i)
+            at = pl.ds(pl.multiple_of(to_chip * M, M), M)
             kv = tn_dot(normed[:, at], gkv[...])
             gq = tn_dot(normed[pl.ds(2 * S, S), at], gqs[:, js])
-            to = pl.ds(pl.multiple_of(j * D + i * T, T), T)
+            to = pl.ds(pl.multiple_of(j * D + to_chip * M, M), M)
             cots[to, pl.ds(0, 2 * H)] = kv.astype(BF)
             cots[to, pl.ds(2 * H, H)] = gq.astype(BF)
             t = (kv[:, :H] * wks[at, js].astype(F32) + kv[:, H:] * wvs[at, js].astype(F32) + gq * wqs[at, js].astype(F32))
-            arow[at, :] = arow[at, :] + jnp.broadcast_to(jnp.sum(t, axis=-1, keepdims=True), (T, 128))
+            arow[at, :] = arow[at, :] + jnp.broadcast_to(jnp.sum(t, axis=-1, keepdims=True), (M, 128))
+
+            @pl.when(i == 0)
+            def _():
+                for x in wsum[j]:
+                    x.start()
             return carry
 
-        lax.fori_loop(0, D // T, rows, 0)
-        wsum[j].start()
+        lax.fori_loop(0, Q, rows, 0)
         skv = split_rows(jnp.sum(gkv[...].astype(F32), axis=0, keepdims=True))
         sq_ = split_rows(jnp.sum(gqs[:, js].astype(F32), axis=0, keepdims=True))
         b = nt_dot(skv[:, :H], wks[:, js]) + nt_dot(skv[:, H:], wvs[:, js]) + nt_dot(sq_, wqs[:, js])
@@ -1213,7 +1261,8 @@
     srow[...] = token_rows(0, c)
     for h in range(hj, 2 * hj):
         back_head(h, h - hj)
-    wsum[0].middle()
+    for x in wsum[0]:
+        x.middle()
     y_middle(1)
     weights(1)
     phalf[...] = phalf[...] + token_rows(1, 1 - c)
@@ -1221,7 +1270,61 @@
     t_x = rcopy(phalf, ggot, ts_(0), tr_(0), sib)
     t_x.start()
     srow[...] = srow[...] + token_rows(1, c)
-
+    rs, rr, rl = al.take(2, 2), al.take(2, B), al.take(2)
+    rows_in = [tgs, outs]
+    rows_out = [tg_o, out_o]
+
+    def row_x(i, p):
+        return rcopy(rows_in[i].at[pl.ds(p * R, R), :], rows_out[i].at[jz], rs(i, p), rr(i, jz), (2 * q + z // B, c * per + p))
+
+    def row_l(i, p):
+        return lcopy(rows_in[i].at[pl.ds(p * R, R), :], rows_out[i].at[jz], rl(i))
+
+    def send_rows(i):
+        for p in range(per):
+            here = (c * per + p == z) & mine
+
+            @pl.when(here)
+            def _():
+                row_l(i, p).start()
+
+            @pl.when(jnp.logical_not(here))
+            def _():
+                row_x(i, p).start()
+
+    outs[...] = (resid[...] + dsum.total() + db[...]).astype(BF)
+    send_rows(1)
+    ozs, ozr = al.take(3, B), al.take(3, Z)
+
+    def z_buf(i, zz):
+        if i == 2:
+            return zo(zz)
+        return got1.at[pl.ds(pl.multiple_of(zz * M + i * M2, M2), M2), pl.ds(0, 3 * H)]
+
+    def z_done(i, j):
+        if i == 2:
+            return odone(j)
+        return downs.at[pl.ds(pl.multiple_of(j * M + i * M2, M2), M2), pl.ds(0, 3 * H)]
+
+    def z_x(i, j):
+        return rcopy(z_done(i, j), z_buf(i, z), ozs(i, j), ozr(i, z), (dp, B * c + j))
+
+    def z_arrive(i, zz):
+        return rcopy(z_buf(i, zz), z_buf(i, zz), ozs(i, 0), ozr(i, zz), (dp, z))
+
+    def to_plane(i, j):
+        z_done(i, j)[...] = (osum[j] if i == 2 else wsum[j][i]).total().astype(BF)
+
+        @pl.when(B * c + j != z)
+        def _():
+            z_x(i, j).start()
+
+    for j in range(B):
+        to_plane(2, j)
+    for x in wsum[1]:
+        x.middle()
+    for half in range(2):
+        to_plane(half, 0)
     acol = jnp.swapaxes(arow[...], 0, 1)[0:1, :]
     bsum = sums[1:2, :]
     sums[0:1, :] = (acol - b1[...] * bsum) / g1[...]
@@ -1230,26 +1333,6 @@
     n1, n2 = al.take(1), al.take(1)
     v_x = rcopy(sums, sgot, n1(0), n2(0), sib)
     v_x.start()
-    ozs, ozr = al.take(2, B), al.take(2, Z)
-
-    def z_x(i, j):
-        src, dst = ((wdone, zb), (odone, zo))[i]
-        return rcopy(src(j), dst(z), ozs(i, j), ozr(i, z), (dp, B * c + j))
-
-    def z_arrive(i, zz):
-        dst = (zb, zo)[i]
-        return rcopy(dst(zz), dst(zz), ozs(i, 0), ozr(i, zz), (dp, z))
-
-    def to_plane(i, j):
-        (wdone, odone)[i](j)[...] = (wsum, osum)[i][j].total().astype(BF)
-
-        @pl.when(B * c + j != z)
-        def _():
-            z_x(i, j).start()
-
-    wsum[1].middle()
-    for j in range(B):
-        to_plane(1, j)
     t_x.wait_recv()
     def norm_rows(i, carry):
         at = pl.ds(pl.multiple_of(i * C, C), C)
@@ -1262,29 +1345,6 @@
         return carry
 
     lax.fori_loop(0, N // C, norm_rows, 0)
-    rs, rr, rl = al.take(2, 2), al.take(2, B), al.take(2)
-    rows_in = [tgs, outs]
-    rows_out = [tg_o, out_o]
-
-    def row_x(i, p):
-        return rcopy(rows_in[i].at[pl.ds(p * R, R), :], rows_out[i].at[jz], rs(i, p), rr(i, jz), (2 * q + z // B, c * per + p))
-
-    def row_l(i, p):
-        return lcopy(rows_in[i].at[pl.ds(p * R, R), :], rows_out[i].at[jz], rl(i))
-
-    def send_rows(i):
-        for p in range(per):
-            here = (c * per + p == z) & mine
-
-            @pl.when(here)
-            def _():
-                row_l(i, p).start()
-
-            @pl.when(jnp.logical_not(here))
-            def _():
-                row_x(i, p).start()
-
-    send_rows(0)
     for i in range(2):
         y_arrive(i)
     fu = y_own(0, 0)[...].astype(F32) + (xu[0].astype(F32) + xu[1].astype(F32))
@@ -1325,14 +1385,6 @@
         return rcopy(src, aub.at[dev(k, c)], bfs(k), bfr(k), sib)
 
     b_l = lcopy(fbs, aub.at[dp], fl(2))
-    ugat.start()
-    dgat.start()
-    for x in f_l:
-        x.start()
-    b_l.start()
-    for k in range(1, Q):
-        b_x(k).start()
-    b_f(0).start()
     v_x.wait()
     srow[0:8, :] = sums[...] + sgot[...]
     pgot[q] = srow[0:8, :]
@@ -1353,9 +1405,6 @@
 
     for k in range(1, Q):
         vp_x(k).start()
-    outs[...] = (resid[...] + dsum.total() + db[...]).astype(BF)
-    send_rows(1)
-    to_plane(0, 0)
     for k in range(1, Q):
         vp_arrive(k).wait_recv()
     psum = pgot[0]
@@ -1365,37 +1414,54 @@
     zgot[z] = psum
     for r in range(1, Z):
         vz_x(r).start()
-    to_plane(0, 1)
+    for half in range(2):
+        to_plane(half, 1)
+    ugat.start()
+    dgat.start()
+    for x in f_l:
+        x.start()
+    b_l.start()
+    for k in range(1, Q):
+        b_x(k).start()
+    b_f(0).start()
 
     def a_loc(ref, n_rows):
         def loc(k, lo, n):
             return ref.at[pl.ds(pl.multiple_of(across(q, k) * n_rows + lo, n), n), :]
         return loc
 
-    wgat = PlaneGather(al, peer, sib, a_loc(aw, M), M, own=wfin)
-    ogat = PlaneGather(al, peer, sib, a_loc(ago, OR), OR, own=ofin)
-    gl = al.take(2)
-    g_l = [lcopy(wfin, a_loc(aw, M)(0, 0, M), gl(0)), lcopy(ofin, a_loc(ago, OR)(0, 0, OR), gl(1))]
+    fins = [wfin.at[pl.ds(0, M2), :], wfin.at[pl.ds(M2, M2), :], ofin]
+
+    def half_loc(half):
+        def loc(k, lo, n):
+            return aw.at[pl.ds(pl.multiple_of(across(q, k) * M + half * M2 + lo, n), n), :]
+        return loc
+
+    locs = [half_loc(0), half_loc(1), a_loc(ago, OR)]
+    gats = [PlaneGather(al, peer, sib, locs[i], OR if i == 2 else M2, own=fins[i]) for i in range(3)]
+    gl = al.take(3)
+    g_l = [lcopy(fins[i], locs[i](0, 0, OR if i == 2 else M2), gl(i)) for i in range(3)]
+    for gat in (ugat, dgat):
+        gat.middle()
+    send_rows(0)
+    for k in range(1, Q):
+        b_arrive(k).wait_recv()
+        b_f(k).start()
 
     @pl.when(mine)
     def _():
-        for i, (fin, done, buf, gat) in ((1, (ofin, odone, zo, ogat)), (0, (wfin, wdone, zb, wgat))):
+        for i in (2, 0, 1):
             for zz in range(Z):
                 @pl.when(zz != z)
                 def _():
                     z_arrive(i, zz).wait_recv()
-            buf(z)[...] = done(jz)[...]
-            t = buf(0)[...].astype(F32)
+            z_buf(i, z)[...] = z_done(i, jz)[...]
+            t = z_buf(i, 0)[...].astype(F32)
             for zz in range(1, Z):
-                t = t + buf(zz)[...].astype(F32)
-            fin[...] = t.astype(BF)
-            gat.start()
-            g_l[1 if i == 1 else 0].start()
-    for gat in (ugat, dgat):
-        gat.middle()
-    for k in range(1, Q):
-        b_arrive(k).wait_recv()
-        b_f(k).start()
+                t = t + z_buf(i, zz)[...].astype(F32)
+            fins[i][...] = t.astype(BF)
+            gats[i].start()
+            g_l[i].start()
     for r in range(1, Z):
         vz_arrive(r).wait_recv()
     zsum = zgot[0]
@@ -1405,22 +1471,22 @@
 
     @pl.when(mine)
     def _():
-        for gat in (ogat, wgat):
-            gat.middle()
+        for i in (2, 0, 1):
+            gats[i].middle()
     for gat in (ugat, dgat):
         gat.last()
 
     @pl.when(mine)
     def _():
-        for gat in (ogat, wgat):
-            gat.last()
+        for i in (2, 0, 1):
+            gats[i].last()
     ugat.arrivals(u_loc(1 - c))
     dgat.arrivals(d_loc(1 - c))
 
     @pl.when(jnp.logical_not(mine))
     def _():
-        ogat.arrivals(a_loc(ago, OR))
-        wgat.arrivals(a_loc(aw, M))
+        for i in range(3):
+            gats[i].arrivals(locs[i])
 
     for k in range(Q):
         rcopy(aub.at[dev(k, 1 - c)], aub.at[dev(k, 1 - c)], bfs(k), bfr(k), sib).wait_recv()
@@ -1437,12 +1503,12 @@
         ub_x(r).wait_send()
     for i in range(2):
         y_drain(i)
-    for x in osum + wsum + [dsum, ugat, dgat]:
+    for x in osum + wsum[0] + wsum[1] + [dsum, ugat, dgat]:
         x.drain()
 
     @pl.when(mine)
     def _():
-        for x in (ogat, wgat):
+        for x in gats:
             x.drain()
         for x in g_l:
             x.wait()
@@ -1450,7 +1516,7 @@
     for j in range(B):
         @pl.when(B * c + j != z)
         def _():
-            for i in range(2):
+            for i in range(3):
                 z_x(i, j).wait_send()
     for p in range(per):
         here = (c * per + p == z) & mine
@@ -1473,13 +1539,18 @@
 
     @pl.when(mine)
     def _():
-        for a in range(4):
-            for r in range(1, Z):
-                w_z(a, r).wait_send()
+        for r in range(1, Z):
+            @pl.when(w_direct(r))
+            def _():
+                for a in range(4):
+                    w_z(a, r).wait_send()
     for j in range(B):
         @pl.when(B * c + j != z)
         def _():
             for a in range(4):
+                @pl.when(relay)
+                def _():
+                    w_onward(a, j).wait_send()
                 for k in range(1, Q):
                     w_p(a, j, k, q).wait_send()
     for s in range(B):
@@ -1543,6 +1614,39 @@
     )(comp, mem, tok, cot, wq, wk, wv, wo, up, down, ub, vc, sq, g1, b1, g2, b2, db)
 
 
+def convert_kernel(w, wo, u, d, t, a0, a1, a2, gk, gv, gq, go, gu, gd, gt, b0, b1, b2):
+    h = gk.shape[1]
+    for i, out in enumerate((gk, gv, gq)):
+        out[...] = w[:, i * h:(i + 1) * h].astype(F32)
+    for src, out in ((wo, go), (u, gu), (d, gd), (t, gt)):
+        out[...] = src[...].astype(F32)
+    for src, out in ((a0, b0), (a1, b1), (a2, b2)):
+        out[...] = src[...]
+
+
+def convert(w, wo, u, d, *rows):
+    steps = 8
+    H = w.shape[1] // 3
+    D = rows[0].shape[2]
+    flat = [r.reshape(-1, D) for r in rows]
+
+    def spec(a, cols=None):
+        return pl.BlockSpec((a.shape[0] // steps, a.shape[1] if cols is None else cols), lambda i: (i, 0))
+
+    ins = [w, wo, u, d] + flat
+    shapes = [sds((w.shape[0], H), F32)] * 3 + [sds(a.shape, F32) for a in (wo, u, d, flat[0])] + [sds(a.shape, BF) for a in flat[1:]]
+    out = pl.pallas_call(
+        convert_kernel,
+        grid=(steps,),
+        out_shape=shapes,
+        in_specs=[spec(a) for a in ins],
+        out_specs=[spec(a) for a in shapes],
+        compiler_params=pltpu.CompilerParams(vmem_limit_bytes=63 << 20),
+        name="convert",
+    )(*ins)
+    return list(out[:6]) + [o.reshape(rows[0].shape) for o in out[6:]]
+
+
 def chip_device(Q, Z, tokens, memory, compressed, valid_counts, attention_norm_gain, attention_norm_bias,
                 query_projection, key_projection, value_projection, out_weight, feedforward_norm_gain,
                 feedforward_norm_bias, up_weight, up_bias, down_weight, down_bias, squeeze_weight, cotangent):
@@ -1556,10 +1660,9 @@
         squeeze_weight, attention_norm_gain.reshape(1, D), attention_norm_bias.reshape(1, D),
         feedforward_norm_gain.reshape(1, D), feedforward_norm_bias.reshape(1, D), down_bias.reshape(1, D),
     )
-    aw = aw.astype(F32)
+    gk, gv, gq, go, gu, gd, g_tokens, out, new_mem, new_comp = convert(aw, ago, afu, afd, o_tg, o_out, o_nm, o_nc)
     return (
-        o_out, o_tg.astype(F32), small[0], small[1], aw[:, 2 * H:], aw[:, :H], aw[:, H:2 * H], ago.astype(F32),
-        small[2], small[3], afu.astype(F32), aub.reshape(FL), afd.astype(F32), small[4], o_nm, o_nc,
+        out, g_tokens, small[0], small[1], gq, gk, gv, go, small[2], small[3], gu, aub.reshape(FL), gd, small[4], new_mem, new_comp,
     )
 
 

time: 287 us -> 263 us (0.916); the launches traced: 287 us -> 258 us
  Pallas kernels: 270 us -> 254 us
  other arithmetic: 7.12 us -> 0 us
  local copies, waits for them, and re-layouts: 9.21 us -> 3.49 us
    pallas_call x1, Pallas kernels: 270 us -> 244 us  [layer(): pl.pallas_call(functools.partial(layer_kernel, Q, Z), out_shape=[sds((D,...]
    pallas_call x0 -> x1, Pallas kernels: none -> 9.81 us  [convert(): pl.pallas_call(convert_kernel, grid=(steps,), out_shape=shapes, in_specs=...]
    convert_element_type x4 -> x0, other arithmetic: 7.12 us -> none  [the longest x1 2.48 us: chip_device(): afu.astype(F32)]
    slice x1 -> x0, local copies, waits for them, and re-layouts: 3.26 us -> none  [chip_device(): aw[:, H:2 * H]]
where the time goes in v3:
time: 263 us; the launch traced here: 258 us
  Pallas kernels  254 us (97%)
  local copies, waits for them, and re-layouts  3.49 us (1%)
    pallas_call x1, Pallas kernels, layer(): pl.pallas_call(functools.partial(layer_kernel, Q, Z), out_shape=[sds((D,...  244 us
    pallas_call x1, Pallas kernels, convert(): pl.pallas_call(convert_kernel, grid=(steps,), out_shape=shapes, in_specs=...  9.81 us

profile of v3, /device:TPU:9, one launch (start us, length us, event | category | flops | bytes accessed | tf_op | source)
XLA Modules:
  0.0 258.4 jit_solution(15558850549029052205)
XLA Ops:
  0.6 1.3 broadcast_in_dim.2.vc
  2.0 244.4 %layer.1 = (bf16[1024,768]{1,0:T(8,128)(2,1)}, bf16[256,1024]{1,0:T(8,128)(2,1)}, bf16[1024,1024]{1,0:T(8,128)(2,1)}, bf16[1024,1024]{1,0:T(8,128)(2,1)}, f32[8,...) custom-call(bf16[2,128,1024]{2,1,0:T(8,128)(2,1)} %comp.1, ...), custom_call_target="tpu_custom_call" | custom-call | tf_op jit(solution)/shard_map/layer/pallas_call | solution.py:1591
  246.4 1.6 fusion
  248.0 0.0 copy-start
  248.0 9.8 %convert.1 = (f32[1024,256]{1,0:T(8,128)}, f32[1024,256]{1,0:T(8,128)}, f32[1024,256]{1,0:T(8,128)}, f32[256,1024]{1,0:T(8,128)}, f32[1024,1024]{1,0:T(8,128)}, ...) custom-call(bf16[1024,768]{1,0:T(8,128)(2,1)} %get-tuple-element.36., ...), custom_call_target="tpu_custom_call" | custom-call | tf_op jit(solution)/shard_map/convert/pallas_call | solution.py:1638
  257.8 0.0 copy-done
  257.8 0.6 copy.35
Async XLA Ops:
  248.0 9.8 %copy-start = (f32[8,1,128]{2,1,0:T(1,128)S(1)}, f32[8,1,128]{2,1,0:T(1,128)}, u32[]{:S(2)}) copy-start(f32[8,1,128]{2,1,0:T(1,128)} %get-tuple-element.52) | copy-start | bytes 12292

commit v4 on v3

--- a/solution.py
+++ b/solution.py
@@ -736,12 +736,22 @@
                     w_onward(a, j).start()
                 for k in range(1, Q):
                     w_p(a, j, k, q).start()
-    for s in range(B):
-        @pl.when(B * c + s != z)
-        def _():
-            for t in range(3):
+    def c_start(t):
+        for s in range(B):
+            @pl.when(B * c + s != z)
+            def _():
                 for h in range(2):
                     c_z(t, s, h).start()
+
+    def c_sent(t):
+        for s in range(B):
+            @pl.when(B * c + s != z)
+            def _():
+                for h in range(2):
+                    c_z(t, s, h).wait_send()
+
+    for t in range(3):
+        c_start(t)
 
     def norm_block(t, zs):
         at = pl.ds(pl.multiple_of(zs * R, R), R)
@@ -767,50 +777,6 @@
     for x in c_in:
         x.wait()
     sums[4:5, :] = jnp.sum(nms[...].astype(F32), axis=0, keepdims=True)
-    for r in range(1, Z):
-        zs = lax.rem(z + r, Z)
-        for t in range(3):
-            c_arrive(t, zs).wait_recv()
-            c_fwd(t, zs, c).start()
-    for s in range(B):
-        @pl.when(B * c + s != z)
-        def _():
-            for t in range(3):
-                for h in range(2):
-                    c_z(t, s, h).wait_send()
-    for s in range(B):
-        here = (B * c + s == z) & mine
-
-        @pl.when(here)
-        def _():
-            t_l().start()
-
-        @pl.when(jnp.logical_not(here))
-        def _():
-            t_z(s).start()
-    x_start(0)
-    for r in range(1, Z):
-        zs = lax.rem(z + r, Z)
-        for t in range(3):
-            c_fwd(t, zs, 1 - c).wait_recv()
-
-        def norm_one(t, carry, zs=zs):
-            norm_block(t, zs)
-            return carry
-
-        lax.fori_loop(0, 3, norm_one, 0)
-    for j in range(B):
-        @pl.when(B * c + j != z)
-        def _():
-            for a in range(4):
-                for k in range(1, Q):
-                    w_p(a, j, k, across(q, k)).wait_recv()
-
-    @pl.when(mine)
-    def _():
-        for a in range(4):
-            w_l(a).wait()
-
     T = 256
 
     def project(i, carry):
@@ -819,13 +785,51 @@
         vs[at, :] = nn_dot(normed[at, :], wvs[...]).astype(BF)
         return carry
 
-    lax.fori_loop(0, 3 * S // T, project, 0)
-
     def project_q(i, carry):
         at = pl.ds(pl.multiple_of(i * T, T), T)
         qs[at, :] = nn_dot(normed[pl.ds(pl.multiple_of(2 * S + i * T, T), T), :], wqs[...]).astype(BF)
         return carry
 
+    for t in range(3):
+        for r in range(1, Z):
+            zs = lax.rem(z + r, Z)
+            c_arrive(t, zs).wait_recv()
+            c_fwd(t, zs, c).start()
+        if t == 2:
+            for u in range(3):
+                c_sent(u)
+            for s in range(B):
+                here = (B * c + s == z) & mine
+
+                @pl.when(here)
+                def _():
+                    t_l().start()
+
+                @pl.when(jnp.logical_not(here))
+                def _():
+                    t_z(s).start()
+            x_start(0)
+        for r in range(1, Z):
+            c_fwd(t, lax.rem(z + r, Z), 1 - c).wait_recv()
+
+        def norm_one(r, carry, t=t):
+            norm_block(t, lax.rem(z + r, Z))
+            return carry
+
+        lax.fori_loop(1, Z, norm_one, 0)
+        if t == 0:
+            for j in range(B):
+                @pl.when(B * c + j != z)
+                def _():
+                    for a in range(4):
+                        for k in range(1, Q):
+                            w_p(a, j, k, across(q, k)).wait_recv()
+
+            @pl.when(mine)
+            def _():
+                for a in range(4):
+                    w_l(a).wait()
+        lax.fori_loop(t * S // T, (t + 1) * S // T, project, 0)
     lax.fori_loop(0, S // T, project_q, 0)
     x_start(1)
 
@@ -1614,7 +1618,9 @@
     )(comp, mem, tok, cot, wq, wk, wv, wo, up, down, ub, vc, sq, g1, b1, g2, b2, db)
 
 
-def convert_kernel(w, wo, u, d, t, a0, a1, a2, gk, gv, gq, go, gu, gd, gt, b0, b1, b2):
+def convert_kernel(w, wo, u, d, t, a0, a1, a2, v, gk, gv, gq, go, gu, gd, gt, b0, b1, b2, *vecs):
+    for i, out in enumerate(vecs):
+        out[...] = v[i, :]
     h = gk.shape[1]
     for i, out in enumerate((gk, gv, gq)):
         out[...] = w[:, i * h:(i + 1) * h].astype(F32)
@@ -1624,8 +1630,8 @@
         out[...] = src[...]
 
 
-def convert(w, wo, u, d, *rows):
-    steps = 8
+def convert(small, w, wo, u, d, *rows):
+    steps = 2
     H = w.shape[1] // 3
     D = rows[0].shape[2]
     flat = [r.reshape(-1, D) for r in rows]
@@ -1638,13 +1644,13 @@
     out = pl.pallas_call(
         convert_kernel,
         grid=(steps,),
-        out_shape=shapes,
-        in_specs=[spec(a) for a in ins],
-        out_specs=[spec(a) for a in shapes],
+        out_shape=shapes + [sds((D,), F32)] * 5,
+        in_specs=[spec(a) for a in ins] + [pl.BlockSpec(small.shape, lambda i: (0, 0))],
+        out_specs=[spec(a) for a in shapes] + [pl.BlockSpec((D,), lambda i: (0,))] * 5,
         compiler_params=pltpu.CompilerParams(vmem_limit_bytes=63 << 20),
         name="convert",
-    )(*ins)
-    return list(out[:6]) + [o.reshape(rows[0].shape) for o in out[6:]]
+    )(*ins, small)
+    return list(out[:6]) + [o.reshape(rows[0].shape) for o in out[6:10]] + list(out[10:])
 
 
 def chip_device(Q, Z, tokens, memory, compressed, valid_counts, attention_norm_gain, attention_norm_bias,
@@ -1660,9 +1666,9 @@
         squeeze_weight, attention_norm_gain.reshape(1, D), attention_norm_bias.reshape(1, D),
         feedforward_norm_gain.reshape(1, D), feedforward_norm_bias.reshape(1, D), down_bias.reshape(1, D),
     )
-    gk, gv, gq, go, gu, gd, g_tokens, out, new_mem, new_comp = convert(aw, ago, afu, afd, o_tg, o_out, o_nm, o_nc)
+    gk, gv, gq, go, gu, gd, g_tokens, out, new_mem, new_comp, *vecs = convert(small, aw, ago, afu, afd, o_tg, o_out, o_nm, o_nc)
     return (
-        out, g_tokens, small[0], small[1], gq, gk, gv, go, small[2], small[3], gu, aub.reshape(FL), gd, small[4], new_mem, new_comp,
+        out, g_tokens, vecs[0], vecs[1], gq, gk, gv, go, vecs[2], vecs[3], gu, aub.reshape(FL), gd, vecs[4], new_mem, new_comp,
     )
 
 

time: 263 us -> 258 us (0.981)
  no operation moved by 1% of the time
where the time goes in v4:
time: 258 us; the launch traced here: 254 us
  Pallas kernels  252 us (98%)
    pallas_call x1, Pallas kernels, layer(): pl.pallas_call(functools.partial(layer_kernel, Q, Z), out_shape=[sds((D,...  243 us
    pallas_call x1, Pallas kernels, convert(): pl.pallas_call(convert_kernel, grid=(steps,), out_shape=shapes + [sds((D,...  8.52 us

profile of v4, /device:TPU:9, one launch (start us, length us, event | category | flops | bytes accessed | tf_op | source)
XLA Modules:
  0.0 254.4 jit_solution(9180795459980696315)
XLA Ops:
  0.6 1.3 broadcast_in_dim.2.vc
  2.0 243.3 %layer.1 = (bf16[1024,768]{1,0:T(8,128)(2,1)}, bf16[256,1024]{1,0:T(8,128)(2,1)}, bf16[1024,1024]{1,0:T(8,128)(2,1)}, bf16[1024,1024]{1,0:T(8,128)(2,1)}, f32[8,...) custom-call(bf16[2,128,1024]{2,1,0:T(8,128)(2,1)} %comp.1, ...), custom_call_target="tpu_custom_call" | custom-call | tf_op jit(solution)/shard_map/layer/pallas_call | solution.py:1595
  245.2 0.0 copy-start
  245.2 8.5 %convert.1 = (f32[1024,256]{1,0:T(8,128)}, f32[1024,256]{1,0:T(8,128)}, f32[1024,256]{1,0:T(8,128)}, f32[256,1024]{1,0:T(8,128)}, f32[1024,1024]{1,0:T(8,128)}, ...) custom-call(bf16[1024,768]{1,0:T(8,128)(2,1)} %get-tuple-element.41., ...), custom_call_target="tpu_custom_call" | custom-call | tf_op jit(solution)/shard_map/convert/pallas_call | solution.py:1644
  253.8 0.0 copy-done
  253.8 0.6 copy.35
Async XLA Ops:
  245.2 8.5 %copy-start = (f32[8,1,128]{2,1,0:T(1,128)S(1)}, f32[8,1,128]{2,1,0:T(1,128)}, u32[]{:S(2)}) copy-start(f32[8,1,128]{2,1,0:T(1,128)} %get-tuple-element.61) | copy-start | bytes 12292

commit v5 on v4

--- a/solution.py
+++ b/solution.py
@@ -1662,7 +1662,7 @@
     E = FL // (2 * Q)
     aw, ago, afu, afd, aub, small, o_out, o_tg, o_nm, o_nc = layer(
         Q, Z, compressed, memory, tokens, cotangent, query_projection, key_projection, value_projection, out_weight,
-        up_weight, down_weight, up_bias.reshape(2 * Q, 1, E), jnp.broadcast_to(valid_counts[:, None, None], (B, 8, 128)),
+        up_weight, down_weight, up_bias.reshape(2 * Q, 1, E), valid_counts.reshape(B, 1, 1),
         squeeze_weight, attention_norm_gain.reshape(1, D), attention_norm_bias.reshape(1, D),
         feedforward_norm_gain.reshape(1, D), feedforward_norm_bias.reshape(1, D), down_bias.reshape(1, D),
     )

time: 258 us -> 258 us (level)
  no operation moved by 1% of the time
where the time goes in v5:
time: 258 us; the launch traced here: 254 us
  Pallas kernels  252 us (98%)
    pallas_call x1, Pallas kernels, layer(): pl.pallas_call(functools.partial(layer_kernel, Q, Z), out_shape=[sds((D,...  243 us
    pallas_call x1, Pallas kernels, convert(): pl.pallas_call(convert_kernel, grid=(steps,), out_shape=shapes + [sds((D,...  8.52 us

profile of v5, /device:TPU:9, one launch (start us, length us, event | category | flops | bytes accessed | tf_op | source)
XLA Modules:
  0.0 254.3 jit_solution(3423182194707272707)
XLA Ops:
  0.6 1.3 copy.34.vc
  1.9 243.2 %layer.1 = (bf16[1024,768]{1,0:T(8,128)(2,1)}, bf16[256,1024]{1,0:T(8,128)(2,1)}, bf16[1024,1024]{1,0:T(8,128)(2,1)}, bf16[1024,1024]{1,0:T(8,128)(2,1)}, f32[8,...) custom-call(bf16[2,128,1024]{2,1,0:T(8,128)(2,1)} %comp.1, ...), custom_call_target="tpu_custom_call" | custom-call | tf_op jit(solution)/shard_map/layer/pallas_call | solution.py:1595
  245.1 0.0 copy-start
  245.1 8.5 %convert.1 = (f32[1024,256]{1,0:T(8,128)}, f32[1024,256]{1,0:T(8,128)}, f32[1024,256]{1,0:T(8,128)}, f32[256,1024]{1,0:T(8,128)}, f32[1024,1024]{1,0:T(8,128)}, ...) custom-call(bf16[1024,768]{1,0:T(8,128)(2,1)} %get-tuple-element.41., ...), custom_call_target="tpu_custom_call" | custom-call | tf_op jit(solution)/shard_map/convert/pallas_call | solution.py:1644
  253.7 0.0 copy-done
  253.7 0.6 copy.36
Async XLA Ops:
  245.1 8.5 %copy-start = (f32[8,1,128]{2,1,0:T(1,128)S(1)}, f32[8,1,128]{2,1,0:T(1,128)}, u32[]{:S(2)}) copy-start(f32[8,1,128]{2,1,0:T(1,128)} %get-tuple-element.61) | copy-start | bytes 12292
